TPU v7x, 512 devices: a whole 4x8x8 slice. The times are simulated.
512 devices in a mesh: seq: 64 (over y, z), tp: 8 (over x, core).
Axes of the slice: x: 4, y: 8, z: 8, core: 2. Of those that a mesh axis runs over, the one named last changes fastest.
Arguments:
- queries: bfloat16 [16384, 4096], P('seq', 'tp'), may hold values from -6 to 6
- keys: bfloat16 [16384, 4096], P('seq', 'tp'), may hold values from -6 to 6
- values: bfloat16 [16384, 4096], P('seq', 'tp'), may hold values from -6 to 6
- out_cotangent: bfloat16 [16384, 2048], P('seq', 'tp'), may hold values from -16 to 16
- proj_weight: bfloat16 [4096, 2048], P('tp', 'seq'), may hold values from -0.125 to 0.125
Outputs:
- grad_queries: bfloat16 [16384, 4096], P('seq', 'tp')
- grad_keys: bfloat16 [16384, 4096], P('seq', 'tp')
- grad_values: bfloat16 [16384, 4096], P('seq', 'tp')
- grad_proj: float32 [4096, 2048], P('tp', 'seq')
All inputs are finite; a program needn't handle non-finite values.
Results may differ from a plain program's by a relative error of at most 0.0058.
Values may be sent and summed in bfloat16 or wider, within the bound.
No kernel may reach another device: no remote copies, remote signals or barrier semaphores. Data moves between devices by JAX's collectives and lax.ppermute only.
A program may use at most 128 MiB of HBM per device.

v0:
```python
import jax
import jax.numpy as jnp
from jax import lax
from jax.sharding import PartitionSpec as P

DH = 128


def entering(part, axis, combine, identity, reverse):
    count = lax.axis_size(axis)
    place = lax.axis_index(axis)
    ahead = count - 1 - place if reverse else place
    gathered = lax.all_gather(part, axis)
    state = jnp.zeros_like(part) + jnp.asarray(identity, part.dtype)

    def one(step, state):
        source = count - 1 - step if reverse else step
        return combine(state, lax.dynamic_index_in_dim(gathered, source, 0, False))

    return lax.fori_loop(0, ahead, one, state)


def add_pair(earlier, later_one):
    return earlier + later_one


def per_device(queries, keys, values, out_cotangent, proj_weight):
    tok = queries.shape[0]
    heads = queries.shape[1] // DH
    seq_count = lax.axis_size("seq")
    scale = 1.0 / jnp.sqrt(jnp.float32(DH * tok * seq_count))
    q_heads = queries.reshape(tok, heads, DH)
    k_heads = keys.reshape(tok, heads, DH)
    v_heads = values.reshape(tok, heads, DH)
    kv_state = jnp.einsum("thd,the->hde", k_heads, v_heads, preferred_element_type=jnp.float32)
    zero_state = jnp.zeros_like(kv_state)
    prior_sum = entering(kv_state, "seq", add_pair, zero_state, False)
    full_cot = lax.all_gather(out_cotangent, "tp", axis=1, tiled=True)
    grad_out = lax.dot_general(
        full_cot,
        lax.all_gather(proj_weight, "seq", axis=1, tiled=True),
        (((1,), (1,)), ((), ())),
        preferred_element_type=jnp.float32,
    ).astype(jnp.bfloat16)
    g_heads = grad_out.reshape(tok, heads, DH)
    qg_state = jnp.einsum("thd,the->hde", q_heads, g_heads, preferred_element_type=jnp.float32)
    later_sum = entering(qg_state, "seq", add_pair, zero_state, True)
    prior = prior_sum.astype(jnp.bfloat16)
    later = later_sum.astype(jnp.bfloat16)
    rows = jnp.arange(tok)
    causal = (rows[:, None] >= rows[None, :])[None]
    attn = jnp.where(
        causal,
        jnp.einsum("thd,shd->hts", q_heads, k_heads, preferred_element_type=jnp.float32),
        0.0,
    ).astype(jnp.bfloat16)
    back = jnp.where(
        causal,
        jnp.einsum("thd,shd->hts", g_heads, v_heads, preferred_element_type=jnp.float32),
        0.0,
    ).astype(jnp.bfloat16)
    attn_out = scale * (
        jnp.einsum("hts,she->the", attn, v_heads, preferred_element_type=jnp.float32)
        + jnp.einsum("thd,hde->the", q_heads, prior, preferred_element_type=jnp.float32)
    )
    grad_q = scale * (
        jnp.einsum("hts,shd->thd", back, k_heads, preferred_element_type=jnp.float32)
        + jnp.einsum("the,hde->thd", g_heads, prior, preferred_element_type=jnp.float32)
    )
    grad_k = scale * (
        jnp.einsum("hts,thd->shd", back, q_heads, preferred_element_type=jnp.float32)
        + jnp.einsum("she,hde->shd", v_heads, later, preferred_element_type=jnp.float32)
    )
    grad_v = scale * (
        jnp.einsum("hts,the->she", attn, g_heads, preferred_element_type=jnp.float32)
        + jnp.einsum("shd,hde->she", k_heads, later, preferred_element_type=jnp.float32)
    )
    out_flat = attn_out.astype(jnp.bfloat16).reshape(tok, heads * DH)
    proj_term = lax.dot_general(
        out_flat, full_cot, (((0,), (0,)), ((), ())), preferred_element_type=jnp.float32
    )
    proj_sum = lax.psum_scatter(proj_term, "seq", scatter_dimension=1, tiled=True)
    grad_proj = proj_sum / jnp.sqrt(jnp.float32(tok * seq_count))
    width = heads * DH
    return (
        grad_q.astype(jnp.bfloat16).reshape(tok, width),
        grad_k.astype(jnp.bfloat16).reshape(tok, width),
        grad_v.astype(jnp.bfloat16).reshape(tok, width),
        grad_proj,
    )


def solution(mesh):
    return jax.shard_map(
        per_device,
        mesh=mesh,
        in_specs=(P("seq", "tp"), P("seq", "tp"), P("seq", "tp"), P("seq", "tp"), P("tp", "seq")),
        out_specs=(P("seq", "tp"), P("seq", "tp"), P("seq", "tp"), P("tp", "seq")),
        check_vma=False,
    )
```

profile of v0, /device:TPU:6, one launch (start us, length us, event | category | flops | bytes accessed | tf_op | source)
XLA Modules:
  0.0 670.4 jit_solution(11894771848935743379)
XLA Ops:
  8.7 1.1 copy.56
  9.8 1.9 fusion.17
  11.8 31.0 %all-gather.7.cloned.1.call-done = bf16[256,2048]{1,0:T(8,128)(2,1)} async-done(((bf16[256,256]{1,0:T(8,128)(2,1)}), bf16[256,2048]{1,0:T(8,128)(2,1)}) %all-gather.7.cloned.1.call-update) | async-done | bytes 1048592 | tf_op jit(solution)/shard_map/all_gather | solution.py:38
  42.8 88.5 %all-gather.9.cloned.1.call-done = bf16[512,2048]{0,1:T(8,128)(2,1)} async-done(((bf16[512,32]{0,1:T(8,128)(2,1)}), bf16[512,2048]{0,1:T(8,128)(2,1)}) %all-gather.9.cloned.1.call-update) | async-done | bytes 2097168 | tf_op jit(solution)/shard_map/all_gather | solution.py:41
  131.3 2.6 convolution_convert_fusion
  135.9 135.8 %all-gather.11.cloned.1.call-done = f32[256,128,128]{2,1,0:T(8,128)} async-done(((f32[4,128,128]{2,1,0:T(8,128)}), f32[256,128,128]{2,1,0:T(8,128)}) %all-gather.11.cloned.1.call-update) | async-done | bytes 16777232 | tf_op jit(solution)/shard_map/all_gather | solution.py:13
  272.0 2.7 fusion.35
  277.0 136.3 %all-gather.13.cloned.1.call-done = f32[256,128,128]{2,1,0:T(8,128)} async-done(((f32[4,128,128]{2,1,0:T(8,128)}), f32[256,128,128]{2,1,0:T(8,128)}) %all-gather.13.cloned.1.call-update) | async-done | bytes 16777232 | tf_op jit(solution)/shard_map/all_gather | solution.py:13
  413.3 65.1 %while.23 = (s32[]{:T(128)}, f32[4,128,128]{2,1,0:T(8,128)S(1)}, s32[]{:T(128)}, f32[64,4,128,128]{3,2,1,0:T(8,128)}, s32[]{:T(128)}, /*index=5*/s32[]{:T(128)}, s32[]{:T(128)}, s32[]{:T(128)}) while((s32[]{:T(128)}, f32[4,128,128]{2,1,0:T(8,128)S(1)}, s32[]{:T(128)}, f32[64,4,128,128]{3,2,1,0:T(8,128)}, s32[]{:T(128)}, /*index=5*/s32[]{:T(128)}, ...), condition=%wide.region_3.4_spmd, body=%wide.region_2.3_spmd.sunk | while | flops 65542 | bytes 786575 | solution.py:20
  414.4 1.0 bitcast_add_fusion.5
  415.4 1.0 bitcast_add_fusion.5
  416.5 1.0 bitcast_add_fusion.5
  423.7 1.0 bitcast_add_fusion.5
  424.7 1.0 bitcast_add_fusion.5
  425.8 1.0 bitcast_add_fusion.5
  429.9 1.0 bitcast_add_fusion.5
  430.9 1.0 bitcast_add_fusion.5
  432.0 1.0 bitcast_add_fusion.5
  435.1 1.0 bitcast_add_fusion.5
  436.1 1.0 bitcast_add_fusion.5
  438.2 1.0 bitcast_add_fusion.5
  439.2 1.0 bitcast_add_fusion.5
  440.2 1.0 bitcast_add_fusion.5
  441.3 1.0 bitcast_add_fusion.5
  443.3 1.0 bitcast_add_fusion.5
  444.4 1.0 bitcast_add_fusion.5
  445.4 1.0 bitcast_add_fusion.5
  446.4 1.0 bitcast_add_fusion.5
  447.5 1.0 bitcast_add_fusion.5
  449.5 1.0 bitcast_add_fusion.5
  450.6 1.0 bitcast_add_fusion.5
  453.7 1.0 bitcast_add_fusion.5
  456.8 1.0 bitcast_add_fusion.5
  457.8 1.0 bitcast_add_fusion.5
  460.9 1.0 bitcast_add_fusion.5
  461.9 1.0 bitcast_add_fusion.5
  464.0 1.0 bitcast_add_fusion.5
  465.0 1.0 bitcast_add_fusion.5
  467.1 1.0 bitcast_add_fusion.5
  468.2 1.0 bitcast_add_fusion.5
  470.2 1.0 bitcast_add_fusion.5
  471.3 1.0 bitcast_add_fusion.5
  473.3 1.0 bitcast_add_fusion.5
  474.4 1.0 bitcast_add_fusion.5
  476.4 1.0 bitcast_add_fusion.5
  477.5 1.0 bitcast_add_fusion.5
  480.7 181.7 %reduce-scatter.2.cloned.1.call-done = f32[512,32]{0,1:T(8,128)} async-done(((f32[512,2048]{0,1:T(8,128)}), f32[512,32]{0,1:T(8,128)}) %reduce-scatter.2.cloned.1.call-update) | async-done | bytes 65552 | tf_op jit(solution)/shard_map/reduce_scatter | solution.py:82
  662.4 1.5 broadcast_multiply_fusion
  (62 shorter events, 34.4 us)
Async XLA Ops:
  7.2 126.9 %copy-start = (bf16[256,512]{1,0:T(8,128)(2,1)S(1)}, bf16[256,512]{1,0:T(8,128)(2,1)}, u32[]{:S(2)}) copy-start(bf16[256,512]{1,0:T(8,128)(2,1)} %param.9) | copy-start | bytes 786436
  7.2 128.1 %copy-start.1 = (bf16[256,512]{1,0:T(8,128)(2,1)S(1)}, bf16[256,512]{1,0:T(8,128)(2,1)}, u32[]{:S(2)}) copy-start(bf16[256,512]{1,0:T(8,128)(2,1)} %param.10) | copy-start | bytes 786436
  7.2 35.6 %all-gather.7.cloned.1.call-start = ((), (), s32[]{:S(2)}) async-start(), calls=%async_computation.1 | async-start | bytes 1179648 | tf_op jit(solution)/shard_map/all_gather | solution.py:38
  7.9 123.4 %all-gather.9.cloned.1.call-start = ((), (), s32[]{:S(2)}) async-start(), calls=%async_computation.2 | async-start | bytes 2129920 | tf_op jit(solution)/shard_map/all_gather | solution.py:41
  8.7 263.0 %all-gather.11.cloned.1.call-start = ((), (), s32[]{:S(2)}) async-start(), calls=%async_computation.4 | async-start | bytes 17039360 | tf_op jit(solution)/shard_map/all_gather | solution.py:13
  11.8 401.5 %all-gather.13.cloned.1.call-start = ((), (), s32[]{:S(2)}) async-start(), calls=%async_computation.5 | async-start | bytes 17039360 | tf_op jit(solution)/shard_map/all_gather | solution.py:13
  135.1 527.2 %reduce-scatter.2.cloned.1.call-start = ((), (), s32[]{:S(2)}) async-start(), calls=%async_computation.3 | async-start | bytes 4259840 | tf_op jit(solution)/shard_map/reduce_scatter | solution.py:82
  135.2 136.8 %copy-start.2 = (bf16[256,2048]{1,0:T(8,128)(2,1)S(1)}, bf16[256,2048]{1,0:T(8,128)(2,1)}, u32[]{:S(2)}) copy-start(bf16[256,2048]{1,0:T(8,128)(2,1)} %all-gather.7.cloned.1.call-done) | copy-start | bytes 3145732
Sparse Core Ops, SparseCore 0:
  10.1 32.6 all-gather.6
  45.8 85.4 all-gather.8
  134.9 136.7 all-gather.10
  275.1 138.1 all-gather.12
  417.2 245.0 reduce-scatter.1
where the time goes:
time: 673 us; the launch traced here: 670 us
  waiting for transfers between devices  575 us (85%)
  other arithmetic  65.2 us (10%)
  between operations  14 us (2%)
  matrix products  10.2 us (2%)
    all_gather x2, waiting for transfers between devices, entering(): gathered = lax.all_gather(part, axis)  272 us
    reduce_scatter x1, waiting for transfers between devices, per_device(): lax.psum_scatter(proj_term, 'seq', scatter_dimension=1, tiled=True)  182 us
    all_gather x1, waiting for transfers between devices, per_device(): lax.all_gather(proj_weight, 'seq', axis=1, tiled=True)  88.5 us
    add x63, other arithmetic, add_pair(): return earlier + later_one  63.7 us
    all_gather x1, waiting for transfers between devices, per_device(): full_cot = lax.all_gather(out_cotangent, 'tp', axis=1, tiled=True)  31 us
  transfers between devices with their start and end apart: 5, of which 5 were waited for; matrix products, arithmetic and copies ran while one was open for 12% of the time, Pallas kernels for 0%

commit v1 on v0

v1 whole, which is shorter than its diff:
```python
import jax
import jax.numpy as jnp
from jax import lax
from jax.experimental import pallas as pl
from jax.experimental.pallas import tpu as pltpu
from jax.sharding import Mesh, PartitionSpec as P

DH = 128
SEQ = ("y", "z")
BF16 = jnp.bfloat16
F32 = jnp.float32


def gather_by_exchange(part, axis):
    count = lax.axis_size(axis)
    copies = jnp.broadcast_to(part[None], (count,) + part.shape)
    return lax.all_to_all(copies, axis, 0, 0, tiled=True)


def running_kernel(reverse, parts_ref, sums_ref):
    count = parts_ref.shape[0]
    total = jnp.zeros(parts_ref.shape[1:], F32)
    for step in range(count):
        at = count - 1 - step if reverse else step
        sums_ref[at] = total.astype(sums_ref.dtype)
        total = total + parts_ref[at].astype(F32)


def entering(state, reverse):
    count = lax.axis_size(SEQ)
    heads, rows, cols = state.shape
    pieces = state.astype(BF16).reshape(count, heads * rows // count, cols)
    mine = lax.all_to_all(pieces, SEQ, 0, 0, tiled=True)
    sums = pl.pallas_call(
        lambda i, o: running_kernel(reverse, i, o),
        out_shape=jax.ShapeDtypeStruct(mine.shape, BF16),
    )(mine)
    back = lax.all_to_all(sums, SEQ, 0, 0, tiled=True)
    return back.reshape(heads, rows, cols)


def dot(spec, a, b):
    return jnp.einsum(spec, a, b, preferred_element_type=F32)


def per_device(queries, keys, values, out_cotangent, proj_weight):
    tok = queries.shape[0]
    heads = queries.shape[1] // DH
    seq_count = lax.axis_size(SEQ)
    scale = 1.0 / jnp.sqrt(F32(DH * tok * seq_count))
    q_heads = queries.reshape(tok, heads, DH)
    k_heads = keys.reshape(tok, heads, DH)
    v_heads = values.reshape(tok, heads, DH)
    weight_z = gather_by_exchange(proj_weight.T, "z")
    weight_t = lax.all_gather(weight_z, "y", axis=0, tiled=True)
    kv_state = dot("thd,the->hde", k_heads, v_heads)
    prior = entering(kv_state, False)
    full_cot = gather_by_exchange(out_cotangent, "tp")
    count_tp, _, cols = full_cot.shape
    weight_t = weight_t.reshape(count_tp, cols, heads * DH)
    grad_out = dot("ptc,pcd->td", full_cot, weight_t).astype(BF16)
    g_heads = grad_out.reshape(tok, heads, DH)
    qg_state = dot("thd,the->hde", q_heads, g_heads)
    later = entering(qg_state, True)
    rows = jnp.arange(tok)
    causal = (rows[:, None] >= rows[None, :])[None]
    attn = jnp.where(causal, dot("thd,shd->hts", q_heads, k_heads), 0.0).astype(BF16)
    back = jnp.where(causal, dot("thd,shd->hts", g_heads, v_heads), 0.0).astype(BF16)
    attn_out = scale * (dot("hts,she->the", attn, v_heads) + dot("thd,hde->the", q_heads, prior))
    grad_q = scale * (dot("hts,shd->thd", back, k_heads) + dot("the,hde->thd", g_heads, prior))
    grad_k = scale * (dot("hts,thd->shd", back, q_heads) + dot("she,hde->shd", v_heads, later))
    grad_v = scale * (dot("hts,the->she", attn, g_heads) + dot("shd,hde->she", k_heads, later))
    width = heads * DH
    out_flat = attn_out.astype(BF16).reshape(tok, width)
    proj_term = dot("ptc,td->pcd", full_cot, out_flat).astype(BF16)
    proj_parts = lax.all_to_all(
        proj_term.reshape(seq_count, -1, width), SEQ, 0, 0, tiled=True
    )
    proj_sum = jnp.sum(proj_parts.astype(F32), axis=0)
    grad_proj = (proj_sum / jnp.sqrt(F32(tok * seq_count))).T
    return (
        grad_q.astype(BF16).reshape(tok, width),
        grad_k.astype(BF16).reshape(tok, width),
        grad_v.astype(BF16).reshape(tok, width),
        grad_proj,
    )


def solution(mesh):
    seq, tp = mesh.devices.shape
    inner = 8
    grid = Mesh(mesh.devices.reshape(seq // inner, inner, tp), ("y", "z", "tp"))
    tokens, weight = P(SEQ, "tp"), P("tp", SEQ)
    return jax.shard_map(
        per_device,
        mesh=grid,
        in_specs=(tokens, tokens, tokens, tokens, weight),
        out_specs=(tokens, tokens, tokens, weight),
        check_vma=False,
    )
```

time: 673 us -> 194 us (0.29)
  waiting for transfers between devices: 575 us -> 82.1 us
  other arithmetic: 65.2 us -> 0.98 us
  blocking collectives: 0 us -> 43.6 us
  starting transfers between devices: 0.2 us -> 23.4 us
    all_gather x4 -> x1, waiting for transfers between devices: 392 us -> 0.02 us  [per_device(): weight_t = lax.all_gather(weight_z, 'y', axis=0, tiled=True)]
    reduce_scatter x1 -> x0, waiting for transfers between devices: 182 us -> none  [per_device(): lax.psum_scatter(proj_term, 'seq', scatter_dimension=1, tiled=True)]
    all_to_all x0 -> x5, waiting for transfers between devices: none -> 82 us  [the longest x1 38.2 us: per_device(): lax.all_to_all(proj_term.reshape(seq_count, -1, width), SEQ, 0, 0, tiled=...]
    add x63 -> x0, other arithmetic: 63.7 us -> none  [add_pair(): return earlier + later_one]
    all_to_all x0 -> x2, blocking collectives: none -> 43.6 us  [the longest x1 22.1 us: gather_by_exchange(): return lax.all_to_all(copies, axis, 0, 0, tiled=True)]
    all_to_all x0 -> x5, starting transfers between devices: none -> 23.3 us  [the longest x2 9.24 us: entering(): back = lax.all_to_all(sums, SEQ, 0, 0, tiled=True)]
  transfers between devices with their start and end apart: 5 -> 6, of which waited for: 5 -> 5; matrix products, arithmetic and copies ran while one was open for 12% -> 11% of each run, Pallas kernels for 0% -> 1%
where the time goes in v1:
time: 194 us; the launch traced here: 190 us
  waiting for transfers between devices  82.1 us (42%)
  blocking collectives  43.6 us (22%)
  starting transfers between devices  23.4 us (12%)
  matrix products  14.8 us (8%)
  between operations  14.2 us (7%)
  local copies, waits for them, and re-layouts  7.95 us (4%)
  Pallas kernels  3.4 us (2%)
    all_to_all x1, waiting for transfers between devices, per_device(): lax.all_to_all(proj_term.reshape(seq_count, -1, width), SEQ, 0, 0, tiled=...  38.2 us
    all_to_all x1, blocking collectives, gather_by_exchange(): return lax.all_to_all(copies, axis, 0, 0, tiled=True)  22.1 us
    all_to_all x1, blocking collectives, entering(): mine = lax.all_to_all(pieces, SEQ, 0, 0, tiled=True)  21.5 us
    all_to_all x2, waiting for transfers between devices, entering(): back = lax.all_to_all(sums, SEQ, 0, 0, tiled=True)  20 us
    dot_general x14, matrix products, dot(): return jnp.einsum(spec, a, b, preferred_element_type=F32)  14.8 us
    all_to_all x1, waiting for transfers between devices, entering(): mine = lax.all_to_all(pieces, SEQ, 0, 0, tiled=True)  12.1 us
    all_to_all x1, waiting for transfers between devices, gather_by_exchange(): return lax.all_to_all(copies, axis, 0, 0, tiled=True)  11.7 us
    all_to_all x2, starting transfers between devices, entering(): back = lax.all_to_all(sums, SEQ, 0, 0, tiled=True)  9.24 us
  transfers between devices with their start and end apart: 6, of which 5 were waited for; matrix products, arithmetic and copies ran while one was open for 11% of the time, Pallas kernels for 1%

profile of v1, /device:TPU:6, one launch (start us, length us, event | category | flops | bytes accessed | tf_op | source)
XLA Modules:
  0.0 190.4 jit_solution(685772522663619621)
XLA Ops:
  7.2 0.0 copy-start
  7.2 0.0 copy-start.8
  7.2 0.0 all-gather.2.cloned.1.call-start
  7.2 0.8 broadcast_in_dim.35
  8.1 22.1 %all_to_all.35 = bf16[8,32,512]{2,1,0:T(8,128)(2,1)} all-to-all(bf16[8,32,512]{2,1,0:T(8,128)(2,1)S(1)} %broadcast_in_dim.35), channel_id=1, replica_groups=mesh['y'=8,'z'=8,'tp'=8] {'z'}, dimensions={0} | all-to-all | bytes 524288 | tf_op jit(solution)/shard_map/all_to_all | solution.py:17
  30.2 0.0 all-gather.2.cloned.1.call-update
  30.2 1.1 copy.61
  31.3 0.0 copy-start.1
  31.3 1.3 convolution_convert_fusion.2
  32.6 21.5 %all_to_all.36.i = bf16[64,8,128]{2,1,0:T(8,128)(2,1)} all-to-all(bf16[64,8,128]{2,1,0:T(8,128)(2,1)S(1)} %bitcast.137), channel_id=1, replica_groups=mesh['y'=8,'z'=8,'tp'=8] {'y','z'}, dimensions={0} | all-to-all | bytes 262144 | tf_op jit(solution)/shard_map/all_to_all | solution.py:33
  54.1 1.0 broadcast_in_dim.34
  55.1 4.8 %all-to-all-start = ((bf16[8,256,256]{2,1,0:T(8,128)(2,1)}), bf16[8,256,256]{2,1,0:T(8,128)(2,1)S(1)}, u32[]{:S(2)}, u32[]{:S(2)}) async-start(bf16[8,256,256]{2,1,0:T(8,128)(2,1)} %broadcast_in_dim.34), calls=%async_computation | async-start | bytes 2097152 | tf_op jit(solution)/shard_map/all_to_all | solution.py:17
  60.0 0.0 copy-start.7
  60.0 0.3 fusion.1
  60.3 1.8 shard_map.84
  62.1 11.7 %all-to-all-done = bf16[8,256,256]{2,1,0:T(8,128)(2,1)S(1)} async-done(((bf16[8,256,256]{2,1,0:T(8,128)(2,1)}), bf16[8,256,256]{2,1,0:T(8,128)(2,1)S(1)}, u32[]{:S(2)}, u32[]{:S(2)}) %all-to-all-start) | async-done | bytes 1048608 | tf_op jit(solution)/shard_map/all_to_all | solution.py:17
  73.8 4.6 %all-to-all-start.3 = ((bf16[64,8,128]{2,1,0:T(8,128)(2,1)}), bf16[64,8,128]{2,1,0:T(8,128)(2,1)S(1)}, u32[]{:S(2)}, u32[]{:S(2)}) async-start(bf16[64,8,128]{2,1,0:T(8,128)(2,1)} %shard_map.84), calls=%async_computation.3 | async-start | bytes 262144 | tf_op jit(solution)/shard_map/all_to_all | solution.py:38
  78.5 0.0 all-gather.2.cloned.1.call-done
  78.5 2.3 %fusion.13 = bf16[256,512]{1,0:T(8,128)(2,1)S(1)} fusion(bf16[8,256,256]{2,1,0:T(8,128)(2,1)S(1)} %all-to-all-done, bf16[8,256,512]{2,1,0:T(8,128)(2,1)} %bitcast.139), kind=kOutput, calls=%fused_computation.25 | convolution fusion | flops 537001984 | bytes 3407872 | tf_op jit(solution)/shard_map/ptc,pcd->td/dot_general | solution.py:43
  80.8 0.1 copy.60
  80.9 0.9 convolution_convert_fusion.1
  81.9 9.4 %all-to-all-done.3 = bf16[64,8,128]{2,1,0:T(8,128)(2,1)S(1)} async-done(((bf16[64,8,128]{2,1,0:T(8,128)(2,1)}), bf16[64,8,128]{2,1,0:T(8,128)(2,1)S(1)}, u32[]{:S(2)}, u32[]{:S(2)}) %all-to-all-start.3) | async-done | bytes 131104 | tf_op jit(solution)/shard_map/all_to_all | solution.py:38
  91.3 4.6 %all-to-all-start.4 = ((bf16[64,8,128]{2,1,0:T(8,128)(2,1)}), bf16[64,8,128]{2,1,0:T(8,128)(2,1)S(1)}, u32[]{:S(2)}, u32[]{:S(2)}) async-start(bf16[64,8,128]{2,1,0:T(8,128)(2,1)} %bitcast.10), calls=%async_computation.4 | async-start | bytes 262144 | tf_op jit(solution)/shard_map/all_to_all | solution.py:33
  95.9 0.0 copy-done.3
  95.9 0.3 convolution_bitcast_fusion.2
  96.2 0.3 fusion.10
  96.5 12.1 %all-to-all-done.4.i = bf16[64,8,128]{2,1,0:T(8,128)(2,1)S(1)} async-done(((bf16[64,8,128]{2,1,0:T(8,128)(2,1)}), bf16[64,8,128]{2,1,0:T(8,128)(2,1)S(1)}, u32[]{:S(2)}, u32[]{:S(2)}) %all-to-all-start.4) | async-done | bytes 131104 | tf_op jit(solution)/shard_map/all_to_all | solution.py:33
  108.6 0.7 copy-done.6
  109.3 1.6 shard_map.85
  110.9 4.6 %all-to-all-start.5 = ((bf16[64,8,128]{2,1,0:T(8,128)(2,1)}), bf16[64,8,128]{2,1,0:T(8,128)(2,1)S(1)}, u32[]{:S(2)}, u32[]{:S(2)}) async-start(bf16[64,8,128]{2,1,0:T(8,128)(2,1)} %shard_map.85), calls=%async_computation.5 | async-start | bytes 262144 | tf_op jit(solution)/shard_map/all_to_all | solution.py:38
  115.5 2.1 %convolution_convert_fusion = bf16[512,8,256]{0,2,1:T(8,128)(2,1)} fusion(bf16[256,512,1]{0,1,2:T(8,128)(2,1)S(1)} %bitcast.136, bf16[8,256,256]{2,1,0:T(8,128)(2,1)S(1)} %all-to-all-done), kind=kOutput, calls=%fused_computation.1 | convolution fusion | flops 537919488 | bytes 3407872 | tf_op jit(solution)/shard_map/ptc,td->pcd/dot_general | solution.py:43
  117.6 10.6 %all-to-all-done.5 = bf16[64,8,128]{2,1,0:T(8,128)(2,1)S(1)} async-done(((bf16[64,8,128]{2,1,0:T(8,128)(2,1)}), bf16[64,8,128]{2,1,0:T(8,128)(2,1)S(1)}, u32[]{:S(2)}, u32[]{:S(2)}) %all-to-all-start.5) | async-done | bytes 131104 | tf_op jit(solution)/shard_map/all_to_all | solution.py:38
  128.2 0.7 copy-done.4
  128.9 4.7 %all-to-all-start.6 = ((bf16[64,32,512]{2,1,0:T(8,128)(2,1)}), bf16[64,32,512]{2,1,0:T(8,128)(2,1)S(1)}, u32[]{:S(2)}, u32[]{:S(2)}) async-start(bf16[64,32,512]{2,1,0:T(8,128)(2,1)} %bitcast.21), calls=%async_computation.6 | async-start | bytes 4194304 | tf_op jit(solution)/shard_map/all_to_all | solution.py:76
  133.6 1.2 fusion
  134.8 1.3 convolution_bitcast_fusion.5
  136.0 0.9 fusion.12
  137.0 1.8 copy.52
  138.8 0.3 convolution_bitcast_fusion
  139.1 0.0 copy-start.2
  139.1 2.1 %fusion.30 = f32[4,128,256]{2,1,0:T(8,128)} fusion(bf16[256,4,128]{0,2,1:T(8,128)(2,1)S(1)} %bitcast.128, bf16[4,256,256]{2,1,0:T(8,128)(2,1)} %copy-done.3), kind=kOutput, calls=%fused_computation.46 | convolution fusion | flops 67108864 | bytes 1310720 | tf_op jit(solution)/shard_map/hts,the->she/dot_general | solution.py:43
  141.2 0.2 fusion.11
  141.4 0.8 copy.53
  142.3 1.3 fusion.9
  143.6 0.8 copy.54
  144.4 38.2 %all-to-all-done.6 = bf16[64,32,512]{2,1,0:T(8,128)(2,1)S(1)} async-done(((bf16[64,32,512]{2,1,0:T(8,128)(2,1)}), bf16[64,32,512]{2,1,0:T(8,128)(2,1)S(1)}, u32[]{:S(2)}, u32[]{:S(2)}) %all-to-all-start.6) | async-done | bytes 2097184 | tf_op jit(solution)/shard_map/all_to_all | solution.py:76
  182.6 0.3 convert_reduce_fusion
  182.9 0.6 multiply_bitcast_fusion
  (11 shorter events, 0.0 us)
Async XLA Ops:
  7.2 52.8 %copy-start = (bf16[256,512]{1,0:T(8,128)(2,1)S(1)}, bf16[256,512]{1,0:T(8,128)(2,1)}, u32[]{:S(2)}) copy-start(bf16[256,512]{1,0:T(8,128)(2,1)} %param.5) | copy-start | bytes 786436
  7.2 46.9 %copy-start.8 = (bf16[256,256]{1,0:T(8,128)(2,1)S(1)}, bf16[256,256]{1,0:T(8,128)(2,1)}, u32[]{:S(2)}) copy-start(bf16[256,256]{1,0:T(8,128)(2,1)} %param.8) | copy-start | bytes 393220
  7.2 71.3 %all-gather.2.cloned.1.call-start = ((), (), s32[]{:S(2)}) async-start(), calls=%async_computation.7 | async-start | bytes 2359296 | tf_op jit(solution)/shard_map/all_gather | solution.py:55
  31.3 28.7 %copy-start.1 = (bf16[256,512]{1,0:T(8,128)(2,1)S(1)}, bf16[256,512]{1,0:T(8,128)(2,1)}, u32[]{:S(2)}) copy-start(bf16[256,512]{1,0:T(8,128)(2,1)} %param.6) | copy-start | bytes 786436
  55.1 18.7 %all-to-all-start = ((bf16[8,256,256]{2,1,0:T(8,128)(2,1)}), bf16[8,256,256]{2,1,0:T(8,128)(2,1)S(1)}, u32[]{:S(2)}, u32[]{:S(2)}) async-start(bf16[8,256,256]{2,1,0:T(8,128)(2,1)} %broadcast_in_dim.34), calls=%async_computation | async-start | bytes 2097152 | tf_op jit(solution)/shard_map/all_to_all | solution.py:17
  60.0 13.9 %copy-start.7 = (pred[256,256]{1,0:T(8,128)(4,1)}, pred[256,256]{1,0:T(8,128)(4,1)S(1)}, u32[]{:S(2)}) copy-start(pred[256,256]{1,0:T(8,128)(4,1)S(1)} %iota_compare_fusion) | copy-start | bytes 196612
  60.3 35.6 %copy-start.3 = (bf16[4,256,256]{2,1,0:T(8,128)(2,1)}, bf16[4,256,256]{2,1,0:T(8,128)(2,1)S(1)}, u32[]{:S(2)}) copy-start(bf16[4,256,256]{2,1,0:T(8,128)(2,1)S(1)} %fusion.1) | copy-start | bytes 1572868
  73.8 17.5 %all-to-all-start.3 = ((bf16[64,8,128]{2,1,0:T(8,128)(2,1)}), bf16[64,8,128]{2,1,0:T(8,128)(2,1)S(1)}, u32[]{:S(2)}, u32[]{:S(2)}) async-start(bf16[64,8,128]{2,1,0:T(8,128)(2,1)} %shard_map.84), calls=%async_computation.3 | async-start | bytes 262144 | tf_op jit(solution)/shard_map/all_to_all | solution.py:38
  91.3 17.3 %all-to-all-start.4 = ((bf16[64,8,128]{2,1,0:T(8,128)(2,1)}), bf16[64,8,128]{2,1,0:T(8,128)(2,1)S(1)}, u32[]{:S(2)}, u32[]{:S(2)}) async-start(bf16[64,8,128]{2,1,0:T(8,128)(2,1)} %bitcast.10), calls=%async_computation.4 | async-start | bytes 262144 | tf_op jit(solution)/shard_map/all_to_all | solution.py:33
  108.6 0.7 copy-start.6
  110.9 17.3 %all-to-all-start.5 = ((bf16[64,8,128]{2,1,0:T(8,128)(2,1)}), bf16[64,8,128]{2,1,0:T(8,128)(2,1)S(1)}, u32[]{:S(2)}, u32[]{:S(2)}) async-start(bf16[64,8,128]{2,1,0:T(8,128)(2,1)} %shard_map.85), calls=%async_computation.5 | async-start | bytes 262144 | tf_op jit(solution)/shard_map/all_to_all | solution.py:38
  128.2 0.7 copy-start.4
  128.9 53.7 %all-to-all-start.6 = ((bf16[64,32,512]{2,1,0:T(8,128)(2,1)}), bf16[64,32,512]{2,1,0:T(8,128)(2,1)S(1)}, u32[]{:S(2)}, u32[]{:S(2)}) async-start(bf16[64,32,512]{2,1,0:T(8,128)(2,1)} %bitcast.21), calls=%async_computation.6 | async-start | bytes 4194304 | tf_op jit(solution)/shard_map/all_to_all | solution.py:76
  136.9 4.2 %copy-start.5 = (bf16[64,8,128]{2,1,0:T(8,128)(2,1)S(1)}, bf16[64,8,128]{2,1,0:T(8,128)(2,1)}, u32[]{:S(2)}) copy-start(bf16[64,8,128]{2,1,0:T(8,128)(2,1)} %copy-done.4) | copy-start | bytes 393220
  139.1 3.2 %copy-start.2 = (bf16[256,512]{1,0:T(8,128)(2,1)S(1)}, bf16[256,512]{1,0:T(8,128)(2,1)}, u32[]{:S(2)}) copy-start(bf16[256,512]{1,0:T(8,128)(2,1)} %param.6) | copy-start | bytes 786436
Sparse Core Ops, SparseCore 0:
  30.3 41.0 all-gather.1

commit v2 on v1

v2 whole, which is shorter than its diff:
```python
import functools

import jax
import jax.numpy as jnp
from jax import lax
from jax.experimental import pallas as pl
from jax.experimental.pallas import tpu as pltpu
from jax.sharding import Mesh, PartitionSpec as P

DH = 128
SEQ = ("y", "z")
BF16 = jnp.bfloat16
F32 = jnp.float32
VMEM_BYTES = 48 * 1024 * 1024


def mm(a, b, ca, cb):
    return lax.dot_general(a, b, (((ca,), (cb,)), ((), ())), preferred_element_type=F32)


def head(h):
    return slice(h * DH, (h + 1) * DH)


def local_call(kernel, out_shape, flops, moved, **kwargs):
    return pl.pallas_call(
        kernel,
        out_shape=out_shape,
        cost_estimate=pl.CostEstimate(flops=flops, transcendentals=0, bytes_accessed=moved),
        compiler_params=pltpu.CompilerParams(vmem_limit_bytes=VMEM_BYTES),
        **kwargs,
    )


def causal(tok):
    rows = lax.broadcasted_iota(jnp.int32, (tok, tok), 0)
    cols = lax.broadcasted_iota(jnp.int32, (tok, tok), 1)
    return rows >= cols


def exchange(x, axis):
    return lax.all_to_all(x, axis, 0, 0, tiled=True)


def first_kernel(k_ref, v_ref, w_ref, out_ref):
    peers, rows, width = out_ref.shape
    own = w_ref.shape[0]
    share = rows - own
    for h in range(width // DH):
        kv = mm(k_ref[:, head(h)], v_ref[:, head(h)], 0, 0).astype(BF16)
        for p in range(peers):
            out_ref[p, own:, head(h)] = kv[p * share : (p + 1) * share]
    for p in range(peers):
        out_ref[p, :own, :] = w_ref[...]


def split_kernel(got_ref, weight_ref, part_ref, total_ref):
    peers, rows, width = got_ref.shape
    own = weight_ref.shape[0] // peers
    running = jnp.zeros((rows - own, width), F32)
    for p in range(peers):
        weight_ref[p * own : (p + 1) * own, :] = got_ref[p, :own, :]
        part_ref[p] = running
        running = running + got_ref[p, own:, :].astype(F32)
    for p in range(total_ref.shape[0]):
        total_ref[p] = running


def back_scan_kernel(got_ref, part_ref, total_ref):
    peers, rows, width = got_ref.shape
    running = jnp.zeros((rows, width), F32)
    for p in reversed(range(peers)):
        part_ref[p] = running
        running = running + got_ref[p].astype(F32)
    for p in range(total_ref.shape[0]):
        total_ref[p] = running


def join_kernel(reverse, place_ref, totals_ref, part_ref, out_ref):
    place = place_ref[0]
    base = jnp.zeros(totals_ref.shape[1:], F32)
    for other in range(totals_ref.shape[0]):
        counts = place < other if reverse else place > other
        base = base + jnp.where(counts, totals_ref[other], 0.0)
    for p in range(part_ref.shape[0]):
        out_ref[p] = (base + part_ref[p]).astype(out_ref.dtype)


def attn_kernel(q_ref, k_ref, v_ref, attn_ref, inner_ref):
    mask = causal(q_ref.shape[0])
    for h in range(q_ref.shape[1] // DH):
        scores = mm(q_ref[:, head(h)], k_ref[:, head(h)], 1, 1)
        attn = jnp.where(mask, scores, 0.0).astype(BF16)
        attn_ref[h] = attn
        inner_ref[:, head(h)] = mm(attn, v_ref[:, head(h)], 1, 0)


def proj_kernel(scale, q_ref, prior_ref, inner_ref, cot_ref, out_ref, attn_out_ref):
    @pl.when(pl.program_id(0) == 0)
    def _():
        for h in range(q_ref.shape[1] // DH):
            far = mm(q_ref[:, head(h)], prior_ref[:, head(h)], 1, 0)
            attn_out_ref[:, head(h)] = (scale * (inner_ref[:, head(h)] + far)).astype(BF16)

    out_ref[...] = mm(cot_ref[0], attn_out_ref[...], 0, 0)


def grad_out_kernel(cot_ref, w_ref, q_ref, g_ref, qg_ref, acc_ref):
    step = pl.program_id(0)
    term = mm(cot_ref[0], w_ref[...], 1, 0)

    @pl.when(step == 0)
    def _():
        acc_ref[...] = term

    @pl.when(step > 0)
    def _():
        acc_ref[...] += term

    @pl.when(step == pl.num_programs(0) - 1)
    def _():
        g = acc_ref[...].astype(BF16)
        g_ref[...] = g
        for h in range(g.shape[1] // DH):
            qg_ref[:, head(h)] = mm(q_ref[:, head(h)], g[:, head(h)], 0, 0).astype(BF16)


def inner_grads_kernel(scale, q_ref, k_ref, v_ref, g_ref, attn_ref, prior_ref, dq_ref, dk_ref, dv_ref):
    mask = causal(q_ref.shape[0])
    for h in range(q_ref.shape[1] // DH):
        g = g_ref[:, head(h)]
        back = jnp.where(mask, mm(g, v_ref[:, head(h)], 1, 1), 0.0).astype(BF16)
        near = mm(back, k_ref[:, head(h)], 1, 0)
        far = mm(g, prior_ref[:, head(h)], 1, 1)
        dq_ref[:, head(h)] = (scale * (near + far)).astype(BF16)
        dk_ref[:, head(h)] = mm(back, q_ref[:, head(h)], 0, 0)
        dv_ref[:, head(h)] = mm(attn_ref[h], g, 0, 0)


def outer_grads_kernel(scale, k_ref, v_ref, later_ref, near_k_ref, near_v_ref, dk_ref, dv_ref):
    for h in range(k_ref.shape[1] // DH):
        later = later_ref[:, head(h)]
        far_k = mm(v_ref[:, head(h)], later, 1, 1)
        dk_ref[:, head(h)] = (scale * (near_k_ref[:, head(h)] + far_k)).astype(BF16)
        far_v = mm(k_ref[:, head(h)], later, 1, 0)
        dv_ref[:, head(h)] = (scale * (near_v_ref[:, head(h)] + far_v)).astype(BF16)


def shape(dims, dtype):
    return jax.ShapeDtypeStruct(dims, dtype)


def join(place, totals, part, reverse):
    return local_call(
        functools.partial(join_kernel, reverse),
        shape(part.shape, BF16),
        0,
        3 * part.size * 4,
        in_specs=[
            pl.BlockSpec(memory_space=pltpu.SMEM),
            pl.BlockSpec(memory_space=pltpu.VMEM),
            pl.BlockSpec(memory_space=pltpu.VMEM),
        ],
    )(place, totals, part)


def per_device(queries, keys, values, out_cotangent, proj_weight):
    tok, width = queries.shape
    heads = width // DH
    ny, nz = lax.axis_size("y"), lax.axis_size("z")
    nx, nc = lax.axis_size("x"), lax.axis_size("c")
    cols = out_cotangent.shape[1]
    scale = (DH * tok * ny * nz) ** -0.5
    place = lax.axis_index("y").reshape(1)
    weight_t = proj_weight.T
    own = weight_t.shape[0]
    share = DH // nz
    square = 2 * tok * DH * DH * heads
    wide = 2 * tok * tok * DH * heads
    big = tok * width

    sent = local_call(
        first_kernel, shape((nz, own + share, width), BF16), square, 3 * big
    )(keys, values, weight_t)
    got = exchange(sent, "z")
    weight_z, kv_part, kv_total = local_call(
        split_kernel,
        (
            shape((nz * own, width), BF16),
            shape((nz, share, width), F32),
            shape((ny, share, width), F32),
        ),
        0,
        2 * big,
    )(got)
    weight_full = lax.all_gather(weight_z, "y", axis=0, tiled=True)
    cot_own, kv_total = lax.optimization_barrier((out_cotangent, kv_total))
    cot_c = lax.all_gather(cot_own, "c")
    cot_all = exchange(jnp.broadcast_to(cot_c[None], (nx,) + cot_c.shape), "x")
    attn, attn_inner = local_call(
        attn_kernel,
        (shape((heads, tok, tok), BF16), shape((tok, width), F32)),
        2 * wide,
        10 * big,
    )(queries, keys, values)
    prior = exchange(join(place, exchange(kv_total, "y"), kv_part, False), "z")
    prior = prior.reshape(DH, width)

    n_blocks = nx * nc
    cot_blocks = cot_all.reshape(n_blocks, tok, cols)

    whole = pl.BlockSpec((tok, width), lambda i: (0, 0))
    state = pl.BlockSpec((DH, width), lambda i: (0, 0))
    cot_spec = pl.BlockSpec((1, tok, cols), lambda i: (i, 0, 0))
    by_block = pl.BlockSpec((cols, width), lambda i: (i, 0))
    proj_term = local_call(
        functools.partial(proj_kernel, scale),
        shape((n_blocks * cols, width), F32),
        square + 2 * tok * cols * width * n_blocks,
        4 * n_blocks * cols * width,
        grid=(n_blocks,),
        in_specs=[whole, state, whole, cot_spec],
        out_specs=by_block,
        scratch_shapes=[pltpu.VMEM((tok, width), BF16)],
    )(queries, prior, attn_inner, cot_blocks)
    proj_y = lax.psum_scatter(proj_term, "y", scatter_dimension=0, tiled=True)

    grad_out, qg = local_call(
        grad_out_kernel,
        (shape((tok, width), BF16), shape((DH, width), BF16)),
        square + 2 * tok * cols * width * n_blocks,
        2 * n_blocks * cols * width,
        grid=(n_blocks,),
        in_specs=[cot_spec, by_block, whole],
        out_specs=[whole, state],
        scratch_shapes=[pltpu.VMEM((tok, width), F32)],
    )(cot_blocks, weight_full, queries)
    qg_got = exchange(qg.reshape(nz, share, width), "z")
    qg_part, qg_total = local_call(
        back_scan_kernel,
        (shape((nz, share, width), F32), shape((ny, share, width), F32)),
        0,
        2 * big,
    )(qg_got)
    grad_q, near_k, near_v = local_call(
        functools.partial(inner_grads_kernel, scale),
        (shape((tok, width), BF16), shape((tok, width), F32), shape((tok, width), F32)),
        4 * wide + square,
        16 * big,
    )(queries, keys, values, grad_out, attn, prior)
    later = exchange(join(place, exchange(qg_total, "y"), qg_part, True), "z")
    later = later.reshape(DH, width)
    grad_k, grad_v = local_call(
        functools.partial(outer_grads_kernel, scale),
        (shape((tok, width), BF16), shape((tok, width), BF16)),
        2 * square,
        12 * big,
    )(keys, values, later, near_k, near_v)

    proj_parts = exchange(proj_y.astype(BF16).reshape(nz, own, width), "z")
    proj_sum = jnp.sum(proj_parts.astype(F32), axis=0)
    grad_proj = (proj_sum / jnp.sqrt(F32(tok * ny * nz))).T
    return grad_q, grad_k, grad_v, grad_proj


def solution(mesh):
    seq, tp = mesh.devices.shape
    inner, cores = 8, 2
    grid = Mesh(
        mesh.devices.reshape(seq // inner, inner, tp // cores, cores), ("y", "z", "x", "c")
    )
    tokens, weight = P(SEQ, ("x", "c")), P(("x", "c"), SEQ)
    return jax.shard_map(
        per_device,
        mesh=grid,
        in_specs=(tokens, tokens, tokens, tokens, weight),
        out_specs=(tokens, tokens, tokens, weight),
        check_vma=False,
    )
```

time: 194 us -> 175 us (0.902); the launches traced: 190 us -> 174 us
  waiting for transfers between devices: 82.1 us -> 55.8 us
  matrix products: 14.8 us -> 0 us
  blocking collectives: 43.6 us -> 57.1 us
  Pallas kernels: 3.4 us -> 10.9 us
  starting transfers between devices: 23.4 us -> 26 us
    all_to_all x5, waiting for transfers between devices: 82 us -> 36.3 us  [exchange(): return lax.all_to_all(x, axis, 0, 0, tiled=True)]
    reduce_scatter x0 -> x1, waiting for transfers between devices: none -> 19.4 us  [per_device(): proj_y = lax.psum_scatter(proj_term, 'y', scatter_dimension=0, tiled=True)]
    dot_general x14 -> x0, matrix products: 14.8 us -> none  [dot(): return jnp.einsum(spec, a, b, preferred_element_type=F32)]
    all_to_all x2 -> x3, blocking collectives: 43.6 us -> 54.8 us  [exchange(): return lax.all_to_all(x, axis, 0, 0, tiled=True)]
    pallas_call x2 -> x10, Pallas kernels: 3.4 us -> 10.9 us  [the longest x1 2.49 us: per_device(): local_call(grad_out_kernel, (shape((tok, width), BF16), shape((DH, width)...]
    all_to_all x5, starting transfers between devices: 23.3 us -> 26 us  [exchange(): return lax.all_to_all(x, axis, 0, 0, tiled=True)]
    all_gather x0 -> x1, blocking collectives: none -> 2.21 us  [per_device(): cot_c = lax.all_gather(cot_own, 'c')]
    unnamed x21 -> x16, local copies, waits for them, and re-layouts: 4.87 us -> 6.22 us
  transfers between devices with their start and end apart: 6 -> 7, of which waited for: 5 -> 5; matrix products, arithmetic and copies ran while one was open for 11% -> 2% of each run, Pallas kernels for 1% -> 6%
where the time goes in v2:
time: 175 us; the launch traced here: 174 us
  blocking collectives  57.1 us (33%)
  waiting for transfers between devices  55.8 us (32%)
  starting transfers between devices  26 us (15%)
  between operations  14.1 us (8%)
  Pallas kernels  10.9 us (6%)
  local copies, waits for them, and re-layouts  7.28 us (4%)
  other arithmetic  2.46 us (1%)
    all_to_all x3, blocking collectives, exchange(): return lax.all_to_all(x, axis, 0, 0, tiled=True)  54.8 us
    all_to_all x5, waiting for transfers between devices, exchange(): return lax.all_to_all(x, axis, 0, 0, tiled=True)  36.3 us
    all_to_all x5, starting transfers between devices, exchange(): return lax.all_to_all(x, axis, 0, 0, tiled=True)  26 us
    reduce_scatter x1, waiting for transfers between devices, per_device(): proj_y = lax.psum_scatter(proj_term, 'y', scatter_dimension=0, tiled=True)  19.4 us
    unnamed x16, local copies, waits for them, and re-layouts  6.22 us
  transfers between devices with their start and end apart: 7, of which 5 were waited for; matrix products, arithmetic and copies ran while one was open for 2% of the time, Pallas kernels for 6%

profile of v2, /device:TPU:6, one launch (start us, length us, event | category | flops | bytes accessed | tf_op | source)
XLA Modules:
  0.0 173.7 jit_solution(2733252434069273896)
XLA Ops:
  7.2 0.0 copy-start.1
  7.2 0.0 all-gather.3.cloned.1.call-start
  7.2 0.0 copy-start.2
  7.2 1.0 copy-done.2
  8.2 0.0 copy-start.4
  8.2 0.9 copy-done.4
  9.2 0.0 copy-start.7
  9.2 0.8 copy-done.7
  9.9 0.0 copy-start.3
  9.9 0.0 copy-start.5
  9.9 0.3 shard_map.84
  10.2 24.8 %all_to_all.40.got_ref = bf16[8,48,512]{2,1,0:T(8,128)(2,1)S(1)} all-to-all(bf16[8,48,512]{2,1,0:T(8,128)(2,1)S(1)} %shard_map.84), channel_id=1, replica_groups=mesh['y'=8,'z'=8,'x'=4,'c'=2] {'z'}, dimensions={0} | all-to-all | bytes 786432 | tf_op jit(solution)/shard_map/all_to_all | solution.py:42
  35.0 0.8 shard_map.85
  35.8 0.0 all-gather.3.cloned.1.call-update
  35.8 7.1 %all-to-all-start.2 = ((f32[8,16,512]{2,1,0:T(8,128)}), f32[8,16,512]{2,1,0:T(8,128)S(1)}, u32[]{:S(2)}, u32[]{:S(2)}) async-start(f32[8,16,512]{2,1,0:T(8,128)} %get-tuple-element.25), calls=%async_computation.2 | async-start | bytes 524288 | tf_op jit(solution)/shard_map/all_to_all | solution.py:42
  42.9 12.5 %all-to-all-done.2.totals_ref = f32[8,16,512]{2,1,0:T(8,128)S(1)} async-done(((f32[8,16,512]{2,1,0:T(8,128)}), f32[8,16,512]{2,1,0:T(8,128)S(1)}, u32[]{:S(2)}, u32[]{:S(2)}) %all-to-all-start.2) | async-done | bytes 262176 | tf_op jit(solution)/shard_map/all_to_all | solution.py:42
  55.4 0.7 shard_map.88
  56.1 3.4 %all-to-all-start.3 = ((bf16[8,16,512]{2,1,0:T(8,128)(2,1)}), bf16[8,16,512]{2,1,0:T(8,128)(2,1)S(1)}, u32[]{:S(2)}, u32[]{:S(2)}) async-start(bf16[8,16,512]{2,1,0:T(8,128)(2,1)} %shard_map.88), calls=%async_computation.3 | async-start | bytes 262144 | tf_op jit(solution)/shard_map/all_to_all | solution.py:42
  59.5 2.2 %all-gather = bf16[512,256]{1,0:T(8,128)(2,1)S(1)} all-gather(bf16[256,256]{1,0:T(8,128)(2,1)} %param.8), channel_id=2, replica_groups=mesh['y'=8,'z'=8,'x'=4,'c'=2] {'c'}, dimensions={0}, use_global_device_ids=true | all-gather | bytes 393216 | tf_op jit(solution)/shard_map/all_gather | solution.py:198
  61.7 6.8 %all-to-all-done.3 = bf16[8,16,512]{2,1,0:T(8,128)(2,1)S(1)} async-done(((bf16[8,16,512]{2,1,0:T(8,128)(2,1)}), bf16[8,16,512]{2,1,0:T(8,128)(2,1)S(1)}, u32[]{:S(2)}, u32[]{:S(2)}) %all-to-all-start.3) | async-done | bytes 131104 | tf_op jit(solution)/shard_map/all_to_all | solution.py:42
  68.5 1.1 broadcast_in_dim.2
  69.5 4.8 %all-to-all-start.1 = ((bf16[4,2,256,256]{3,2,1,0:T(8,128)(2,1)}), bf16[4,2,256,256]{3,2,1,0:T(8,128)(2,1)S(1)}, u32[]{:S(2)}, u32[]{:S(2)}) async-start(bf16[4,2,256,256]{3,2,1,0:T(8,128)(2,1)} %broadcast_in_dim.2), calls=%async_computation.1 | async-start | bytes 2097152 | tf_op jit(solution)/shard_map/all_to_all | solution.py:42
  74.3 0.0 reduce-scatter.2.cloned.1.call-start
  74.3 0.0 copy-done.1
  74.3 0.0 copy-done.3
  74.3 0.0 copy-done.5
  74.3 0.7 shard_map.87
  75.0 8.1 %all-to-all-done.1 = bf16[4,2,256,256]{3,2,1,0:T(8,128)(2,1)S(1)} async-done(((bf16[4,2,256,256]{3,2,1,0:T(8,128)(2,1)}), bf16[4,2,256,256]{3,2,1,0:T(8,128)(2,1)S(1)}, u32[]{:S(2)}, u32[]{:S(2)}) %all-to-all-start.1) | async-done | bytes 1048608 | tf_op jit(solution)/shard_map/all_to_all | solution.py:42
  83.2 2.2 %shard_map.93 = f32[2048,512]{1,0:T(8,128)S(1)} custom-call(bf16[256,512]{1,0:T(8,128)(2,1)S(1)} %copy-done.1, bf16[128,512]{1,0:T(8,128)(2,1)S(1)} %bitcast.12, f32[256,512]{1,0:T(8,128)S(1)} %get-tuple-element.35.inner_ref, bf16[8,256,256]{2,1,0:T(8,128)(2,1)S(1)} %bitcast.10), custom_call_target="tpu_custom_call" | custom-call | flops 570425344 | bytes 4194304 | tf_op jit(solution)/shard_map/pallas_call | solution.py:216
  85.4 0.0 copy-start
  85.4 1.9 %copy-done = f32[2048,512]{1,0:T(8,128)} copy-done((f32[2048,512]{1,0:T(8,128)}, f32[2048,512]{1,0:T(8,128)S(1)}, u32[]{:S(2)}) %copy-start) | copy-done | bytes 4194328
  87.3 0.0 reduce-scatter.2.cloned.1.call-update
  87.4 0.0 all-gather.3.cloned.1.call-done.w_ref
  87.4 0.0 copy-start.6
  87.4 1.6 copy-done.6
  89.0 2.5 %shard_map.86 = (bf16[256,512]{1,0:T(8,128)(2,1)S(1)}, bf16[128,512]{1,0:T(8,128)(2,1)S(1)}) custom-call(bf16[8,256,256]{2,1,0:T(8,128)(2,1)S(1)} %bitcast.11, bf16[2048,512]{1,0:T(8,128)(2,1)S(1)} %copy-done.6, bf16[256,512]{1,0:T(8,128)(2,1)S(1)} %copy-done.1), custom_call_target="tpu_custom_call" | custom-call | flops 570425344 | bytes 2097152 | tf_op jit(solution)/shard_map/pallas_call | solution.py:228
  91.5 13.7 %all_to_all.41.got_ref = bf16[8,16,512]{2,1,0:T(8,128)(2,1)S(1)} all-to-all(bf16[8,16,512]{2,1,0:T(8,128)(2,1)S(1)} %bitcast.15), channel_id=1, replica_groups=mesh['y'=8,'z'=8,'x'=4,'c'=2] {'z'}, dimensions={0} | all-to-all | bytes 262144 | tf_op jit(solution)/shard_map/all_to_all | solution.py:42
  105.3 16.3 %all_to_all.42.totals_ref = f32[8,16,512]{2,1,0:T(8,128)S(1)} all-to-all(f32[8,16,512]{2,1,0:T(8,128)S(1)} %get-tuple-element.29), channel_id=1, replica_groups=mesh['y'=8,'z'=8,'x'=4,'c'=2] {'y'}, dimensions={0} | all-to-all | bytes 524288 | tf_op jit(solution)/shard_map/all_to_all | solution.py:42
  121.6 0.7 shard_map.91
  122.3 3.4 %all-to-all-start.6 = ((bf16[8,16,512]{2,1,0:T(8,128)(2,1)}), bf16[8,16,512]{2,1,0:T(8,128)(2,1)S(1)}, u32[]{:S(2)}, u32[]{:S(2)}) async-start(bf16[8,16,512]{2,1,0:T(8,128)(2,1)} %shard_map.91), calls=%async_computation.6 | async-start | bytes 262144 | tf_op jit(solution)/shard_map/all_to_all | solution.py:42
  125.7 19.4 %reduce-scatter.2.cloned.1.call-done = f32[256,512]{1,0:T(8,128)} async-done(((f32[2048,512]{1,0:T(8,128)}), f32[256,512]{1,0:T(8,128)}) %reduce-scatter.2.cloned.1.call-update) | async-done | bytes 524304 | tf_op jit(solution)/shard_map/reduce_scatter | solution.py:226
  145.1 1.8 %convert_element_type.6 = bf16[256,512]{1,0:T(8,128)(2,1)} convert(f32[256,512]{1,0:T(8,128)} %reduce-scatter.2.cloned.1.call-done) | non-fusion elementwise | flops 131072 | bytes 786432 | tf_op jit(solution)/shard_map/convert_element_type | solution.py:260
  146.9 0.0 all-to-all-done.6
  146.9 7.4 %all-to-all-start.7 = ((bf16[8,32,512]{2,1,0:T(8,128)(2,1)}), bf16[8,32,512]{2,1,0:T(8,128)(2,1)S(1)}, u32[]{:S(2)}, u32[]{:S(2)}) async-start(bf16[8,32,512]{2,1,0:T(8,128)(2,1)} %bitcast.7), calls=%async_computation.8 | async-start | bytes 524288 | tf_op jit(solution)/shard_map/all_to_all | solution.py:42
  154.2 1.9 %shard_map.89 = (bf16[256,512]{1,0:T(8,128)(2,1)}, f32[256,512]{1,0:T(8,128)S(1)}, f32[256,512]{1,0:T(8,128)S(1)}) custom-call(bf16[256,512]{1,0:T(8,128)(2,1)S(1)} %copy-done.1, bf16[256,512]{1,0:T(8,128)(2,1)S(1)} %copy-done.3, bf16[256,512]{1,0:T(8,128)(2,1)S(1)} %copy-done.5, bf16[256,512]{1,0:T(8,128)(2,1)S(1)} %get-tuple-element.23.g_ref, ...), custom_call_target="tpu_custom_call" | custom-call | flops 301989888 | bytes 2097152 | tf_op jit(solution)/shard_map/pallas_call | solution.py:245
  156.1 1.1 shard_map.92
  157.2 8.9 %all-to-all-done.7 = bf16[8,32,512]{2,1,0:T(8,128)(2,1)S(1)} async-done(((bf16[8,32,512]{2,1,0:T(8,128)(2,1)}), bf16[8,32,512]{2,1,0:T(8,128)(2,1)S(1)}, u32[]{:S(2)}, u32[]{:S(2)}) %all-to-all-start.7) | async-done | bytes 262176 | tf_op jit(solution)/shard_map/all_to_all | solution.py:42
  166.2 0.6 multiply_bitcast_fusion
  (2 shorter events, 0.1 us)
Async XLA Ops:
  7.2 67.2 %copy-start.1 = (bf16[256,512]{1,0:T(8,128)(2,1)S(1)}, bf16[256,512]{1,0:T(8,128)(2,1)}, u32[]{:S(2)}) copy-start(bf16[256,512]{1,0:T(8,128)(2,1)} %q_ref.7) | copy-start | bytes 786436
  7.2 80.2 %all-gather.3.cloned.1.call-start = ((), (), s32[]{:S(2)}) async-start(), calls=%async_computation.9 | async-start | bytes 2359296 | tf_op jit(solution)/shard_map/all_gather | solution.py:196
  7.2 1.0 copy-start.2
  8.2 0.9 copy-start.4
  9.2 0.8 copy-start.7
  9.9 64.4 %copy-start.3 = (bf16[256,512]{1,0:T(8,128)(2,1)S(1)}, bf16[256,512]{1,0:T(8,128)(2,1)}, u32[]{:S(2)}) copy-start(bf16[256,512]{1,0:T(8,128)(2,1)} %k_ref.7) | copy-start | bytes 786436
  9.9 64.4 %copy-start.5 = (bf16[256,512]{1,0:T(8,128)(2,1)S(1)}, bf16[256,512]{1,0:T(8,128)(2,1)}, u32[]{:S(2)}) copy-start(bf16[256,512]{1,0:T(8,128)(2,1)} %v_ref.7) | copy-start | bytes 786436
  35.8 19.6 %all-to-all-start.2 = ((f32[8,16,512]{2,1,0:T(8,128)}), f32[8,16,512]{2,1,0:T(8,128)S(1)}, u32[]{:S(2)}, u32[]{:S(2)}) async-start(f32[8,16,512]{2,1,0:T(8,128)} %get-tuple-element.25), calls=%async_computation.2 | async-start | bytes 524288 | tf_op jit(solution)/shard_map/all_to_all | solution.py:42
  56.1 12.4 %all-to-all-start.3 = ((bf16[8,16,512]{2,1,0:T(8,128)(2,1)}), bf16[8,16,512]{2,1,0:T(8,128)(2,1)S(1)}, u32[]{:S(2)}, u32[]{:S(2)}) async-start(bf16[8,16,512]{2,1,0:T(8,128)(2,1)} %shard_map.88), calls=%async_computation.3 | async-start | bytes 262144 | tf_op jit(solution)/shard_map/all_to_all | solution.py:42
  69.5 13.6 %all-to-all-start.1 = ((bf16[4,2,256,256]{3,2,1,0:T(8,128)(2,1)}), bf16[4,2,256,256]{3,2,1,0:T(8,128)(2,1)S(1)}, u32[]{:S(2)}, u32[]{:S(2)}) async-start(bf16[4,2,256,256]{3,2,1,0:T(8,128)(2,1)} %broadcast_in_dim.2), calls=%async_computation.1 | async-start | bytes 2097152 | tf_op jit(solution)/shard_map/all_to_all | solution.py:42
  74.3 70.7 %reduce-scatter.2.cloned.1.call-start = ((), (), s32[]{:S(2)}) async-start(), calls=%async_computation.10 | async-start | bytes 4718592 | tf_op jit(solution)/shard_map/reduce_scatter | solution.py:226
  85.4 1.9 %copy-start = (f32[2048,512]{1,0:T(8,128)}, f32[2048,512]{1,0:T(8,128)S(1)}, u32[]{:S(2)}) copy-start(f32[2048,512]{1,0:T(8,128)S(1)} %shard_map.93) | copy-start | bytes 12582916
  87.4 1.6 copy-start.6
  122.3 24.6 %all-to-all-start.6 = ((bf16[8,16,512]{2,1,0:T(8,128)(2,1)}), bf16[8,16,512]{2,1,0:T(8,128)(2,1)S(1)}, u32[]{:S(2)}, u32[]{:S(2)}) async-start(bf16[8,16,512]{2,1,0:T(8,128)(2,1)} %shard_map.91), calls=%async_computation.6 | async-start | bytes 262144 | tf_op jit(solution)/shard_map/all_to_all | solution.py:42
  146.9 19.3 %all-to-all-start.7 = ((bf16[8,32,512]{2,1,0:T(8,128)(2,1)}), bf16[8,32,512]{2,1,0:T(8,128)(2,1)S(1)}, u32[]{:S(2)}, u32[]{:S(2)}) async-start(bf16[8,32,512]{2,1,0:T(8,128)(2,1)} %bitcast.7), calls=%async_computation.8 | async-start | bytes 524288 | tf_op jit(solution)/shard_map/all_to_all | solution.py:42
Sparse Core Ops, SparseCore 0:
  35.9 40.8 all-gather.2
  87.5 57.5 reduce-scatter.1

commit v3 on v2

--- a/solution.py
+++ b/solution.py
@@ -95,19 +95,21 @@
         inner_ref[:, head(h)] = mm(attn, v_ref[:, head(h)], 1, 0)
 
 
-def proj_kernel(scale, q_ref, prior_ref, inner_ref, cot_ref, out_ref, attn_out_ref):
+def proj_kernel(scale, q_ref, prior_ref, inner_ref, top_ref, low_ref, out_ref, attn_out_ref):
     @pl.when(pl.program_id(0) == 0)
     def _():
         for h in range(q_ref.shape[1] // DH):
             far = mm(q_ref[:, head(h)], prior_ref[:, head(h)], 1, 0)
             attn_out_ref[:, head(h)] = (scale * (inner_ref[:, head(h)] + far)).astype(BF16)
 
-    out_ref[...] = mm(cot_ref[0], attn_out_ref[...], 0, 0)
-
-
-def grad_out_kernel(cot_ref, w_ref, q_ref, g_ref, qg_ref, acc_ref):
+    cot = jnp.concatenate([top_ref[0], low_ref[0]], axis=0)
+    out_ref[...] = mm(cot, attn_out_ref[...], 0, 0)
+
+
+def grad_out_kernel(top_ref, low_ref, w_ref, q_ref, g_ref, qg_ref, acc_ref):
     step = pl.program_id(0)
-    term = mm(cot_ref[0], w_ref[...], 1, 0)
+    cot = jnp.concatenate([top_ref[0], low_ref[0]], axis=0)
+    term = mm(cot, w_ref[...], 1, 0)
 
     @pl.when(step == 0)
     def _():
@@ -148,6 +150,10 @@
 
 def shape(dims, dtype):
     return jax.ShapeDtypeStruct(dims, dtype)
+
+
+def in_hbm(x):
+    return pltpu.with_memory_space_constraint(x, pltpu.HBM)
 
 
 def join(place, totals, part, reverse):
@@ -181,7 +187,7 @@
 
     sent = local_call(
         first_kernel, shape((nz, own + share, width), BF16), square, 3 * big
-    )(keys, values, weight_t)
+    )(in_hbm(keys), in_hbm(values), in_hbm(weight_t))
     got = exchange(sent, "z")
     weight_z, kv_part, kv_total = local_call(
         split_kernel,
@@ -195,8 +201,10 @@
     )(got)
     weight_full = lax.all_gather(weight_z, "y", axis=0, tiled=True)
     cot_own, kv_total = lax.optimization_barrier((out_cotangent, kv_total))
-    cot_c = lax.all_gather(cot_own, "c")
-    cot_all = exchange(jnp.broadcast_to(cot_c[None], (nx,) + cot_c.shape), "x")
+    cot_x = lax.all_gather(cot_own, "x")
+    half = tok // 2
+    cot_top = lax.all_gather(cot_x[:, :half], "c").reshape(nx * nc, half, cols)
+    cot_low = lax.all_gather(cot_x[:, half:], "c").reshape(nx * nc, half, cols)
     attn, attn_inner = local_call(
         attn_kernel,
         (shape((heads, tok, tok), BF16), shape((tok, width), F32)),
@@ -207,22 +215,24 @@
     prior = prior.reshape(DH, width)
 
     n_blocks = nx * nc
-    cot_blocks = cot_all.reshape(n_blocks, tok, cols)
+
+    def block_of(i):
+        return (i % nx) * nc + i // nx
 
     whole = pl.BlockSpec((tok, width), lambda i: (0, 0))
     state = pl.BlockSpec((DH, width), lambda i: (0, 0))
-    cot_spec = pl.BlockSpec((1, tok, cols), lambda i: (i, 0, 0))
-    by_block = pl.BlockSpec((cols, width), lambda i: (i, 0))
+    cot_spec = pl.BlockSpec((1, half, cols), lambda i: (i, 0, 0))
+    by_block = pl.BlockSpec((cols, width), lambda i: (block_of(i), 0))
     proj_term = local_call(
         functools.partial(proj_kernel, scale),
-        shape((n_blocks * cols, width), F32),
+        pltpu.HBM((n_blocks * cols, width), F32),
         square + 2 * tok * cols * width * n_blocks,
         4 * n_blocks * cols * width,
         grid=(n_blocks,),
-        in_specs=[whole, state, whole, cot_spec],
+        in_specs=[whole, state, whole, cot_spec, cot_spec],
         out_specs=by_block,
         scratch_shapes=[pltpu.VMEM((tok, width), BF16)],
-    )(queries, prior, attn_inner, cot_blocks)
+    )(queries, prior, attn_inner, cot_top, cot_low)
     proj_y = lax.psum_scatter(proj_term, "y", scatter_dimension=0, tiled=True)
 
     grad_out, qg = local_call(
@@ -231,10 +241,10 @@
         square + 2 * tok * cols * width * n_blocks,
         2 * n_blocks * cols * width,
         grid=(n_blocks,),
-        in_specs=[cot_spec, by_block, whole],
+        in_specs=[cot_spec, cot_spec, by_block, whole],
         out_specs=[whole, state],
         scratch_shapes=[pltpu.VMEM((tok, width), F32)],
-    )(cot_blocks, weight_full, queries)
+    )(cot_top, cot_low, in_hbm(weight_full), queries)
     qg_got = exchange(qg.reshape(nz, share, width), "z")
     qg_part, qg_total = local_call(
         back_scan_kernel,

time: 175 us -> 169 us (0.966)
  waiting for transfers between devices: 55.8 us -> 34 us
  blocking collectives: 57.1 us -> 75.5 us
  Pallas kernels: 10.9 us -> 17.6 us
  starting transfers between devices: 26 us -> 21.3 us
  local copies, waits for them, and re-layouts: 7.28 us -> 2.9 us
    all_to_all x5 -> x4, waiting for transfers between devices: 36.3 us -> 13.5 us  [exchange(): return lax.all_to_all(x, axis, 0, 0, tiled=True)]
    all_gather x1 -> x3, blocking collectives: 2.21 us -> 17.3 us  [the longest x1 13 us: per_device(): cot_x = lax.all_gather(cot_own, 'x')]
    all_to_all x5 -> x4, starting transfers between devices: 26 us -> 21.3 us  [exchange(): return lax.all_to_all(x, axis, 0, 0, tiled=True)]
    unnamed x16 -> x12, local copies, waits for them, and re-layouts: 6.22 us -> 2.86 us
    all_to_all x3, blocking collectives: 54.8 us -> 58.2 us  [exchange(): return lax.all_to_all(x, axis, 0, 0, tiled=True)]
    pallas_call x1, Pallas kernels: 2.49 us -> 5.69 us  [per_device(): local_call(grad_out_kernel, (shape((tok, width), BF16), shape((DH, width)...]
    pallas_call x1, Pallas kernels: 2.24 us -> 4.68 us  [per_device(): local_call(functools.partial(proj_kernel, scale), pltpu.HBM((n_blocks * c...]
  transfers between devices with their start and end apart: 7 -> 6, of which waited for: 5 -> 3; matrix products, arithmetic and copies ran while one was open for 2% -> 1% of each run, Pallas kernels for 6% -> 9%
where the time goes in v3:
time: 169 us; the launch traced here: 168 us
  blocking collectives  75.5 us (45%)
  waiting for transfers between devices  34 us (20%)
  starting transfers between devices  21.3 us (13%)
  Pallas kernels  17.6 us (10%)
  between operations  14.1 us (8%)
  local copies, waits for them, and re-layouts  2.9 us (2%)
  other arithmetic  2.44 us (1%)
    all_to_all x3, blocking collectives, exchange(): return lax.all_to_all(x, axis, 0, 0, tiled=True)  58.2 us
    all_to_all x4, starting transfers between devices, exchange(): return lax.all_to_all(x, axis, 0, 0, tiled=True)  21.3 us
    reduce_scatter x1, waiting for transfers between devices, per_device(): proj_y = lax.psum_scatter(proj_term, 'y', scatter_dimension=0, tiled=True)  20.4 us
    all_to_all x4, waiting for transfers between devices, exchange(): return lax.all_to_all(x, axis, 0, 0, tiled=True)  13.5 us
    all_gather x1, blocking collectives, per_device(): cot_x = lax.all_gather(cot_own, 'x')  13 us
    pallas_call x1, Pallas kernels, per_device(): local_call(grad_out_kernel, (shape((tok, width), BF16), shape((DH, width)...  5.69 us
    pallas_call x1, Pallas kernels, per_device(): local_call(functools.partial(proj_kernel, scale), pltpu.HBM((n_blocks * c...  4.68 us
  transfers between devices with their start and end apart: 6, of which 3 were waited for; matrix products, arithmetic and copies ran while one was open for 1% of the time, Pallas kernels for 9%

profile of v3, /device:TPU:6, one launch (start us, length us, event | category | flops | bytes accessed | tf_op | source)
XLA Modules:
  0.0 167.9 jit_solution(3937815287567128072)
XLA Ops:
  7.2 0.0 copy-start.1
  7.2 0.0 all-gather.5.cloned.1.call-start
  7.2 1.3 shard_map.84
  8.6 24.8 %all_to_all.35.got_ref = bf16[8,48,512]{2,1,0:T(8,128)(2,1)S(1)} all-to-all(bf16[8,48,512]{2,1,0:T(8,128)(2,1)S(1)} %shard_map.84), channel_id=1, replica_groups=mesh['y'=8,'z'=8,'x'=4,'c'=2] {'z'}, dimensions={0} | all-to-all | bytes 786432 | tf_op jit(solution)/shard_map/all_to_all | solution.py:42
  33.4 0.8 shard_map.85
  34.2 0.0 all-gather.5.cloned.1.call-update
  34.2 7.1 %all-to-all-start.1 = ((f32[8,16,512]{2,1,0:T(8,128)}), f32[8,16,512]{2,1,0:T(8,128)S(1)}, u32[]{:S(2)}, u32[]{:S(2)}) async-start(f32[8,16,512]{2,1,0:T(8,128)} %get-tuple-element.25), calls=%async_computation.1 | async-start | bytes 524288 | tf_op jit(solution)/shard_map/all_to_all | solution.py:42
  41.3 0.0 copy-start
  41.3 0.9 copy-done
  42.3 0.0 copy-start.2
  42.3 0.9 copy-done.2
  43.2 0.0 copy-start.4
  43.2 0.9 copy-done.4
  44.2 0.7 shard_map.87
  44.8 13.0 %all-gather = bf16[1024,256]{1,0:T(8,128)(2,1)S(1)} all-gather(bf16[256,256]{1,0:T(8,128)(2,1)} %param.8), channel_id=2, replica_groups=mesh['y'=8,'z'=8,'x'=4,'c'=2] {'x'}, dimensions={0}, use_global_device_ids=true | all-gather | bytes 655360 | tf_op jit(solution)/shard_map/all_gather | solution.py:204
  57.9 0.0 all-to-all-done.1.totals_ref
  57.9 0.7 shard_map.88
  58.6 3.4 %all-to-all-start.2 = ((bf16[8,16,512]{2,1,0:T(8,128)(2,1)}), bf16[8,16,512]{2,1,0:T(8,128)(2,1)S(1)}, u32[]{:S(2)}, u32[]{:S(2)}) async-start(bf16[8,16,512]{2,1,0:T(8,128)(2,1)} %shard_map.88), calls=%async_computation.2 | async-start | bytes 262144 | tf_op jit(solution)/shard_map/all_to_all | solution.py:42
  62.0 0.0 reduce-scatter.2.cloned.1.call-start
  62.0 2.2 %all-gather.2.low_ref = bf16[8,128,256]{2,1,0:T(8,128)(2,1)S(1)} all-gather(bf16[4,128,256]{2,1,0:T(8,128)(2,1)S(1)} %get-tuple-element.36), channel_id=4, replica_groups=mesh['y'=8,'z'=8,'x'=4,'c'=2] {'c'}, dimensions={0}, use_global_device_ids=true | all-gather | bytes 786432 | tf_op jit(solution)/shard_map/all_gather | solution.py:207
  64.2 2.2 %all-gather.1.top_ref = bf16[8,128,256]{2,1,0:T(8,128)(2,1)S(1)} all-gather(bf16[4,128,256]{2,1,0:T(8,128)(2,1)S(1)} %get-tuple-element.37), channel_id=3, replica_groups=mesh['y'=8,'z'=8,'x'=4,'c'=2] {'c'}, dimensions={0}, use_global_device_ids=true | all-gather | bytes 786432 | tf_op jit(solution)/shard_map/all_gather | solution.py:206
  66.4 4.6 %all-to-all-done.2 = bf16[8,16,512]{2,1,0:T(8,128)(2,1)S(1)} async-done(((bf16[8,16,512]{2,1,0:T(8,128)(2,1)}), bf16[8,16,512]{2,1,0:T(8,128)(2,1)S(1)}, u32[]{:S(2)}, u32[]{:S(2)}) %all-to-all-start.2) | async-done | bytes 131104 | tf_op jit(solution)/shard_map/all_to_all | solution.py:42
  71.0 0.0 copy-done.1
  71.0 4.7 %shard_map.93 = f32[2048,512]{1,0:T(8,128)} custom-call(bf16[256,512]{1,0:T(8,128)(2,1)S(1)} %copy-done.1, bf16[128,512]{1,0:T(8,128)(2,1)S(1)} %bitcast.9, f32[256,512]{1,0:T(8,128)S(1)} %get-tuple-element.35.inner_ref, bf16[8,128,256]{2,1,0:T(8,128)(2,1)S(1)} %all-gather.1.top_ref, bf16[8,128,256]{2,1,0:T(8,128)(2,1)S(1)} %all-gather.2.low_ref), custom_call_target="tpu_custom_call" | custom-call | flops 570425344 | bytes 4194304 | tf_op jit(solution)/shard_map/pallas_call | solution.py:226
  75.6 0.0 reduce-scatter.2.cloned.1.call-update
  75.7 0.0 copy-start.3
  75.7 0.0 copy-start.5
  75.7 0.0 all-gather.5.cloned.1.call-done.w_ref
  75.7 5.7 %shard_map.86 = (bf16[256,512]{1,0:T(8,128)(2,1)S(1)}, bf16[128,512]{1,0:T(8,128)(2,1)S(1)}) custom-call(bf16[8,128,256]{2,1,0:T(8,128)(2,1)S(1)} %all-gather.1.top_ref, bf16[8,128,256]{2,1,0:T(8,128)(2,1)S(1)} %all-gather.2.low_ref, bf16[2048,512]{1,0:T(8,128)(2,1)} %all-gather.5.cloned.1.call-done.w_ref, bf16[256,512]{1,0:T(8,128)(2,1)S(1)} %copy-done.1), custom_call_target="tpu_custom_call" | custom-call | flops 570425344 | bytes 2097152 | tf_op jit(solution)/shard_map/pallas_call | solution.py:238
  81.4 14.4 %all_to_all.36.got_ref = bf16[8,16,512]{2,1,0:T(8,128)(2,1)S(1)} all-to-all(bf16[8,16,512]{2,1,0:T(8,128)(2,1)S(1)} %bitcast.12), channel_id=1, replica_groups=mesh['y'=8,'z'=8,'x'=4,'c'=2] {'z'}, dimensions={0} | all-to-all | bytes 262144 | tf_op jit(solution)/shard_map/all_to_all | solution.py:42
  95.9 18.9 %all_to_all.37.totals_ref = f32[8,16,512]{2,1,0:T(8,128)S(1)} all-to-all(f32[8,16,512]{2,1,0:T(8,128)S(1)} %get-tuple-element.29), channel_id=1, replica_groups=mesh['y'=8,'z'=8,'x'=4,'c'=2] {'y'}, dimensions={0} | all-to-all | bytes 524288 | tf_op jit(solution)/shard_map/all_to_all | solution.py:42
  114.8 0.7 shard_map.91
  115.5 3.4 %all-to-all-start.5 = ((bf16[8,16,512]{2,1,0:T(8,128)(2,1)}), bf16[8,16,512]{2,1,0:T(8,128)(2,1)S(1)}, u32[]{:S(2)}, u32[]{:S(2)}) async-start(bf16[8,16,512]{2,1,0:T(8,128)(2,1)} %shard_map.91), calls=%async_computation.5 | async-start | bytes 262144 | tf_op jit(solution)/shard_map/all_to_all | solution.py:42
  118.9 20.4 %reduce-scatter.2.cloned.1.call-done = f32[256,512]{1,0:T(8,128)} async-done(((f32[2048,512]{1,0:T(8,128)}), f32[256,512]{1,0:T(8,128)}) %reduce-scatter.2.cloned.1.call-update) | async-done | bytes 524304 | tf_op jit(solution)/shard_map/reduce_scatter | solution.py:236
  139.3 1.8 %convert_element_type.6 = bf16[256,512]{1,0:T(8,128)(2,1)} convert(f32[256,512]{1,0:T(8,128)} %reduce-scatter.2.cloned.1.call-done) | non-fusion elementwise | flops 131072 | bytes 786432 | tf_op jit(solution)/shard_map/convert_element_type | solution.py:270
  141.1 0.0 all-to-all-done.5
  141.1 7.4 %all-to-all-start.6 = ((bf16[8,32,512]{2,1,0:T(8,128)(2,1)}), bf16[8,32,512]{2,1,0:T(8,128)(2,1)S(1)}, u32[]{:S(2)}, u32[]{:S(2)}) async-start(bf16[8,32,512]{2,1,0:T(8,128)(2,1)} %bitcast.6), calls=%async_computation.7 | async-start | bytes 524288 | tf_op jit(solution)/shard_map/all_to_all | solution.py:42
  148.5 0.0 copy-done.3
  148.5 0.0 copy-done.5
  148.5 1.9 %shard_map.89 = (bf16[256,512]{1,0:T(8,128)(2,1)}, f32[256,512]{1,0:T(8,128)S(1)}, f32[256,512]{1,0:T(8,128)S(1)}) custom-call(bf16[256,512]{1,0:T(8,128)(2,1)S(1)} %copy-done.1, bf16[256,512]{1,0:T(8,128)(2,1)S(1)} %copy-done.3, bf16[256,512]{1,0:T(8,128)(2,1)S(1)} %copy-done.5, bf16[256,512]{1,0:T(8,128)(2,1)S(1)} %get-tuple-element.23.g_ref, ...), custom_call_target="tpu_custom_call" | custom-call | flops 301989888 | bytes 2097152 | tf_op jit(solution)/shard_map/pallas_call | solution.py:255
  150.4 1.1 shard_map.92
  151.5 8.9 %all-to-all-done.6 = bf16[8,32,512]{2,1,0:T(8,128)(2,1)S(1)} async-done(((bf16[8,32,512]{2,1,0:T(8,128)(2,1)}), bf16[8,32,512]{2,1,0:T(8,128)(2,1)S(1)}, u32[]{:S(2)}, u32[]{:S(2)}) %all-to-all-start.6) | async-done | bytes 262176 | tf_op jit(solution)/shard_map/all_to_all | solution.py:42
  160.4 0.6 multiply_bitcast_fusion
  (3 shorter events, 0.1 us)
Async XLA Ops:
  7.2 63.8 %copy-start.1 = (bf16[256,512]{1,0:T(8,128)(2,1)S(1)}, bf16[256,512]{1,0:T(8,128)(2,1)}, u32[]{:S(2)}) copy-start(bf16[256,512]{1,0:T(8,128)(2,1)} %q_ref.7) | copy-start | bytes 786436
  7.2 68.5 %all-gather.5.cloned.1.call-start = ((), (), s32[]{:S(2)}) async-start(), calls=%async_computation.8 | async-start | bytes 2359296 | tf_op jit(solution)/shard_map/all_gather | solution.py:202
  34.2 23.7 %all-to-all-start.1 = ((f32[8,16,512]{2,1,0:T(8,128)}), f32[8,16,512]{2,1,0:T(8,128)S(1)}, u32[]{:S(2)}, u32[]{:S(2)}) async-start(f32[8,16,512]{2,1,0:T(8,128)} %get-tuple-element.25), calls=%async_computation.1 | async-start | bytes 524288 | tf_op jit(solution)/shard_map/all_to_all | solution.py:42
  41.3 0.9 copy-start
  42.3 0.9 copy-start.2
  43.2 0.9 copy-start.4
  58.6 12.4 %all-to-all-start.2 = ((bf16[8,16,512]{2,1,0:T(8,128)(2,1)}), bf16[8,16,512]{2,1,0:T(8,128)(2,1)S(1)}, u32[]{:S(2)}, u32[]{:S(2)}) async-start(bf16[8,16,512]{2,1,0:T(8,128)(2,1)} %shard_map.88), calls=%async_computation.2 | async-start | bytes 262144 | tf_op jit(solution)/shard_map/all_to_all | solution.py:42
  62.0 77.3 %reduce-scatter.2.cloned.1.call-start = ((), (), s32[]{:S(2)}) async-start(), calls=%async_computation.9 | async-start | bytes 4718592 | tf_op jit(solution)/shard_map/reduce_scatter | solution.py:236
  75.7 72.8 %copy-start.3 = (bf16[256,512]{1,0:T(8,128)(2,1)S(1)}, bf16[256,512]{1,0:T(8,128)(2,1)}, u32[]{:S(2)}) copy-start(bf16[256,512]{1,0:T(8,128)(2,1)} %k_ref.7) | copy-start | bytes 786436
  75.7 72.8 %copy-start.5 = (bf16[256,512]{1,0:T(8,128)(2,1)S(1)}, bf16[256,512]{1,0:T(8,128)(2,1)}, u32[]{:S(2)}) copy-start(bf16[256,512]{1,0:T(8,128)(2,1)} %v_ref.7) | copy-start | bytes 786436
  115.5 25.6 %all-to-all-start.5 = ((bf16[8,16,512]{2,1,0:T(8,128)(2,1)}), bf16[8,16,512]{2,1,0:T(8,128)(2,1)S(1)}, u32[]{:S(2)}, u32[]{:S(2)}) async-start(bf16[8,16,512]{2,1,0:T(8,128)(2,1)} %shard_map.91), calls=%async_computation.5 | async-start | bytes 262144 | tf_op jit(solution)/shard_map/all_to_all | solution.py:42
  141.1 19.3 %all-to-all-start.6 = ((bf16[8,32,512]{2,1,0:T(8,128)(2,1)}), bf16[8,32,512]{2,1,0:T(8,128)(2,1)S(1)}, u32[]{:S(2)}, u32[]{:S(2)}) async-start(bf16[8,32,512]{2,1,0:T(8,128)(2,1)} %bitcast.6), calls=%async_computation.7 | async-start | bytes 524288 | tf_op jit(solution)/shard_map/all_to_all | solution.py:42
Sparse Core Ops, SparseCore 0:
  34.3 40.7 all-gather.4
  77.9 61.3 reduce-scatter.1

commit v4 on v3

--- a/solution.py
+++ b/solution.py
@@ -45,11 +45,14 @@
 def first_kernel(k_ref, v_ref, w_ref, out_ref):
     peers, rows, width = out_ref.shape
     own = w_ref.shape[0]
-    share = rows - own
+    share = (rows - own) // 2
     for h in range(width // DH):
-        kv = mm(k_ref[:, head(h)], v_ref[:, head(h)], 0, 0).astype(BF16)
+        kv = mm(k_ref[:, head(h)], v_ref[:, head(h)], 0, 0)
+        high = kv.astype(BF16)
+        low = (kv - high.astype(F32)).astype(BF16)
         for p in range(peers):
-            out_ref[p, own:, head(h)] = kv[p * share : (p + 1) * share]
+            out_ref[p, own : own + share, head(h)] = high[p * share : (p + 1) * share]
+            out_ref[p, own + share :, head(h)] = low[p * share : (p + 1) * share]
     for p in range(peers):
         out_ref[p, :own, :] = w_ref[...]
 
@@ -57,11 +60,13 @@
 def split_kernel(got_ref, weight_ref, part_ref, total_ref):
     peers, rows, width = got_ref.shape
     own = weight_ref.shape[0] // peers
-    running = jnp.zeros((rows - own, width), F32)
+    share = (rows - own) // 2
+    running = jnp.zeros((share, width), F32)
     for p in range(peers):
         weight_ref[p * own : (p + 1) * own, :] = got_ref[p, :own, :]
         part_ref[p] = running
-        running = running + got_ref[p, own:, :].astype(F32)
+        high = got_ref[p, own : own + share, :].astype(F32)
+        running = running + (high + got_ref[p, own + share :, :].astype(F32))
     for p in range(total_ref.shape[0]):
         total_ref[p] = running
 
@@ -71,7 +76,7 @@
     running = jnp.zeros((rows, width), F32)
     for p in reversed(range(peers)):
         part_ref[p] = running
-        running = running + got_ref[p].astype(F32)
+        running = running + got_ref[p]
     for p in range(total_ref.shape[0]):
         total_ref[p] = running
 
@@ -102,14 +107,18 @@
             far = mm(q_ref[:, head(h)], prior_ref[:, head(h)], 1, 0)
             attn_out_ref[:, head(h)] = (scale * (inner_ref[:, head(h)] + far)).astype(BF16)
 
-    cot = jnp.concatenate([top_ref[0], low_ref[0]], axis=0)
-    out_ref[...] = mm(cot, attn_out_ref[...], 0, 0)
+    for x in range(out_ref.shape[0]):
+        cot = jnp.concatenate([top_ref[0, x], low_ref[0, x]], axis=0)
+        out_ref[x, 0] = mm(cot, attn_out_ref[...], 0, 0).astype(BF16)
 
 
 def grad_out_kernel(top_ref, low_ref, w_ref, q_ref, g_ref, qg_ref, acc_ref):
     step = pl.program_id(0)
-    cot = jnp.concatenate([top_ref[0], low_ref[0]], axis=0)
-    term = mm(cot, w_ref[...], 1, 0)
+    term = None
+    for x in range(w_ref.shape[0]):
+        cot = jnp.concatenate([top_ref[0, x], low_ref[0, x]], axis=0)
+        one = mm(cot, w_ref[x, 0], 1, 0)
+        term = one if term is None else term + one
 
     @pl.when(step == 0)
     def _():
@@ -124,7 +133,7 @@
         g = acc_ref[...].astype(BF16)
         g_ref[...] = g
         for h in range(g.shape[1] // DH):
-            qg_ref[:, head(h)] = mm(q_ref[:, head(h)], g[:, head(h)], 0, 0).astype(BF16)
+            qg_ref[:, head(h)] = mm(q_ref[:, head(h)], g[:, head(h)], 0, 0)
 
 
 def inner_grads_kernel(scale, q_ref, k_ref, v_ref, g_ref, attn_ref, prior_ref, dq_ref, dk_ref, dv_ref):
@@ -186,7 +195,7 @@
     big = tok * width
 
     sent = local_call(
-        first_kernel, shape((nz, own + share, width), BF16), square, 3 * big
+        first_kernel, shape((nz, own + 2 * share, width), BF16), square, 3 * big
     )(in_hbm(keys), in_hbm(values), in_hbm(weight_t))
     got = exchange(sent, "z")
     weight_z, kv_part, kv_total = local_call(
@@ -203,8 +212,8 @@
     cot_own, kv_total = lax.optimization_barrier((out_cotangent, kv_total))
     cot_x = lax.all_gather(cot_own, "x")
     half = tok // 2
-    cot_top = lax.all_gather(cot_x[:, :half], "c").reshape(nx * nc, half, cols)
-    cot_low = lax.all_gather(cot_x[:, half:], "c").reshape(nx * nc, half, cols)
+    cot_top = lax.all_gather(cot_x[:, :half], "c")
+    cot_low = lax.all_gather(cot_x[:, half:], "c")
     attn, attn_inner = local_call(
         attn_kernel,
         (shape((heads, tok, tok), BF16), shape((tok, width), F32)),
@@ -216,35 +225,33 @@
 
     n_blocks = nx * nc
 
-    def block_of(i):
-        return (i % nx) * nc + i // nx
-
     whole = pl.BlockSpec((tok, width), lambda i: (0, 0))
     state = pl.BlockSpec((DH, width), lambda i: (0, 0))
-    cot_spec = pl.BlockSpec((1, half, cols), lambda i: (i, 0, 0))
-    by_block = pl.BlockSpec((cols, width), lambda i: (block_of(i), 0))
+    cot_spec = pl.BlockSpec((1, nx, half, cols), lambda i: (i, 0, 0, 0))
+    by_core = pl.BlockSpec((nx, 1, cols, width), lambda i: (0, i, 0, 0))
     proj_term = local_call(
         functools.partial(proj_kernel, scale),
-        pltpu.HBM((n_blocks * cols, width), F32),
+        pltpu.HBM((nx, nc, cols, width), BF16),
         square + 2 * tok * cols * width * n_blocks,
-        4 * n_blocks * cols * width,
-        grid=(n_blocks,),
+        2 * n_blocks * cols * width,
+        grid=(nc,),
         in_specs=[whole, state, whole, cot_spec, cot_spec],
-        out_specs=by_block,
+        out_specs=by_core,
         scratch_shapes=[pltpu.VMEM((tok, width), BF16)],
     )(queries, prior, attn_inner, cot_top, cot_low)
+    proj_term = proj_term.reshape(n_blocks * cols, width)
     proj_y = lax.psum_scatter(proj_term, "y", scatter_dimension=0, tiled=True)
 
     grad_out, qg = local_call(
         grad_out_kernel,
-        (shape((tok, width), BF16), shape((DH, width), BF16)),
+        (shape((tok, width), BF16), shape((DH, width), F32)),
         square + 2 * tok * cols * width * n_blocks,
         2 * n_blocks * cols * width,
-        grid=(n_blocks,),
-        in_specs=[cot_spec, cot_spec, by_block, whole],
+        grid=(nc,),
+        in_specs=[cot_spec, cot_spec, by_core, whole],
         out_specs=[whole, state],
         scratch_shapes=[pltpu.VMEM((tok, width), F32)],
-    )(cot_top, cot_low, in_hbm(weight_full), queries)
+    )(cot_top, cot_low, in_hbm(weight_full.reshape(nx, nc, cols, width)), queries)
     qg_got = exchange(qg.reshape(nz, share, width), "z")
     qg_part, qg_total = local_call(
         back_scan_kernel,
@@ -267,7 +274,7 @@
         12 * big,
     )(keys, values, later, near_k, near_v)
 
-    proj_parts = exchange(proj_y.astype(BF16).reshape(nz, own, width), "z")
+    proj_parts = exchange(proj_y.reshape(nz, own, width), "z")
     proj_sum = jnp.sum(proj_parts.astype(F32), axis=0)
     grad_proj = (proj_sum / jnp.sqrt(F32(tok * ny * nz))).T
     return grad_q, grad_k, grad_v, grad_proj

time: 169 us -> 152 us (0.90)
  waiting for transfers between devices: 34 us -> 18.5 us
  blocking collectives: 75.5 us -> 89.8 us
  Pallas kernels: 17.6 us -> 11.2 us
  starting transfers between devices: 21.3 us -> 17 us
  local copies, waits for them, and re-layouts: 2.9 us -> 0.05 us
  other arithmetic: 2.44 us -> 0.67 us
    reduce_scatter x1, waiting for transfers between devices: 20.4 us -> 0.99 us  [per_device(): proj_y = lax.psum_scatter(proj_term, 'y', scatter_dimension=0, tiled=True)]
    all_to_all x3 -> x4, blocking collectives: 58.2 us -> 72.7 us  [exchange(): return lax.all_to_all(x, axis, 0, 0, tiled=True)]
    all_gather x1, waiting for transfers between devices: 0.02 us -> 5.41 us  [per_device(): weight_full = lax.all_gather(weight_z, 'y', axis=0, tiled=True)]
    all_to_all x4 -> x3, starting transfers between devices: 21.3 us -> 16.9 us  [exchange(): return lax.all_to_all(x, axis, 0, 0, tiled=True)]
    pallas_call x1, Pallas kernels: 5.69 us -> 2.47 us  [per_device(): local_call(grad_out_kernel, (shape((tok, width), BF16), shape((DH, width)...]
    unnamed x12 -> x8, local copies, waits for them, and re-layouts: 2.86 us -> 0.02 us
    pallas_call x2, Pallas kernels: 6.01 us -> 3.52 us  [the longest x1 2.15 us: per_device(): local_call(functools.partial(proj_kernel, scale), pltpu.HBM((nx, nc, cols...]
    convert_element_type x1 -> x0, other arithmetic: 1.77 us -> none  [per_device(): proj_parts = exchange(proj_y.astype(BF16).reshape(nz, own, width), 'z')]
  transfers between devices with their start and end apart: 6 -> 5, of which waited for: 3 -> 4; matrix products, arithmetic and copies ran while one was open for 1% -> 0% of each run, Pallas kernels for 9% -> 6%
where the time goes in v4:
time: 152 us; the launch traced here: 151 us
  blocking collectives  89.8 us (59%)
  waiting for transfers between devices  18.5 us (12%)
  starting transfers between devices  17 us (11%)
  between operations  14.2 us (9%)
  Pallas kernels  11.2 us (7%)
    all_to_all x4, blocking collectives, exchange(): return lax.all_to_all(x, axis, 0, 0, tiled=True)  72.7 us
    all_to_all x3, starting transfers between devices, exchange(): return lax.all_to_all(x, axis, 0, 0, tiled=True)  16.9 us
    all_gather x1, blocking collectives, per_device(): cot_x = lax.all_gather(cot_own, 'x')  12.8 us
    all_to_all x3, waiting for transfers between devices, exchange(): return lax.all_to_all(x, axis, 0, 0, tiled=True)  12.1 us
    all_gather x1, waiting for transfers between devices, per_device(): weight_full = lax.all_gather(weight_z, 'y', axis=0, tiled=True)  5.41 us
  transfers between devices with their start and end apart: 5, of which 4 were waited for; matrix products, arithmetic and copies ran while one was open for 0% of the time, Pallas kernels for 6%

profile of v4, /device:TPU:6, one launch (start us, length us, event | category | flops | bytes accessed | tf_op | source)
XLA Modules:
  0.0 151.4 jit_solution(7102046575370216326)
XLA Ops:
  7.2 0.0 copy-start.1
  7.2 0.0 copy-start.2
  7.2 0.0 copy-start
  7.2 0.0 all-gather.5.cloned.1.call-start
  7.2 0.0 copy-start.3
  7.3 1.4 shard_map.84
  8.6 27.6 %all_to_all.35.got_ref = bf16[8,64,512]{2,1,0:T(8,128)(2,1)S(1)} all-to-all(bf16[8,64,512]{2,1,0:T(8,128)(2,1)S(1)} %shard_map.84), channel_id=1, replica_groups=mesh['y'=8,'z'=8,'x'=4,'c'=2] {'z'}, dimensions={0} | all-to-all | bytes 1048576 | tf_op jit(solution)/shard_map/all_to_all | solution.py:42
  36.2 0.8 shard_map.85
  37.1 0.0 all-gather.5.cloned.1.call-update
  37.1 7.1 %all-to-all-start.1 = ((f32[8,16,512]{2,1,0:T(8,128)}), f32[8,16,512]{2,1,0:T(8,128)S(1)}, u32[]{:S(2)}, u32[]{:S(2)}) async-start(f32[8,16,512]{2,1,0:T(8,128)} %get-tuple-element.25), calls=%async_computation.1 | async-start | bytes 524288 | tf_op jit(solution)/shard_map/all_to_all | solution.py:42
  44.2 0.0 copy-done.1
  44.2 0.0 copy-done.2
  44.2 0.0 copy-done
  44.2 0.7 shard_map.87
  44.9 0.0 copy-done.3
  44.9 12.8 %all-gather = bf16[1024,256]{1,0:T(8,128)(2,1)S(1)} all-gather(bf16[256,256]{1,0:T(8,128)(2,1)S(1)} %copy-done.3), channel_id=2, replica_groups=mesh['y'=8,'z'=8,'x'=4,'c'=2] {'x'}, dimensions={0}, use_global_device_ids=true | all-gather | bytes 655360 | tf_op jit(solution)/shard_map/all_gather | solution.py:213
  57.7 0.0 all-to-all-done.1.totals_ref
  57.7 0.7 shard_map.88
  58.4 3.4 %all-to-all-start.2 = ((bf16[8,16,512]{2,1,0:T(8,128)(2,1)}), bf16[8,16,512]{2,1,0:T(8,128)(2,1)S(1)}, u32[]{:S(2)}, u32[]{:S(2)}) async-start(bf16[8,16,512]{2,1,0:T(8,128)(2,1)} %shard_map.88), calls=%async_computation.2 | async-start | bytes 262144 | tf_op jit(solution)/shard_map/all_to_all | solution.py:42
  61.8 0.0 reduce-scatter.2.cloned.1.call-start
  61.9 2.2 %all-gather.1 = bf16[8,128,256]{2,1,0:T(8,128)(2,1)S(1)} all-gather(bf16[4,128,256]{2,1,0:T(8,128)(2,1)S(1)} %get-tuple-element.37), channel_id=3, replica_groups=mesh['y'=8,'z'=8,'x'=4,'c'=2] {'c'}, dimensions={0}, use_global_device_ids=true | all-gather | bytes 786432 | tf_op jit(solution)/shard_map/all_gather | solution.py:215
  64.0 2.2 %all-gather.2 = bf16[8,128,256]{2,1,0:T(8,128)(2,1)S(1)} all-gather(bf16[4,128,256]{2,1,0:T(8,128)(2,1)S(1)} %get-tuple-element.36), channel_id=4, replica_groups=mesh['y'=8,'z'=8,'x'=4,'c'=2] {'c'}, dimensions={0}, use_global_device_ids=true | all-gather | bytes 786432 | tf_op jit(solution)/shard_map/all_gather | solution.py:216
  66.2 4.6 %all-to-all-done.2 = bf16[8,16,512]{2,1,0:T(8,128)(2,1)S(1)} async-done(((bf16[8,16,512]{2,1,0:T(8,128)(2,1)}), bf16[8,16,512]{2,1,0:T(8,128)(2,1)S(1)}, u32[]{:S(2)}, u32[]{:S(2)}) %all-to-all-start.2) | async-done | bytes 131104 | tf_op jit(solution)/shard_map/all_to_all | solution.py:42
  70.8 2.1 %shard_map.93 = bf16[4,2,256,512]{3,2,1,0:T(8,128)(2,1)} custom-call(bf16[256,512]{1,0:T(8,128)(2,1)S(1)} %copy-done, bf16[128,512]{1,0:T(8,128)(2,1)S(1)} %bitcast.17, f32[256,512]{1,0:T(8,128)S(1)} %get-tuple-element.35.inner_ref, bf16[2,4,128,256]{3,2,1,0:T(8,128)(2,1)S(1)} %bitcast.13, bf16[2,4,128,256]{3,2,1,0:T(8,128)(2,1)S(1)} %bitcast.15), custom_call_target="tpu_custom_call" | custom-call | flops 570425344 | bytes 2097152 | tf_op jit(solution)/shard_map/pallas_call | solution.py:232
  73.0 0.0 reduce-scatter.2.cloned.1.call-update
  73.0 5.4 %all-gather.5.cloned.1.call-done = bf16[2048,512]{1,0:T(8,128)(2,1)} async-done(((bf16[256,512]{1,0:T(8,128)(2,1)}), bf16[2048,512]{1,0:T(8,128)(2,1)}) %all-gather.5.cloned.1.call-update) | async-done | bytes 2097168 | tf_op jit(solution)/shard_map/all_gather | solution.py:211
  78.4 2.5 %shard_map.86 = (bf16[256,512]{1,0:T(8,128)(2,1)S(1)}, f32[128,512]{1,0:T(8,128)S(1)}) custom-call(bf16[2,4,128,256]{3,2,1,0:T(8,128)(2,1)S(1)} %bitcast.14, bf16[2,4,128,256]{3,2,1,0:T(8,128)(2,1)S(1)} %bitcast.16, bf16[4,2,256,512]{3,2,1,0:T(8,128)(2,1)} %bitcast.23, bf16[256,512]{1,0:T(8,128)(2,1)S(1)} %copy-done), custom_call_target="tpu_custom_call" | custom-call | flops 570425344 | bytes 2097152 | tf_op jit(solution)/shard_map/pallas_call | solution.py:245
  80.9 16.4 %all_to_all.36.got_ref = f32[8,16,512]{2,1,0:T(8,128)S(1)} all-to-all(f32[8,16,512]{2,1,0:T(8,128)S(1)} %bitcast.20), channel_id=1, replica_groups=mesh['y'=8,'z'=8,'x'=4,'c'=2] {'z'}, dimensions={0} | all-to-all | bytes 524288 | tf_op jit(solution)/shard_map/all_to_all | solution.py:42
  97.3 17.2 %all_to_all.37.totals_ref = f32[8,16,512]{2,1,0:T(8,128)S(1)} all-to-all(f32[8,16,512]{2,1,0:T(8,128)S(1)} %get-tuple-element.29), channel_id=1, replica_groups=mesh['y'=8,'z'=8,'x'=4,'c'=2] {'y'}, dimensions={0} | all-to-all | bytes 524288 | tf_op jit(solution)/shard_map/all_to_all | solution.py:42
  114.5 11.5 %all_to_all.38 = bf16[8,16,512]{2,1,0:T(8,128)(2,1)S(1)} all-to-all(bf16[8,16,512]{2,1,0:T(8,128)(2,1)S(1)} %shard_map.91), channel_id=1, replica_groups=mesh['y'=8,'z'=8,'x'=4,'c'=2] {'z'}, dimensions={0} | all-to-all | bytes 262144 | tf_op jit(solution)/shard_map/all_to_all | solution.py:42
  126.0 1.0 reduce-scatter.2.cloned.1.call-done
  127.0 6.4 %all-to-all-start.6 = ((bf16[8,32,512]{2,1,0:T(8,128)(2,1)}), bf16[8,32,512]{2,1,0:T(8,128)(2,1)S(1)}, u32[]{:S(2)}, u32[]{:S(2)}) async-start(bf16[8,32,512]{2,1,0:T(8,128)(2,1)} %bitcast.24), calls=%async_computation.7 | async-start | bytes 524288 | tf_op jit(solution)/shard_map/all_to_all | solution.py:42
  133.4 1.9 %shard_map.89 = (bf16[256,512]{1,0:T(8,128)(2,1)}, f32[256,512]{1,0:T(8,128)S(1)}, f32[256,512]{1,0:T(8,128)S(1)}) custom-call(bf16[256,512]{1,0:T(8,128)(2,1)S(1)} %copy-done, bf16[256,512]{1,0:T(8,128)(2,1)S(1)} %copy-done.1, bf16[256,512]{1,0:T(8,128)(2,1)S(1)} %copy-done.2, bf16[256,512]{1,0:T(8,128)(2,1)S(1)} %get-tuple-element.23.g_ref, ...), custom_call_target="tpu_custom_call" | custom-call | flops 301989888 | bytes 2097152 | tf_op jit(solution)/shard_map/pallas_call | solution.py:262
  135.3 1.1 shard_map.92
  136.4 7.5 %all-to-all-done.6 = bf16[8,32,512]{2,1,0:T(8,128)(2,1)S(1)} async-done(((bf16[8,32,512]{2,1,0:T(8,128)(2,1)}), bf16[8,32,512]{2,1,0:T(8,128)(2,1)S(1)}, u32[]{:S(2)}, u32[]{:S(2)}) %all-to-all-start.6) | async-done | bytes 262176 | tf_op jit(solution)/shard_map/all_to_all | solution.py:42
  143.9 0.6 multiply_bitcast_fusion
  (4 shorter events, 0.1 us)
Async XLA Ops:
  7.2 37.0 %copy-start.1 = (bf16[256,512]{1,0:T(8,128)(2,1)S(1)}, bf16[256,512]{1,0:T(8,128)(2,1)}, u32[]{:S(2)}) copy-start(bf16[256,512]{1,0:T(8,128)(2,1)} %k_ref.7) | copy-start | bytes 786436
  7.2 37.0 %copy-start.2 = (bf16[256,512]{1,0:T(8,128)(2,1)S(1)}, bf16[256,512]{1,0:T(8,128)(2,1)}, u32[]{:S(2)}) copy-start(bf16[256,512]{1,0:T(8,128)(2,1)} %v_ref.7) | copy-start | bytes 786436
  7.2 37.0 %copy-start = (bf16[256,512]{1,0:T(8,128)(2,1)S(1)}, bf16[256,512]{1,0:T(8,128)(2,1)}, u32[]{:S(2)}) copy-start(bf16[256,512]{1,0:T(8,128)(2,1)} %q_ref.7) | copy-start | bytes 786436
  7.2 71.2 %all-gather.5.cloned.1.call-start = ((), (), s32[]{:S(2)}) async-start(), calls=%async_computation.8 | async-start | bytes 2359296 | tf_op jit(solution)/shard_map/all_gather | solution.py:211
  7.2 37.6 %copy-start.3 = (bf16[256,256]{1,0:T(8,128)(2,1)S(1)}, bf16[256,256]{1,0:T(8,128)(2,1)}, u32[]{:S(2)}) copy-start(bf16[256,256]{1,0:T(8,128)(2,1)} %param.8) | copy-start | bytes 393220
  37.1 20.6 %all-to-all-start.1 = ((f32[8,16,512]{2,1,0:T(8,128)}), f32[8,16,512]{2,1,0:T(8,128)S(1)}, u32[]{:S(2)}, u32[]{:S(2)}) async-start(f32[8,16,512]{2,1,0:T(8,128)} %get-tuple-element.25), calls=%async_computation.1 | async-start | bytes 524288 | tf_op jit(solution)/shard_map/all_to_all | solution.py:42
  58.4 12.4 %all-to-all-start.2 = ((bf16[8,16,512]{2,1,0:T(8,128)(2,1)}), bf16[8,16,512]{2,1,0:T(8,128)(2,1)S(1)}, u32[]{:S(2)}, u32[]{:S(2)}) async-start(bf16[8,16,512]{2,1,0:T(8,128)(2,1)} %shard_map.88), calls=%async_computation.2 | async-start | bytes 262144 | tf_op jit(solution)/shard_map/all_to_all | solution.py:42
  61.8 65.2 %reduce-scatter.2.cloned.1.call-start = ((), (), s32[]{:S(2)}) async-start(), calls=%async_computation.9 | async-start | bytes 2359296 | tf_op jit(solution)/shard_map/reduce_scatter | solution.py:243
  127.0 16.9 %all-to-all-start.6 = ((bf16[8,32,512]{2,1,0:T(8,128)(2,1)}), bf16[8,32,512]{2,1,0:T(8,128)(2,1)S(1)}, u32[]{:S(2)}, u32[]{:S(2)}) async-start(bf16[8,32,512]{2,1,0:T(8,128)(2,1)} %bitcast.24), calls=%async_computation.7 | async-start | bytes 524288 | tf_op jit(solution)/shard_map/all_to_all | solution.py:42
Sparse Core Ops, SparseCore 0:
  37.2 41.1 all-gather.4
  81.2 45.7 reduce-scatter.1

commit v5 on v2

v5 whole, which is shorter than its diff:
```python
import functools

import jax
import jax.numpy as jnp
from jax import lax
from jax.experimental import pallas as pl
from jax.experimental.pallas import tpu as pltpu
from jax.sharding import Mesh, PartitionSpec as P

DH = 128
PAIR = "zl"
Z = ("zh", PAIR)
SEQ = ("y",) + Z
TP = ("x", "c")
BF16 = jnp.bfloat16
F32 = jnp.float32
VMEM_BYTES = 48 * 1024 * 1024
IN_VMEM = pl.BlockSpec(memory_space=pltpu.VMEM)
IN_SMEM = pl.BlockSpec(memory_space=pltpu.SMEM)


def mm(a, b, ca, cb):
    return lax.dot_general(a, b, (((ca,), (cb,)), ((), ())), preferred_element_type=F32)


def head(h):
    return slice(h * DH, (h + 1) * DH)


def local_call(kernel, out_shape, flops, moved, **kwargs):
    return pl.pallas_call(
        kernel,
        out_shape=out_shape,
        cost_estimate=pl.CostEstimate(flops=flops, transcendentals=0, bytes_accessed=moved),
        compiler_params=pltpu.CompilerParams(vmem_limit_bytes=VMEM_BYTES),
        **kwargs,
    )


def causal(tok):
    rows = lax.broadcasted_iota(jnp.int32, (tok, tok), 0)
    cols = lax.broadcasted_iota(jnp.int32, (tok, tok), 1)
    return rows >= cols


def exchange(x, axis):
    return lax.all_to_all(x, axis, 0, 0, tiled=True)


def first_kernel(k_ref, v_ref, w_ref, out_ref):
    count, rows, half = out_ref.shape
    own = w_ref.shape[0]
    share = rows - own
    per_head = DH // share
    for h in range(k_ref.shape[1] // DH):
        kv = mm(k_ref[:, head(h)], v_ref[:, head(h)], 0, 0)
        high = kv.astype(BF16)
        low = (kv - high.astype(F32)).astype(BF16)
        for i in range(per_head):
            piece = slice(i * share, (i + 1) * share)
            out_ref[h * per_head + i, own:, :DH] = high[piece]
            out_ref[h * per_head + i, own:, DH:] = low[piece]
    for s in range(count):
        out_ref[s, :own, :] = w_ref[:, (s % 2) * half : (s % 2 + 1) * half]


def prior_kernel(got_ref, sums_ref):
    count, share, _ = sums_ref.shape
    own = got_ref.shape[1] - share
    running = jnp.zeros(sums_ref.shape[1:], F32)
    for s in range(count):
        sums_ref[s] = running.astype(BF16)
        high = got_ref[s, own:, :DH].astype(F32)
        running = running + (high + got_ref[s, own:, DH:].astype(F32))


def later_kernel(got_ref, sums_ref):
    running = jnp.zeros(sums_ref.shape[1:], F32)
    for s in reversed(range(sums_ref.shape[0])):
        sums_ref[s] = running.astype(BF16)
        running = running + got_ref[s].astype(F32)


def attn_kernel(q_ref, k_ref, v_ref, attn_ref, inner_ref):
    mask = causal(q_ref.shape[0])
    for h in range(q_ref.shape[1] // DH):
        scores = mm(q_ref[:, head(h)], k_ref[:, head(h)], 1, 1)
        attn = jnp.where(mask, scores, 0.0).astype(BF16)
        attn_ref[h] = attn
        inner_ref[:, head(h)] = mm(attn, v_ref[:, head(h)], 1, 0)


def half_grad_kernel(place_ref, cot_ref, got_ref, keep_ref, send_ref):
    blocks, _, cols = cot_ref.shape[1:]
    own = cols * blocks // got_ref.shape[0]
    per_block = cols // own
    total = None
    for b in range(blocks):
        weight = got_ref[b * per_block : (b + 1) * per_block, :own, :]
        term = mm(cot_ref[0, b], weight.reshape(cols, weight.shape[2]), 1, 0)
        total = term if total is None else total + term
    mine = place_ref[0] == pl.program_id(0)

    @pl.when(mine)
    def _():
        keep_ref[...] = total.astype(BF16)

    @pl.when(jnp.logical_not(mine))
    def _():
        send_ref[...] = total.astype(BF16)


def proj_kernel(scale, place_ref, q_ref, prior_ref, inner_ref, cot_ref, out_ref, attn_out_ref):
    @pl.when(pl.program_id(0) == 0)
    def _():
        for h in range(q_ref.shape[1] // DH):
            far = mm(q_ref[:, head(h)], prior_ref[head(h), :], 1, 0)
            attn_out_ref[:, head(h)] = (scale * (inner_ref[:, head(h)] + far)).astype(BF16)

    for b in range(out_ref.shape[0]):
        out_ref[b] = mm(cot_ref[0, b], attn_out_ref[...], 0, 0).astype(BF16)


def qg_kernel(place_ref, keep_ref, got_ref, q_ref, g_ref, qg_ref):
    half = keep_ref.shape[1]
    first = place_ref[0] == 0
    g_ref[:, :half] = jnp.where(first, keep_ref[...], got_ref[...])
    g_ref[:, half:] = jnp.where(first, got_ref[...], keep_ref[...])
    for h in range(q_ref.shape[1] // DH):
        qg_ref[head(h), :] = mm(q_ref[:, head(h)], g_ref[:, head(h)], 0, 0).astype(BF16)


def inner_grads_kernel(scale, q_ref, k_ref, v_ref, g_ref, attn_ref, prior_ref, dq_ref, dk_ref, dv_ref):
    mask = causal(q_ref.shape[0])
    for h in range(q_ref.shape[1] // DH):
        g = g_ref[:, head(h)]
        back = jnp.where(mask, mm(g, v_ref[:, head(h)], 1, 1), 0.0).astype(BF16)
        near = mm(back, k_ref[:, head(h)], 1, 0)
        far = mm(g, prior_ref[head(h), :], 1, 1)
        dq_ref[:, head(h)] = (scale * (near + far)).astype(BF16)
        dk_ref[:, head(h)] = mm(back, q_ref[:, head(h)], 0, 0)
        dv_ref[:, head(h)] = mm(attn_ref[h], g, 0, 0)


def outer_grads_kernel(scale, k_ref, v_ref, later_ref, near_k_ref, near_v_ref, dk_ref, dv_ref):
    for h in range(k_ref.shape[1] // DH):
        later = later_ref[head(h), :]
        far_k = mm(v_ref[:, head(h)], later, 1, 1)
        dk_ref[:, head(h)] = (scale * (near_k_ref[:, head(h)] + far_k)).astype(BF16)
        far_v = mm(k_ref[:, head(h)], later, 1, 0)
        dv_ref[:, head(h)] = (scale * (near_v_ref[:, head(h)] + far_v)).astype(BF16)


def shape(dims, dtype):
    return jax.ShapeDtypeStruct(dims, dtype)


def in_hbm(x):
    return pltpu.with_memory_space_constraint(x, pltpu.HBM)


def per_device(queries, keys, values, out_cotangent, proj_weight):
    tok, width = queries.shape
    heads = width // DH
    count, nz, ny = lax.axis_size(SEQ), lax.axis_size(Z), lax.axis_size("y")
    blocks = lax.axis_size(TP)
    cols = out_cotangent.shape[1]
    scale = (DH * tok * count) ** -0.5
    place = lax.axis_index(PAIR).reshape(1)
    weight_t = proj_weight.T
    own = weight_t.shape[0]
    half = width // 2
    share = heads * DH // count
    square = 2 * tok * DH * DH * heads
    wide = 2 * tok * tok * DH * heads
    full = 2 * tok * cols * width * blocks
    big = tok * width

    sent = local_call(
        first_kernel, shape((count, own + share, half), BF16), square, 12 * big
    )(in_hbm(keys), in_hbm(values), in_hbm(weight_t))
    cot = lax.all_gather(out_cotangent, (PAIR,) + TP).reshape(2, blocks, tok, cols)
    got = exchange(sent, SEQ)
    attn, attn_inner = local_call(
        attn_kernel,
        (shape((heads, tok, tok), BF16), shape((tok, width), F32)),
        2 * wide,
        10 * big,
    )(queries, keys, values)
    sums = local_call(prior_kernel, shape((count, share, DH), BF16), 0, 4 * big)(got)
    prior = exchange(sums, SEQ).reshape(heads * DH, DH)

    keep, send = local_call(
        half_grad_kernel,
        (shape((tok, half), BF16), shape((tok, half), BF16)),
        full,
        24 * big,
        grid=(2,),
        in_specs=[
            IN_SMEM,
            pl.BlockSpec((1, blocks, tok, cols), lambda m: (m, 0, 0, 0)),
            pl.BlockSpec(got.shape, lambda m: (0, 0, 0)),
        ],
        out_specs=[pl.BlockSpec((tok, half), lambda m: (0, 0))] * 2,
    )(place, in_hbm(cot), got)
    swapped = lax.ppermute(send, PAIR, [(0, 1), (1, 0)])

    step = blocks // 2
    whole = pl.BlockSpec((tok, width), lambda i, p: (0, 0))
    proj_term = local_call(
        functools.partial(proj_kernel, scale),
        pltpu.HBM((blocks, cols, width), BF16),
        square + full,
        24 * big,
        grid_spec=pltpu.PrefetchScalarGridSpec(
            num_scalar_prefetch=1,
            grid=(blocks // step,),
            in_specs=[
                whole,
                pl.BlockSpec((heads * DH, DH), lambda i, p: (0, 0)),
                whole,
                pl.BlockSpec((1, step, tok, cols), lambda i, p: (p[0], i, 0, 0)),
            ],
            out_specs=pl.BlockSpec((step, cols, width), lambda i, p: (i, 0, 0)),
            scratch_shapes=[pltpu.VMEM((tok, width), BF16)],
        ),
    )(place, queries, prior, attn_inner, in_hbm(cot))
    proj_y = lax.psum_scatter(
        proj_term.reshape(blocks * cols, width), "y", scatter_dimension=0, tiled=True
    )

    grad_out, qg = local_call(
        qg_kernel,
        (shape((tok, width), BF16), shape((heads * DH, DH), BF16)),
        square,
        6 * big,
        in_specs=[IN_SMEM, IN_VMEM, IN_VMEM, IN_VMEM],
    )(place, keep, swapped, queries)
    qg_got = exchange(qg.reshape(count, share, DH), SEQ)
    sums = local_call(later_kernel, shape((count, share, DH), BF16), 0, 2 * big)(qg_got)
    later = exchange(sums, SEQ).reshape(heads * DH, DH)
    grad_q, near_k, near_v = local_call(
        functools.partial(inner_grads_kernel, scale),
        (shape((tok, width), BF16), shape((tok, width), F32), shape((tok, width), F32)),
        4 * wide + square,
        16 * big,
    )(queries, keys, values, grad_out, attn, prior)
    grad_k, grad_v = local_call(
        functools.partial(outer_grads_kernel, scale),
        (shape((tok, width), BF16), shape((tok, width), BF16)),
        2 * square,
        12 * big,
    )(keys, values, later, near_k, near_v)

    proj_parts = exchange(proj_y.reshape(nz, own, width), Z)
    proj_sum = jnp.sum(proj_parts.astype(F32), axis=0)
    grad_proj = (proj_sum / jnp.sqrt(F32(tok * count))).T
    return grad_q, grad_k, grad_v, grad_proj


def solution(mesh):
    seq, tp = mesh.devices.shape
    inner, cores = 8, 2
    grid = Mesh(
        mesh.devices.reshape(seq // inner, inner // 2, 2, tp // cores, cores),
        ("y", "zh", PAIR, "x", "c"),
    )
    tokens, weight = P(SEQ, TP), P(TP, SEQ)
    return jax.shard_map(
        per_device,
        mesh=grid,
        in_specs=(tokens, tokens, tokens, tokens, weight),
        out_specs=(tokens, tokens, tokens, weight),
        check_vma=False,
    )
```

time: 175 us -> 157 us (0.90)
  blocking collectives: 57.1 us -> 89.5 us
  waiting for transfers between devices: 55.8 us -> 24.4 us
  starting transfers between devices: 26 us -> 15.3 us
  local copies, waits for them, and re-layouts: 7.28 us -> 0.02 us
  other arithmetic: 2.46 us -> 0.67 us
    all_to_all x3, blocking collectives: 54.8 us -> 89.5 us  [exchange(): return lax.all_to_all(x, axis, 0, 0, tiled=True)]
    reduce_scatter x1, waiting for transfers between devices: 19.4 us -> 0.01 us  [per_device(): lax.psum_scatter(proj_term.reshape(blocks * cols, width), 'y', scatter_di...]
    all_to_all x5 -> x2, waiting for transfers between devices: 36.3 us -> 19.4 us  [exchange(): return lax.all_to_all(x, axis, 0, 0, tiled=True)]
    all_to_all x5 -> x2, starting transfers between devices: 26 us -> 12.7 us  [exchange(): return lax.all_to_all(x, axis, 0, 0, tiled=True)]
    unnamed x16 -> x6, local copies, waits for them, and re-layouts: 6.22 us -> 0.02 us
    ppermute x0 -> x1, waiting for transfers between devices: none -> 4.3 us  [per_device(): swapped = lax.ppermute(send, PAIR, [(0, 1), (1, 0)])]
    ppermute x0 -> x1, starting transfers between devices: none -> 2.55 us  [per_device(): swapped = lax.ppermute(send, PAIR, [(0, 1), (1, 0)])]
    all_gather x1 -> x0, blocking collectives: 2.21 us -> none  [per_device(): cot_c = lax.all_gather(cot_own, 'c')]
  transfers between devices with their start and end apart: 7 -> 5, of which waited for: 5 -> 3; matrix products, arithmetic and copies ran while one was open for 2% -> 0% of each run, Pallas kernels for 6% -> 5%
where the time goes in v5:
time: 157 us; the launch traced here: 155 us
  blocking collectives  89.5 us (57%)
  waiting for transfers between devices  24.4 us (16%)
  starting transfers between devices  15.3 us (10%)
  between operations  14.1 us (9%)
  Pallas kernels  11.4 us (7%)
    all_to_all x3, blocking collectives, exchange(): return lax.all_to_all(x, axis, 0, 0, tiled=True)  89.5 us
    all_to_all x2, waiting for transfers between devices, exchange(): return lax.all_to_all(x, axis, 0, 0, tiled=True)  19.4 us
    all_to_all x2, starting transfers between devices, exchange(): return lax.all_to_all(x, axis, 0, 0, tiled=True)  12.7 us
    ppermute x1, waiting for transfers between devices, per_device(): swapped = lax.ppermute(send, PAIR, [(0, 1), (1, 0)])  4.3 us
    pallas_call x1, Pallas kernels, per_device(): local_call(functools.partial(proj_kernel, scale), pltpu.HBM((blocks, cols...  3.22 us
  transfers between devices with their start and end apart: 5, of which 3 were waited for; matrix products, arithmetic and copies ran while one was open for 0% of the time, Pallas kernels for 5%

profile of v5, /device:TPU:6, one launch (start us, length us, event | category | flops | bytes accessed | tf_op | source)
XLA Modules:
  0.0 155.4 jit_solution(12293040152037129634)
XLA Ops:
  7.2 0.0 all-gather.3.cloned.1.call-start
  7.2 0.7 all-gather.3.cloned.1.call-update
  7.9 1.3 shard_map.84
  9.2 0.0 copy-start
  9.2 0.0 copy-start.1
  9.3 0.0 copy-start.2
  9.3 51.8 %all_to_all.25.got_ref = bf16[64,40,256]{2,1,0:T(8,128)(2,1)S(1)} all-to-all(bf16[64,40,256]{2,1,0:T(8,128)(2,1)S(1)} %shard_map.84), channel_id=1, replica_groups=mesh['y'=8,'zh'=4,'zl'=2,'x'=4,'c'=2] {'y','zh','zl'}, dimensions={0} | all-to-all | bytes 2621440 | tf_op jit(solution)/shard_map/all_to_all | solution.py:47
  61.0 0.7 shard_map.88
  61.8 8.3 %all-to-all-start.1 = ((bf16[64,8,128]{2,1,0:T(8,128)(2,1)}), bf16[64,8,128]{2,1,0:T(8,128)(2,1)S(1)}, u32[]{:S(2)}, u32[]{:S(2)}) async-start(bf16[64,8,128]{2,1,0:T(8,128)(2,1)} %shard_map.88), calls=%async_computation.1 | async-start | bytes 262144 | tf_op jit(solution)/shard_map/all_to_all | solution.py:47
  70.0 0.0 reduce-scatter.2.cloned.1.call-start
  70.1 0.0 copy-done
  70.1 0.0 copy-done.1
  70.1 0.0 copy-done.2
  70.1 0.7 shard_map.87
  70.8 11.9 %all-to-all-done.1 = bf16[64,8,128]{2,1,0:T(8,128)(2,1)S(1)} async-done(((bf16[64,8,128]{2,1,0:T(8,128)(2,1)}), bf16[64,8,128]{2,1,0:T(8,128)(2,1)S(1)}, u32[]{:S(2)}, u32[]{:S(2)}) %all-to-all-start.1) | async-done | bytes 131104 | tf_op jit(solution)/shard_map/all_to_all | solution.py:47
  82.7 0.0 all-gather.3.cloned.1.call-done
  82.7 3.2 %shard_map.92 = bf16[8,256,512]{2,1,0:T(8,128)(2,1)} custom-call(s32[1]{0:T(128)} %bitcast.place_ref, bf16[256,512]{1,0:T(8,128)(2,1)S(1)} %copy-done.2, bf16[512,128]{1,0:T(8,128)(2,1)S(1)} %bitcast.10, f32[256,512]{1,0:T(8,128)S(1)} %get-tuple-element.25.inner_ref, bf16[2,8,256,256]{3,2,1,0:T(8,128)(2,1)} %bitcast.14), custom_call_target="tpu_custom_call" | custom-call | flops 570425344 | bytes 3145728 | tf_op jit(solution)/shard_map/pallas_call | solution.py:210
  85.9 0.0 reduce-scatter.2.cloned.1.call-update
  85.9 2.2 %shard_map.85 = (bf16[256,256]{1,0:T(8,128)(2,1)S(1)}, bf16[256,256]{1,0:T(8,128)(2,1)S(1)}) custom-call(s32[1]{0:T(128)} %bitcast.place_ref, bf16[2,8,256,256]{3,2,1,0:T(8,128)(2,1)} %bitcast.15, bf16[64,40,256]{2,1,0:T(8,128)(2,1)S(1)} %all_to_all.25.got_ref), custom_call_target="tpu_custom_call" | custom-call | flops 536870912 | bytes 3145728 | tf_op jit(solution)/shard_map/pallas_call | solution.py:193
  88.1 2.6 %collective-permute-start = (bf16[256,256]{1,0:T(8,128)(2,1)S(1)}, bf16[256,256]{1,0:T(8,128)(2,1)S(1)}, u32[]{:S(2)}, u32[]{:S(2)}) collective-permute-start(bf16[256,256]{1,0:T(8,128)(2,1)S(1)} %get-tuple-element.16), channel_id=1, source_target_pairs={{0,8},{8,0},{1,9},{9,1},{2,10},{10,2},{3,11},{11,3},{4,12},{12,4},... | collective-permute-start | bytes 393224 | tf_op jit(solution)/shard_map/ppermute | solution.py:206
  90.6 4.3 %collective-permute-done.got_ref = bf16[256,256]{1,0:T(8,128)(2,1)S(1)} collective-permute-done((bf16[256,256]{1,0:T(8,128)(2,1)S(1)}, bf16[256,256]{1,0:T(8,128)(2,1)S(1)}, u32[]{:S(2)}, u32[]{:S(2)}) %collective-permute-start) | collective-permute-done | bytes 131104 | tf_op jit(solution)/shard_map/ppermute | solution.py:206
  95.0 0.3 shard_map.86
  95.2 20.4 %all_to_all.26.got_ref = bf16[64,8,128]{2,1,0:T(8,128)(2,1)S(1)} all-to-all(bf16[64,8,128]{2,1,0:T(8,128)(2,1)S(1)} %bitcast.13), channel_id=1, replica_groups=mesh['y'=8,'zh'=4,'zl'=2,'x'=4,'c'=2] {'y','zh','zl'}, dimensions={0} | all-to-all | bytes 262144 | tf_op jit(solution)/shard_map/all_to_all | solution.py:47
  115.7 0.1 shard_map.90
  115.7 17.3 %all_to_all.27 = bf16[64,8,128]{2,1,0:T(8,128)(2,1)S(1)} all-to-all(bf16[64,8,128]{2,1,0:T(8,128)(2,1)S(1)} %shard_map.90), channel_id=1, replica_groups=mesh['y'=8,'zh'=4,'zl'=2,'x'=4,'c'=2] {'y','zh','zl'}, dimensions={0} | all-to-all | bytes 262144 | tf_op jit(solution)/shard_map/all_to_all | solution.py:47
  133.0 0.0 reduce-scatter.2.cloned.1.call-done
  133.0 4.4 %all-to-all-start.4 = ((bf16[8,32,512]{2,1,0:T(8,128)(2,1)}), bf16[8,32,512]{2,1,0:T(8,128)(2,1)S(1)}, u32[]{:S(2)}, u32[]{:S(2)}) async-start(bf16[8,32,512]{2,1,0:T(8,128)(2,1)} %bitcast.17), calls=%async_computation.5 | async-start | bytes 524288 | tf_op jit(solution)/shard_map/all_to_all | solution.py:47
  137.4 1.9 %shard_map.89 = (bf16[256,512]{1,0:T(8,128)(2,1)}, f32[256,512]{1,0:T(8,128)S(1)}, f32[256,512]{1,0:T(8,128)S(1)}) custom-call(bf16[256,512]{1,0:T(8,128)(2,1)S(1)} %copy-done.2, bf16[256,512]{1,0:T(8,128)(2,1)S(1)} %copy-done, bf16[256,512]{1,0:T(8,128)(2,1)S(1)} %copy-done.1, bf16[256,512]{1,0:T(8,128)(2,1)S(1)} %get-tuple-element.17.g_ref, ...), custom_call_target="tpu_custom_call" | custom-call | flops 301989888 | bytes 2097152 | tf_op jit(solution)/shard_map/pallas_call | solution.py:242
  139.3 1.1 shard_map.91
  140.4 7.5 %all-to-all-done.4 = bf16[8,32,512]{2,1,0:T(8,128)(2,1)S(1)} async-done(((bf16[8,32,512]{2,1,0:T(8,128)(2,1)}), bf16[8,32,512]{2,1,0:T(8,128)(2,1)S(1)}, u32[]{:S(2)}, u32[]{:S(2)}) %all-to-all-start.4) | async-done | bytes 262176 | tf_op jit(solution)/shard_map/all_to_all | solution.py:47
  147.9 0.6 multiply_bitcast_fusion
  (1 shorter events, 0.0 us)
Async XLA Ops:
  7.2 75.5 %all-gather.3.cloned.1.call-start = ((), (), s32[]{:S(2)}) async-start(), calls=%async_computation.7 | async-start | bytes 2228224 | tf_op jit(solution)/shard_map/all_gather | solution.py:182
  9.2 60.9 %copy-start = (bf16[256,512]{1,0:T(8,128)(2,1)S(1)}, bf16[256,512]{1,0:T(8,128)(2,1)}, u32[]{:S(2)}) copy-start(bf16[256,512]{1,0:T(8,128)(2,1)} %k_ref.7) | copy-start | bytes 786436
  9.2 60.9 %copy-start.1 = (bf16[256,512]{1,0:T(8,128)(2,1)S(1)}, bf16[256,512]{1,0:T(8,128)(2,1)}, u32[]{:S(2)}) copy-start(bf16[256,512]{1,0:T(8,128)(2,1)} %v_ref.7) | copy-start | bytes 786436
  9.3 60.9 %copy-start.2 = (bf16[256,512]{1,0:T(8,128)(2,1)S(1)}, bf16[256,512]{1,0:T(8,128)(2,1)}, u32[]{:S(2)}) copy-start(bf16[256,512]{1,0:T(8,128)(2,1)} %q_ref.7) | copy-start | bytes 786436
  61.8 20.9 %all-to-all-start.1 = ((bf16[64,8,128]{2,1,0:T(8,128)(2,1)}), bf16[64,8,128]{2,1,0:T(8,128)(2,1)S(1)}, u32[]{:S(2)}, u32[]{:S(2)}) async-start(bf16[64,8,128]{2,1,0:T(8,128)(2,1)} %shard_map.88), calls=%async_computation.1 | async-start | bytes 262144 | tf_op jit(solution)/shard_map/all_to_all | solution.py:47
  70.0 63.0 %reduce-scatter.2.cloned.1.call-start = ((), (), s32[]{:S(2)}) async-start(), calls=%async_computation.6 | async-start | bytes 2359296 | tf_op jit(solution)/shard_map/reduce_scatter | solution.py:228
  88.1 6.9 %collective-permute-start = (bf16[256,256]{1,0:T(8,128)(2,1)S(1)}, bf16[256,256]{1,0:T(8,128)(2,1)S(1)}, u32[]{:S(2)}, u32[]{:S(2)}) collective-permute-start(bf16[256,256]{1,0:T(8,128)(2,1)S(1)} %get-tuple-element.16), channel_id=1, source_target_pairs={{0,8},{8,0},{1,9},{9,1},{2,10},{10,2},{3,11},{11,3},{4,12},{12,4},... | collective-permute-start | bytes 393224 | tf_op jit(solution)/shard_map/ppermute | solution.py:206
  133.0 14.9 %all-to-all-start.4 = ((bf16[8,32,512]{2,1,0:T(8,128)(2,1)}), bf16[8,32,512]{2,1,0:T(8,128)(2,1)S(1)}, u32[]{:S(2)}, u32[]{:S(2)}) async-start(bf16[8,32,512]{2,1,0:T(8,128)(2,1)} %bitcast.17), calls=%async_computation.5 | async-start | bytes 524288 | tf_op jit(solution)/shard_map/all_to_all | solution.py:47
Sparse Core Ops, SparseCore 0:
  10.1 67.2 all-gather.2
  86.0 43.9 reduce-scatter.1

commit v6 on v5

--- a/solution.py
+++ b/solution.py
@@ -14,7 +14,7 @@
 TP = ("x", "c")
 BF16 = jnp.bfloat16
 F32 = jnp.float32
-VMEM_BYTES = 48 * 1024 * 1024
+VMEM_BYTES = 24 * 1024 * 1024
 IN_VMEM = pl.BlockSpec(memory_space=pltpu.VMEM)
 IN_SMEM = pl.BlockSpec(memory_space=pltpu.SMEM)
 
@@ -48,9 +48,9 @@
 
 
 def first_kernel(k_ref, v_ref, w_ref, out_ref):
-    count, rows, half = out_ref.shape
+    count, rows, _ = out_ref.shape
     own = w_ref.shape[0]
-    share = rows - own
+    share = (rows - 2 * own) // 2
     per_head = DH // share
     for h in range(k_ref.shape[1] // DH):
         kv = mm(k_ref[:, head(h)], v_ref[:, head(h)], 0, 0)
@@ -58,20 +58,21 @@
         low = (kv - high.astype(F32)).astype(BF16)
         for i in range(per_head):
             piece = slice(i * share, (i + 1) * share)
-            out_ref[h * per_head + i, own:, :DH] = high[piece]
-            out_ref[h * per_head + i, own:, DH:] = low[piece]
+            out_ref[h * per_head + i, 2 * own : 2 * own + share, :] = high[piece]
+            out_ref[h * per_head + i, 2 * own + share :, :] = low[piece]
     for s in range(count):
-        out_ref[s, :own, :] = w_ref[:, (s % 2) * half : (s % 2 + 1) * half]
+        out_ref[s, :own, :] = w_ref[:, head(2 * (s % 2))]
+        out_ref[s, own : 2 * own, :] = w_ref[:, head(2 * (s % 2) + 1)]
 
 
 def prior_kernel(got_ref, sums_ref):
     count, share, _ = sums_ref.shape
-    own = got_ref.shape[1] - share
+    at = got_ref.shape[1] - 2 * share
     running = jnp.zeros(sums_ref.shape[1:], F32)
     for s in range(count):
         sums_ref[s] = running.astype(BF16)
-        high = got_ref[s, own:, :DH].astype(F32)
-        running = running + (high + got_ref[s, own:, DH:].astype(F32))
+        high = got_ref[s, at : at + share, :].astype(F32)
+        running = running + (high + got_ref[s, at + share :, :].astype(F32))
 
 
 def later_kernel(got_ref, sums_ref):
@@ -90,35 +91,37 @@
         inner_ref[:, head(h)] = mm(attn, v_ref[:, head(h)], 1, 0)
 
 
-def half_grad_kernel(place_ref, cot_ref, got_ref, keep_ref, send_ref):
-    blocks, _, cols = cot_ref.shape[1:]
-    own = cols * blocks // got_ref.shape[0]
+def half_grad_kernel(own, top_ref, low_ref, other_top_ref, other_low_ref, got_ref, keep_ref, send_ref):
+    cores, chips, _, cols = top_ref.shape
     per_block = cols // own
-    total = None
-    for b in range(blocks):
-        weight = got_ref[b * per_block : (b + 1) * per_block, :own, :]
-        term = mm(cot_ref[0, b], weight.reshape(cols, weight.shape[2]), 1, 0)
-        total = term if total is None else total + term
-    mine = place_ref[0] == pl.program_id(0)
-
-    @pl.when(mine)
-    def _():
-        keep_ref[...] = total.astype(BF16)
-
-    @pl.when(jnp.logical_not(mine))
-    def _():
-        send_ref[...] = total.astype(BF16)
-
-
-def proj_kernel(scale, place_ref, q_ref, prior_ref, inner_ref, cot_ref, out_ref, attn_out_ref):
+    kept, sent = None, None
+    for x in range(chips):
+        for c in range(cores):
+            b = x * cores + c
+            sources = slice(b * per_block, (b + 1) * per_block)
+            left = got_ref[sources, :own, :].reshape(cols, DH)
+            right = got_ref[sources, own : 2 * own, :].reshape(cols, DH)
+            weight = jnp.concatenate([left, right], axis=1)
+            cot = jnp.concatenate([top_ref[c, x], low_ref[c, x]], axis=0)
+            term = mm(cot, weight, 1, 0)
+            kept = term if kept is None else kept + term
+            cot = jnp.concatenate([other_top_ref[c, x], other_low_ref[c, x]], axis=0)
+            term = mm(cot, weight, 1, 0)
+            sent = term if sent is None else sent + term
+    keep_ref[...] = kept.astype(BF16)
+    send_ref[...] = sent.astype(BF16)
+
+
+def proj_kernel(scale, q_ref, prior_ref, inner_ref, top_ref, low_ref, out_ref, attn_out_ref):
     @pl.when(pl.program_id(0) == 0)
     def _():
         for h in range(q_ref.shape[1] // DH):
             far = mm(q_ref[:, head(h)], prior_ref[head(h), :], 1, 0)
             attn_out_ref[:, head(h)] = (scale * (inner_ref[:, head(h)] + far)).astype(BF16)
 
-    for b in range(out_ref.shape[0]):
-        out_ref[b] = mm(cot_ref[0, b], attn_out_ref[...], 0, 0).astype(BF16)
+    for x in range(out_ref.shape[0]):
+        cot = jnp.concatenate([top_ref[0, x], low_ref[0, x]], axis=0)
+        out_ref[x, 0] = mm(cot, attn_out_ref[...], 0, 0).astype(BF16)
 
 
 def qg_kernel(place_ref, keep_ref, got_ref, q_ref, g_ref, qg_ref):
@@ -163,7 +166,8 @@
     tok, width = queries.shape
     heads = width // DH
     count, nz, ny = lax.axis_size(SEQ), lax.axis_size(Z), lax.axis_size("y")
-    blocks = lax.axis_size(TP)
+    nx, nc = lax.axis_size("x"), lax.axis_size("c")
+    blocks = nx * nc
     cols = out_cotangent.shape[1]
     scale = (DH * tok * count) ** -0.5
     place = lax.axis_index(PAIR).reshape(1)
@@ -177,10 +181,19 @@
     big = tok * width
 
     sent = local_call(
-        first_kernel, shape((count, own + share, half), BF16), square, 12 * big
+        first_kernel, shape((count, 2 * own + 2 * share, DH), BF16), square, 12 * big
     )(in_hbm(keys), in_hbm(values), in_hbm(weight_t))
-    cot = lax.all_gather(out_cotangent, (PAIR,) + TP).reshape(2, blocks, tok, cols)
+    cot_own, sent = lax.optimization_barrier((out_cotangent, sent))
+    cot_other = lax.ppermute(cot_own, PAIR, [(0, 1), (1, 0)])
     got = exchange(sent, SEQ)
+
+    own_x, other_x = lax.all_gather(cot_own, "x"), lax.all_gather(cot_other, "x")
+    got, own_x, other_x = lax.optimization_barrier((got, own_x, other_x))
+    rows = tok // 2
+    own_top = lax.all_gather(own_x[:, :rows], "c")
+    own_low = lax.all_gather(own_x[:, rows:], "c")
+    other_top = lax.all_gather(other_x[:, :rows], "c")
+    other_low = lax.all_gather(other_x[:, rows:], "c")
     attn, attn_inner = local_call(
         attn_kernel,
         (shape((heads, tok, tok), BF16), shape((tok, width), F32)),
@@ -191,40 +204,32 @@
     prior = exchange(sums, SEQ).reshape(heads * DH, DH)
 
     keep, send = local_call(
-        half_grad_kernel,
+        functools.partial(half_grad_kernel, own),
         (shape((tok, half), BF16), shape((tok, half), BF16)),
         full,
         24 * big,
-        grid=(2,),
-        in_specs=[
-            IN_SMEM,
-            pl.BlockSpec((1, blocks, tok, cols), lambda m: (m, 0, 0, 0)),
-            pl.BlockSpec(got.shape, lambda m: (0, 0, 0)),
-        ],
-        out_specs=[pl.BlockSpec((tok, half), lambda m: (0, 0))] * 2,
-    )(place, in_hbm(cot), got)
+    )(own_top, own_low, other_top, other_low, got)
+    prior, keep, send = lax.optimization_barrier((prior, keep, send))
     swapped = lax.ppermute(send, PAIR, [(0, 1), (1, 0)])
 
-    step = blocks // 2
-    whole = pl.BlockSpec((tok, width), lambda i, p: (0, 0))
+    whole = pl.BlockSpec((tok, width), lambda i: (0, 0))
+    cot_spec = pl.BlockSpec((1, nx, tok // 2, cols), lambda i: (i, 0, 0, 0))
     proj_term = local_call(
         functools.partial(proj_kernel, scale),
-        pltpu.HBM((blocks, cols, width), BF16),
+        pltpu.HBM((nx, nc, cols, width), BF16),
         square + full,
         24 * big,
-        grid_spec=pltpu.PrefetchScalarGridSpec(
-            num_scalar_prefetch=1,
-            grid=(blocks // step,),
-            in_specs=[
-                whole,
-                pl.BlockSpec((heads * DH, DH), lambda i, p: (0, 0)),
-                whole,
-                pl.BlockSpec((1, step, tok, cols), lambda i, p: (p[0], i, 0, 0)),
-            ],
-            out_specs=pl.BlockSpec((step, cols, width), lambda i, p: (i, 0, 0)),
-            scratch_shapes=[pltpu.VMEM((tok, width), BF16)],
-        ),
-    )(place, queries, prior, attn_inner, in_hbm(cot))
+        grid=(nc,),
+        in_specs=[
+            whole,
+            pl.BlockSpec((heads * DH, DH), lambda i: (0, 0)),
+            whole,
+            cot_spec,
+            cot_spec,
+        ],
+        out_specs=pl.BlockSpec((nx, 1, cols, width), lambda i: (0, i, 0, 0)),
+        scratch_shapes=[pltpu.VMEM((tok, width), BF16)],
+    )(queries, prior, attn_inner, own_top, own_low)
     proj_y = lax.psum_scatter(
         proj_term.reshape(blocks * cols, width), "y", scatter_dimension=0, tiled=True
     )

time: 157 us -> 174 us (1.11)
  starting transfers between devices: 15.3 us -> 37.4 us
  blocking collectives: 89.5 us -> 79.5 us
  waiting for transfers between devices: 24.4 us -> 29 us
  local copies, waits for them, and re-layouts: 0.02 us -> 2.23 us
    all_to_all x3 -> x2, blocking collectives: 89.5 us -> 42.6 us  [exchange(): return lax.all_to_all(x, axis, 0, 0, tiled=True)]
    all_gather x0 -> x6, blocking collectives: none -> 36.9 us  [the longest x1 14.1 us: per_device(): lax.all_gather(cot_other, 'x')]
    all_to_all x2 -> x3, starting transfers between devices: 12.7 us -> 31.1 us  [exchange(): return lax.all_to_all(x, axis, 0, 0, tiled=True)]
    ppermute x0 -> x1, waiting for transfers between devices: none -> 15.2 us  [per_device(): cot_other = lax.ppermute(cot_own, PAIR, [(0, 1), (1, 0)])]
    all_to_all x2 -> x3, waiting for transfers between devices: 19.4 us -> 9.5 us  [exchange(): return lax.all_to_all(x, axis, 0, 0, tiled=True)]
    ppermute x0 -> x1, starting transfers between devices: none -> 3.48 us  [per_device(): cot_other = lax.ppermute(cot_own, PAIR, [(0, 1), (1, 0)])]
  transfers between devices with their start and end apart: 5 -> 6, of which waited for: 3 -> 4; matrix products, arithmetic and copies ran while one was open for 0% -> 1% of each run, Pallas kernels for 5% -> 3%
where the time goes in v6:
time: 174 us; the launch traced here: 173 us
  blocking collectives  79.5 us (46%)
  starting transfers between devices  37.4 us (21%)
  waiting for transfers between devices  29 us (17%)
  between operations  14.2 us (8%)
  Pallas kernels  9.94 us (6%)
  local copies, waits for them, and re-layouts  2.23 us (1%)
    all_to_all x2, blocking collectives, exchange(): return lax.all_to_all(x, axis, 0, 0, tiled=True)  42.6 us
    all_to_all x3, starting transfers between devices, exchange(): return lax.all_to_all(x, axis, 0, 0, tiled=True)  31.1 us
    ppermute x1, waiting for transfers between devices, per_device(): cot_other = lax.ppermute(cot_own, PAIR, [(0, 1), (1, 0)])  15.2 us
    all_gather x1, blocking collectives, per_device(): lax.all_gather(cot_other, 'x')  14.1 us
    all_gather x1, blocking collectives, per_device(): lax.all_gather(cot_own, 'x')  14 us
    all_to_all x3, waiting for transfers between devices, exchange(): return lax.all_to_all(x, axis, 0, 0, tiled=True)  9.5 us
    ppermute x1, waiting for transfers between devices, per_device(): swapped = lax.ppermute(send, PAIR, [(0, 1), (1, 0)])  4.28 us
  transfers between devices with their start and end apart: 6, of which 4 were waited for; matrix products, arithmetic and copies ran while one was open for 1% of the time, Pallas kernels for 3%

profile of v6, /device:TPU:6, one launch (start us, length us, event | category | flops | bytes accessed | tf_op | source)
XLA Modules:
  0.0 172.9 jit_solution(14436049472348252718)
XLA Ops:
  7.2 2.4 %shard_map.84 = bf16[64,80,128]{2,1,0:T(8,128)(2,1)} custom-call(bf16[256,512]{1,0:T(8,128)(2,1)} %k_ref.7, bf16[256,512]{1,0:T(8,128)(2,1)} %v_ref.7, bf16[32,512]{1,0:T(8,128)(2,1)} %bitcast.29), custom_call_target="tpu_custom_call" | custom-call | flops 33554432 | bytes 1572864 | tf_op jit(solution)/shard_map/pallas_call | solution.py:183
  9.5 0.0 copy-start.8
  9.6 0.0 copy-start
  9.6 0.0 copy-start.1
  9.6 0.0 copy-start.2
  9.6 16.7 %all-to-all-start = ((bf16[64,80,128]{2,1,0:T(8,128)(2,1)}), bf16[64,80,128]{2,1,0:T(8,128)(2,1)S(1)}, u32[]{:S(2)}, u32[]{:S(2)}) async-start(bf16[64,80,128]{2,1,0:T(8,128)(2,1)} %shard_map.84), calls=%async_computation | async-start | bytes 2621440 | tf_op jit(solution)/shard_map/all_to_all | solution.py:47
  26.3 0.0 copy-done.8
  26.3 3.5 %collective-permute-start = (bf16[256,256]{1,0:T(8,128)(2,1)S(1)}, bf16[256,256]{1,0:T(8,128)(2,1)S(1)}, u32[]{:S(2)}, u32[]{:S(2)}) collective-permute-start(bf16[256,256]{1,0:T(8,128)(2,1)S(1)} %copy-done.8), channel_id=1, source_target_pairs={{0,8},{8,0},{1,9},{9,1},{2,10},{10,2},{3,11},{11,3},{4,12},{12,4},... | collective-permute-start | bytes 393224 | tf_op jit(solution)/shard_map/ppermute | solution.py:187
  29.8 0.0 copy-done
  29.8 0.0 copy-done.1
  29.8 0.0 copy-done.2
  29.8 0.7 shard_map.88
  30.5 0.0 copy-start.3
  30.5 0.0 copy-start.5
  30.5 14.0 %all-gather = bf16[1024,256]{1,0:T(8,128)(2,1)} all-gather(bf16[256,256]{1,0:T(8,128)(2,1)S(1)} %copy-done.8), channel_id=2, replica_groups=mesh['y'=8,'zh'=4,'zl'=2,'x'=4,'c'=2] {'x'}, dimensions={0}, use_global_device_ids=true | all-gather | bytes 655360 | tf_op jit(solution)/shard_map/all_gather | solution.py:190
  44.6 15.2 %collective-permute-done = bf16[256,256]{1,0:T(8,128)(2,1)S(1)} collective-permute-done((bf16[256,256]{1,0:T(8,128)(2,1)S(1)}, bf16[256,256]{1,0:T(8,128)(2,1)S(1)}, u32[]{:S(2)}, u32[]{:S(2)}) %collective-permute-start) | collective-permute-done | bytes 131104 | tf_op jit(solution)/shard_map/ppermute | solution.py:187
  59.8 14.1 %all-gather.1 = bf16[1024,256]{1,0:T(8,128)(2,1)} all-gather(bf16[256,256]{1,0:T(8,128)(2,1)S(1)} %collective-permute-done), channel_id=3, replica_groups=mesh['y'=8,'zh'=4,'zl'=2,'x'=4,'c'=2] {'x'}, dimensions={0}, use_global_device_ids=true | all-gather | bytes 655360 | tf_op jit(solution)/shard_map/all_gather | solution.py:190
  73.9 0.0 all-to-all-done.got_ref
  73.9 0.7 shard_map.85
  74.6 0.0 copy-done.3
  74.6 0.0 copy-done.5
  74.6 10.7 %all-to-all-start.1 = ((bf16[64,8,128]{2,1,0:T(8,128)(2,1)}), bf16[64,8,128]{2,1,0:T(8,128)(2,1)S(1)}, u32[]{:S(2)}, u32[]{:S(2)}) async-start(bf16[64,8,128]{2,1,0:T(8,128)(2,1)} %shard_map.85), calls=%async_computation.1 | async-start | bytes 262144 | tf_op jit(solution)/shard_map/all_to_all | solution.py:47
  85.4 0.0 reduce-scatter.2.cloned.1.call-start
  85.4 0.0 copy-start.7
  85.4 1.1 fusion.1
  86.5 2.2 %all-gather.2 = bf16[8,128,256]{2,1,0:T(8,128)(2,1)S(1)} all-gather(bf16[4,128,256]{2,1,0:T(8,128)(2,1)S(1)} %get-tuple-element.45), channel_id=4, replica_groups=mesh['y'=8,'zh'=4,'zl'=2,'x'=4,'c'=2] {'c'}, dimensions={0}, use_global_device_ids=true | all-gather | bytes 786432 | tf_op jit(solution)/shard_map/all_gather | solution.py:193
  88.7 2.2 %all-gather.3 = bf16[8,128,256]{2,1,0:T(8,128)(2,1)S(1)} all-gather(bf16[4,128,256]{2,1,0:T(8,128)(2,1)S(1)} %get-tuple-element.44), channel_id=5, replica_groups=mesh['y'=8,'zh'=4,'zl'=2,'x'=4,'c'=2] {'c'}, dimensions={0}, use_global_device_ids=true | all-gather | bytes 786432 | tf_op jit(solution)/shard_map/all_gather | solution.py:194
  90.9 0.0 copy-done.7
  90.9 2.2 %all-gather.4 = bf16[8,128,256]{2,1,0:T(8,128)(2,1)S(1)} all-gather(bf16[4,128,256]{2,1,0:T(8,128)(2,1)S(1)} %get-tuple-element.43), channel_id=6, replica_groups=mesh['y'=8,'zh'=4,'zl'=2,'x'=4,'c'=2] {'c'}, dimensions={0}, use_global_device_ids=true | all-gather | bytes 786432 | tf_op jit(solution)/shard_map/all_gather | solution.py:195
  93.1 2.2 %all-gather.5 = bf16[8,128,256]{2,1,0:T(8,128)(2,1)S(1)} all-gather(bf16[4,128,256]{2,1,0:T(8,128)(2,1)S(1)} %get-tuple-element.42), channel_id=7, replica_groups=mesh['y'=8,'zh'=4,'zl'=2,'x'=4,'c'=2] {'c'}, dimensions={0}, use_global_device_ids=true | all-gather | bytes 786432 | tf_op jit(solution)/shard_map/all_gather | solution.py:196
  95.3 0.7 shard_map.86
  96.0 2.0 %all-to-all-done.1 = bf16[64,8,128]{2,1,0:T(8,128)(2,1)S(1)} async-done(((bf16[64,8,128]{2,1,0:T(8,128)(2,1)}), bf16[64,8,128]{2,1,0:T(8,128)(2,1)S(1)}, u32[]{:S(2)}, u32[]{:S(2)}) %all-to-all-start.1) | async-done | bytes 131104 | tf_op jit(solution)/shard_map/all_to_all | solution.py:47
  98.0 1.0 copy-done.6
  99.0 2.1 %shard_map.92 = bf16[4,2,256,512]{3,2,1,0:T(8,128)(2,1)} custom-call(bf16[256,512]{1,0:T(8,128)(2,1)S(1)} %copy-done, bf16[512,128]{1,0:T(8,128)(2,1)S(1)} %bitcast.21, f32[256,512]{1,0:T(8,128)S(1)} %copy-done.6, bf16[2,4,128,256]{3,2,1,0:T(8,128)(2,1)S(1)} %bitcast.16, bf16[2,4,128,256]{3,2,1,0:T(8,128)(2,1)S(1)} %bitcast.18), custom_call_target="tpu_custom_call" | custom-call | flops 570425344 | bytes 3145728 | tf_op jit(solution)/shard_map/pallas_call | solution.py:217
  101.2 0.0 reduce-scatter.2.cloned.1.call-update
  101.2 0.0 copy-start.4
  101.2 2.7 %collective-permute-start.1 = (bf16[256,256]{1,0:T(8,128)(2,1)S(1)}, bf16[256,256]{1,0:T(8,128)(2,1)S(1)}, u32[]{:S(2)}, u32[]{:S(2)}) collective-permute-start(bf16[256,256]{1,0:T(8,128)(2,1)S(1)} %get-tuple-element.31), channel_id=1, source_target_pairs={{0,8},{8,0},{1,9},{9,1},{2,10},{10,2},{3,11},{11,3},{4,12},{12,4},... | collective-permute-start | bytes 393224 | tf_op jit(solution)/shard_map/ppermute | solution.py:213
  103.9 4.3 %collective-permute-done.1.got_ref = bf16[256,256]{1,0:T(8,128)(2,1)S(1)} collective-permute-done((bf16[256,256]{1,0:T(8,128)(2,1)S(1)}, bf16[256,256]{1,0:T(8,128)(2,1)S(1)}, u32[]{:S(2)}, u32[]{:S(2)}) %collective-permute-start.1) | collective-permute-done | bytes 131104 | tf_op jit(solution)/shard_map/ppermute | solution.py:213
  108.2 0.3 shard_map.87
  108.5 25.1 %all_to_all.25.got_ref = bf16[64,8,128]{2,1,0:T(8,128)(2,1)S(1)} all-to-all(bf16[64,8,128]{2,1,0:T(8,128)(2,1)S(1)} %bitcast.24), channel_id=1, replica_groups=mesh['y'=8,'zh'=4,'zl'=2,'x'=4,'c'=2] {'y','zh','zl'}, dimensions={0} | all-to-all | bytes 262144 | tf_op jit(solution)/shard_map/all_to_all | solution.py:47
  133.6 0.1 shard_map.90
  133.7 17.5 %all_to_all.26 = bf16[64,8,128]{2,1,0:T(8,128)(2,1)S(1)} all-to-all(bf16[64,8,128]{2,1,0:T(8,128)(2,1)S(1)} %shard_map.90), channel_id=1, replica_groups=mesh['y'=8,'zh'=4,'zl'=2,'x'=4,'c'=2] {'y','zh','zl'}, dimensions={0} | all-to-all | bytes 262144 | tf_op jit(solution)/shard_map/all_to_all | solution.py:47
  151.2 3.7 %all-to-all-start.4 = ((bf16[8,32,512]{2,1,0:T(8,128)(2,1)}), bf16[8,32,512]{2,1,0:T(8,128)(2,1)S(1)}, u32[]{:S(2)}, u32[]{:S(2)}) async-start(bf16[8,32,512]{2,1,0:T(8,128)(2,1)} %bitcast.28), calls=%async_computation.5 | async-start | bytes 524288 | tf_op jit(solution)/shard_map/all_to_all | solution.py:47
  154.9 0.0 copy-done.4
  154.9 1.9 %shard_map.89 = (bf16[256,512]{1,0:T(8,128)(2,1)}, f32[256,512]{1,0:T(8,128)S(1)}, f32[256,512]{1,0:T(8,128)S(1)}) custom-call(bf16[256,512]{1,0:T(8,128)(2,1)S(1)} %copy-done, bf16[256,512]{1,0:T(8,128)(2,1)S(1)} %copy-done.1, bf16[256,512]{1,0:T(8,128)(2,1)S(1)} %copy-done.2, bf16[256,512]{1,0:T(8,128)(2,1)S(1)} %get-tuple-element.32.g_ref, ...), custom_call_target="tpu_custom_call" | custom-call | flops 301989888 | bytes 2097152 | tf_op jit(solution)/shard_map/pallas_call | solution.py:247
  156.8 1.1 shard_map.91
  157.9 7.5 %all-to-all-done.4 = bf16[8,32,512]{2,1,0:T(8,128)(2,1)S(1)} async-done(((bf16[8,32,512]{2,1,0:T(8,128)(2,1)}), bf16[8,32,512]{2,1,0:T(8,128)(2,1)S(1)}, u32[]{:S(2)}, u32[]{:S(2)}) %all-to-all-start.4) | async-done | bytes 262176 | tf_op jit(solution)/shard_map/all_to_all | solution.py:47
  165.4 0.6 multiply_bitcast_fusion
  (4 shorter events, 0.1 us)
Async XLA Ops:
  9.5 16.8 %copy-start.8 = (bf16[256,256]{1,0:T(8,128)(2,1)S(1)}, bf16[256,256]{1,0:T(8,128)(2,1)}, u32[]{:S(2)}) copy-start(bf16[256,256]{1,0:T(8,128)(2,1)} %param.8) | copy-start | bytes 393220
  9.6 20.2 %copy-start = (bf16[256,512]{1,0:T(8,128)(2,1)S(1)}, bf16[256,512]{1,0:T(8,128)(2,1)}, u32[]{:S(2)}) copy-start(bf16[256,512]{1,0:T(8,128)(2,1)} %q_ref.7) | copy-start | bytes 786436
  9.6 20.3 %copy-start.1 = (bf16[256,512]{1,0:T(8,128)(2,1)S(1)}, bf16[256,512]{1,0:T(8,128)(2,1)}, u32[]{:S(2)}) copy-start(bf16[256,512]{1,0:T(8,128)(2,1)} %k_ref.7) | copy-start | bytes 786436
  9.6 20.3 %copy-start.2 = (bf16[256,512]{1,0:T(8,128)(2,1)S(1)}, bf16[256,512]{1,0:T(8,128)(2,1)}, u32[]{:S(2)}) copy-start(bf16[256,512]{1,0:T(8,128)(2,1)} %v_ref.7) | copy-start | bytes 786436
  9.6 64.3 %all-to-all-start = ((bf16[64,80,128]{2,1,0:T(8,128)(2,1)}), bf16[64,80,128]{2,1,0:T(8,128)(2,1)S(1)}, u32[]{:S(2)}, u32[]{:S(2)}) async-start(bf16[64,80,128]{2,1,0:T(8,128)(2,1)} %shard_map.84), calls=%async_computation | async-start | bytes 2621440 | tf_op jit(solution)/shard_map/all_to_all | solution.py:47
  26.3 33.5 %collective-permute-start = (bf16[256,256]{1,0:T(8,128)(2,1)S(1)}, bf16[256,256]{1,0:T(8,128)(2,1)S(1)}, u32[]{:S(2)}, u32[]{:S(2)}) collective-permute-start(bf16[256,256]{1,0:T(8,128)(2,1)S(1)} %copy-done.8), channel_id=1, source_target_pairs={{0,8},{8,0},{1,9},{9,1},{2,10},{10,2},{3,11},{11,3},{4,12},{12,4},... | collective-permute-start | bytes 393224 | tf_op jit(solution)/shard_map/ppermute | solution.py:187
  30.5 44.1 %copy-start.3 = (bf16[4,256,256]{2,1,0:T(8,128)(2,1)}, bf16[4,256,256]{2,1,0:T(8,128)(2,1)S(1)}, u32[]{:S(2)}) copy-start(bf16[4,256,256]{2,1,0:T(8,128)(2,1)S(1)} %get-tuple-element.33.attn_ref) | copy-start | bytes 1572868
  30.5 44.1 %copy-start.5 = (f32[256,512]{1,0:T(8,128)}, f32[256,512]{1,0:T(8,128)S(1)}, u32[]{:S(2)}) copy-start(f32[256,512]{1,0:T(8,128)S(1)} %get-tuple-element.41.inner_ref) | copy-start | bytes 1572868
  74.6 23.4 %all-to-all-start.1 = ((bf16[64,8,128]{2,1,0:T(8,128)(2,1)}), bf16[64,8,128]{2,1,0:T(8,128)(2,1)S(1)}, u32[]{:S(2)}, u32[]{:S(2)}) async-start(bf16[64,8,128]{2,1,0:T(8,128)(2,1)} %shard_map.85), calls=%async_computation.1 | async-start | bytes 262144 | tf_op jit(solution)/shard_map/all_to_all | solution.py:47
  85.4 65.8 %reduce-scatter.2.cloned.1.call-start = ((), (), s32[]{:S(2)}) async-start(), calls=%async_computation.6 | async-start | bytes 2359296 | tf_op jit(solution)/shard_map/reduce_scatter | solution.py:233
  85.4 5.5 %copy-start.7 = (bf16[1024,256]{1,0:T(8,128)(2,1)S(1)}, bf16[1024,256]{1,0:T(8,128)(2,1)}, u32[]{:S(2)}) copy-start(bf16[1024,256]{1,0:T(8,128)(2,1)} %all-gather.1) | copy-start | bytes 1572868
  98.0 1.0 copy-start.6
  101.2 53.7 %copy-start.4 = (bf16[4,256,256]{2,1,0:T(8,128)(2,1)S(1)}, bf16[4,256,256]{2,1,0:T(8,128)(2,1)}, u32[]{:S(2)}) copy-start(bf16[4,256,256]{2,1,0:T(8,128)(2,1)} %copy-done.3) | copy-start | bytes 1572868
  101.2 7.0 %collective-permute-start.1 = (bf16[256,256]{1,0:T(8,128)(2,1)S(1)}, bf16[256,256]{1,0:T(8,128)(2,1)S(1)}, u32[]{:S(2)}, u32[]{:S(2)}) collective-permute-start(bf16[256,256]{1,0:T(8,128)(2,1)S(1)} %get-tuple-element.31), channel_id=1, source_target_pairs={{0,8},{8,0},{1,9},{9,1},{2,10},{10,2},{3,11},{11,3},{4,12},{12,4},... | collective-permute-start | bytes 393224 | tf_op jit(solution)/shard_map/ppermute | solution.py:213
  151.2 14.2 %all-to-all-start.4 = ((bf16[8,32,512]{2,1,0:T(8,128)(2,1)}), bf16[8,32,512]{2,1,0:T(8,128)(2,1)S(1)}, u32[]{:S(2)}, u32[]{:S(2)}) async-start(bf16[8,32,512]{2,1,0:T(8,128)(2,1)} %bitcast.28), calls=%async_computation.5 | async-start | bytes 524288 | tf_op jit(solution)/shard_map/all_to_all | solution.py:47
Sparse Core Ops, SparseCore 0:
  101.3 46.3 reduce-scatter.1

commit v7 on v4

--- a/solution.py
+++ b/solution.py
@@ -11,7 +11,7 @@
 SEQ = ("y", "z")
 BF16 = jnp.bfloat16
 F32 = jnp.float32
-VMEM_BYTES = 48 * 1024 * 1024
+VMEM_BYTES = 24 * 1024 * 1024
 
 
 def mm(a, b, ca, cb):
@@ -45,14 +45,11 @@
 def first_kernel(k_ref, v_ref, w_ref, out_ref):
     peers, rows, width = out_ref.shape
     own = w_ref.shape[0]
-    share = (rows - own) // 2
+    share = rows - own
     for h in range(width // DH):
-        kv = mm(k_ref[:, head(h)], v_ref[:, head(h)], 0, 0)
-        high = kv.astype(BF16)
-        low = (kv - high.astype(F32)).astype(BF16)
+        kv = mm(k_ref[:, head(h)], v_ref[:, head(h)], 0, 0).astype(BF16)
         for p in range(peers):
-            out_ref[p, own : own + share, head(h)] = high[p * share : (p + 1) * share]
-            out_ref[p, own + share :, head(h)] = low[p * share : (p + 1) * share]
+            out_ref[p, own:, head(h)] = kv[p * share : (p + 1) * share]
     for p in range(peers):
         out_ref[p, :own, :] = w_ref[...]
 
@@ -60,32 +57,27 @@
 def split_kernel(got_ref, weight_ref, part_ref, total_ref):
     peers, rows, width = got_ref.shape
     own = weight_ref.shape[0] // peers
-    share = (rows - own) // 2
-    running = jnp.zeros((share, width), F32)
+    running = jnp.zeros((rows - own, width), F32)
     for p in range(peers):
         weight_ref[p * own : (p + 1) * own, :] = got_ref[p, :own, :]
         part_ref[p] = running
-        high = got_ref[p, own : own + share, :].astype(F32)
-        running = running + (high + got_ref[p, own + share :, :].astype(F32))
+        running = running + got_ref[p, own:, :].astype(F32)
     for p in range(total_ref.shape[0]):
         total_ref[p] = running
 
 
-def back_scan_kernel(got_ref, part_ref, total_ref):
-    peers, rows, width = got_ref.shape
-    running = jnp.zeros((rows, width), F32)
-    for p in reversed(range(peers)):
-        part_ref[p] = running
-        running = running + got_ref[p]
-    for p in range(total_ref.shape[0]):
-        total_ref[p] = running
-
-
-def join_kernel(reverse, place_ref, totals_ref, part_ref, out_ref):
+def later_kernel(got_ref, sums_ref):
+    running = jnp.zeros(sums_ref.shape[1:], F32)
+    for s in reversed(range(sums_ref.shape[0])):
+        sums_ref[s] = running.astype(BF16)
+        running = running + got_ref[s].astype(F32)
+
+
+def join_kernel(place_ref, totals_ref, part_ref, out_ref):
     place = place_ref[0]
     base = jnp.zeros(totals_ref.shape[1:], F32)
     for other in range(totals_ref.shape[0]):
-        counts = place < other if reverse else place > other
+        counts = place > other
         base = base + jnp.where(counts, totals_ref[other], 0.0)
     for p in range(part_ref.shape[0]):
         out_ref[p] = (base + part_ref[p]).astype(out_ref.dtype)
@@ -100,16 +92,31 @@
         inner_ref[:, head(h)] = mm(attn, v_ref[:, head(h)], 1, 0)
 
 
-def proj_kernel(scale, q_ref, prior_ref, inner_ref, top_ref, low_ref, out_ref, attn_out_ref):
-    @pl.when(pl.program_id(0) == 0)
-    def _():
-        for h in range(q_ref.shape[1] // DH):
-            far = mm(q_ref[:, head(h)], prior_ref[:, head(h)], 1, 0)
-            attn_out_ref[:, head(h)] = (scale * (inner_ref[:, head(h)] + far)).astype(BF16)
-
-    for x in range(out_ref.shape[0]):
+def attn_out_kernel(scale, q_ref, prior_ref, inner_ref, out_ref):
+    for h in range(q_ref.shape[1] // DH):
+        far = mm(q_ref[:, head(h)], prior_ref[:, head(h)], 1, 0)
+        out_ref[:, head(h)] = (scale * (inner_ref[:, head(h)] + far)).astype(BF16)
+
+
+def proj_kernel(attn_out_ref, top_ref, low_ref, out_ref, acc_ref):
+    step = pl.program_id(0)
+    total = None
+    for x in range(attn_out_ref.shape[0]):
         cot = jnp.concatenate([top_ref[0, x], low_ref[0, x]], axis=0)
-        out_ref[x, 0] = mm(cot, attn_out_ref[...], 0, 0).astype(BF16)
+        term = mm(cot, attn_out_ref[x, 0], 0, 0)
+        total = term if total is None else total + term
+
+    @pl.when(step == 0)
+    def _():
+        acc_ref[...] = total
+
+    @pl.when(step > 0)
+    def _():
+        acc_ref[...] += total
+
+    @pl.when(step == pl.num_programs(0) - 1)
+    def _():
+        out_ref[...] = acc_ref[...].astype(BF16)
 
 
 def grad_out_kernel(top_ref, low_ref, w_ref, q_ref, g_ref, qg_ref, acc_ref):
@@ -133,7 +140,7 @@
         g = acc_ref[...].astype(BF16)
         g_ref[...] = g
         for h in range(g.shape[1] // DH):
-            qg_ref[:, head(h)] = mm(q_ref[:, head(h)], g[:, head(h)], 0, 0)
+            qg_ref[head(h), :] = mm(q_ref[:, head(h)], g[:, head(h)], 0, 0).astype(BF16)
 
 
 def inner_grads_kernel(scale, q_ref, k_ref, v_ref, g_ref, attn_ref, prior_ref, dq_ref, dk_ref, dv_ref):
@@ -150,7 +157,7 @@
 
 def outer_grads_kernel(scale, k_ref, v_ref, later_ref, near_k_ref, near_v_ref, dk_ref, dv_ref):
     for h in range(k_ref.shape[1] // DH):
-        later = later_ref[:, head(h)]
+        later = later_ref[head(h), :]
         far_k = mm(v_ref[:, head(h)], later, 1, 1)
         dk_ref[:, head(h)] = (scale * (near_k_ref[:, head(h)] + far_k)).astype(BF16)
         far_v = mm(k_ref[:, head(h)], later, 1, 0)
@@ -165,9 +172,9 @@
     return pltpu.with_memory_space_constraint(x, pltpu.HBM)
 
 
-def join(place, totals, part, reverse):
+def join(place, totals, part):
     return local_call(
-        functools.partial(join_kernel, reverse),
+        join_kernel,
         shape(part.shape, BF16),
         0,
         3 * part.size * 4,
@@ -195,7 +202,7 @@
     big = tok * width
 
     sent = local_call(
-        first_kernel, shape((nz, own + 2 * share, width), BF16), square, 3 * big
+        first_kernel, shape((nz, own + share, width), BF16), square, 3 * big
     )(in_hbm(keys), in_hbm(values), in_hbm(weight_t))
     got = exchange(sent, "z")
     weight_z, kv_part, kv_total = local_call(
@@ -220,53 +227,43 @@
         2 * wide,
         10 * big,
     )(queries, keys, values)
-    prior = exchange(join(place, exchange(kv_total, "y"), kv_part, False), "z")
-    prior = prior.reshape(DH, width)
+    prior = exchange(join(place, exchange(kv_total, "y"), kv_part), "z").reshape(DH, width)
 
     n_blocks = nx * nc
-
     whole = pl.BlockSpec((tok, width), lambda i: (0, 0))
-    state = pl.BlockSpec((DH, width), lambda i: (0, 0))
     cot_spec = pl.BlockSpec((1, nx, half, cols), lambda i: (i, 0, 0, 0))
     by_core = pl.BlockSpec((nx, 1, cols, width), lambda i: (0, i, 0, 0))
-    proj_term = local_call(
-        functools.partial(proj_kernel, scale),
-        pltpu.HBM((nx, nc, cols, width), BF16),
-        square + 2 * tok * cols * width * n_blocks,
-        2 * n_blocks * cols * width,
-        grid=(nc,),
-        in_specs=[whole, state, whole, cot_spec, cot_spec],
-        out_specs=by_core,
-        scratch_shapes=[pltpu.VMEM((tok, width), BF16)],
-    )(queries, prior, attn_inner, cot_top, cot_low)
-    proj_term = proj_term.reshape(n_blocks * cols, width)
-    proj_y = lax.psum_scatter(proj_term, "y", scatter_dimension=0, tiled=True)
+    attn_out = local_call(
+        functools.partial(attn_out_kernel, scale), shape((tok, width), BF16), square, 8 * big
+    )(queries, prior, attn_inner)
+    attn_out_y = lax.all_gather(attn_out, "y", axis=0, tiled=True)
+    turn = [(y * n_blocks + t, t * ny + y) for y in range(ny) for t in range(n_blocks)]
+    cot_turned = lax.ppermute(cot_own, ("y", "x", "c"), turn)
 
     grad_out, qg = local_call(
         grad_out_kernel,
-        (shape((tok, width), BF16), shape((DH, width), F32)),
+        (shape((tok, width), BF16), shape((heads * DH, DH), BF16)),
         square + 2 * tok * cols * width * n_blocks,
         2 * n_blocks * cols * width,
         grid=(nc,),
         in_specs=[cot_spec, cot_spec, by_core, whole],
-        out_specs=[whole, state],
+        out_specs=[whole, pl.BlockSpec((heads * DH, DH), lambda i: (0, 0))],
         scratch_shapes=[pltpu.VMEM((tok, width), F32)],
     )(cot_top, cot_low, in_hbm(weight_full.reshape(nx, nc, cols, width)), queries)
-    qg_got = exchange(qg.reshape(nz, share, width), "z")
-    qg_part, qg_total = local_call(
-        back_scan_kernel,
-        (shape((nz, share, width), F32), shape((ny, share, width), F32)),
-        0,
-        2 * big,
-    )(qg_got)
+    qg, cot_turned = lax.optimization_barrier((qg, cot_turned))
+    turned_x = lax.all_gather(cot_turned, "x")
+    turned_top = lax.all_gather(turned_x[:, :half], "c")
+    turned_low = lax.all_gather(turned_x[:, half:], "c")
+    pieces = (ny * nz, heads * DH // (ny * nz), DH)
+    qg_got = exchange(qg.reshape(pieces), SEQ)
+    later_sums = local_call(later_kernel, shape(pieces, BF16), 0, 2 * big)(qg_got)
     grad_q, near_k, near_v = local_call(
         functools.partial(inner_grads_kernel, scale),
         (shape((tok, width), BF16), shape((tok, width), F32), shape((tok, width), F32)),
         4 * wide + square,
         16 * big,
     )(queries, keys, values, grad_out, attn, prior)
-    later = exchange(join(place, exchange(qg_total, "y"), qg_part, True), "z")
-    later = later.reshape(DH, width)
+    later = exchange(later_sums, SEQ).reshape(heads * DH, DH)
     grad_k, grad_v = local_call(
         functools.partial(outer_grads_kernel, scale),
         (shape((tok, width), BF16), shape((tok, width), BF16)),
@@ -274,7 +271,17 @@
         12 * big,
     )(keys, values, later, near_k, near_v)
 
-    proj_parts = exchange(proj_y.reshape(nz, own, width), "z")
+    proj_part = local_call(
+        proj_kernel,
+        shape((cols, width), BF16),
+        2 * tok * cols * width * n_blocks,
+        24 * big,
+        grid=(nc,),
+        in_specs=[by_core, cot_spec, cot_spec],
+        out_specs=pl.BlockSpec((cols, width), lambda i: (0, 0)),
+        scratch_shapes=[pltpu.VMEM((cols, width), F32)],
+    )(in_hbm(attn_out_y.reshape(nx, nc, tok, width)), turned_top, turned_low)
+    proj_parts = exchange(proj_part.reshape(nz, own, width), "z")
     proj_sum = jnp.sum(proj_parts.astype(F32), axis=0)
     grad_proj = (proj_sum / jnp.sqrt(F32(tok * ny * nz))).T
     return grad_q, grad_k, grad_v, grad_proj

time: 152 us -> 162 us (1.066); the launches traced: 151 us -> 159 us
  blocking collectives: 89.8 us -> 60.1 us
  starting transfers between devices: 17 us -> 35.1 us
  waiting for transfers between devices: 18.5 us -> 34.8 us
  Pallas kernels: 11.2 us -> 14.3 us
    all_to_all x4 -> x1, blocking collectives: 72.7 us -> 24.8 us  [exchange(): return lax.all_to_all(x, axis, 0, 0, tiled=True)]
    all_to_all x3 -> x5, waiting for transfers between devices: 12.1 us -> 34.8 us  [exchange(): return lax.all_to_all(x, axis, 0, 0, tiled=True)]
    all_gather x0 -> x3, blocking collectives: none -> 17.1 us  [the longest x1 12.8 us: per_device(): turned_x = lax.all_gather(cot_turned, 'x')]
    all_to_all x3 -> x5, starting transfers between devices: 16.9 us -> 32.6 us  [exchange(): return lax.all_to_all(x, axis, 0, 0, tiled=True)]
    all_gather x1, waiting for transfers between devices: 5.41 us -> 0.01 us  [per_device(): weight_full = lax.all_gather(weight_z, 'y', axis=0, tiled=True)]
    pallas_call x6, Pallas kernels: 6.77 us -> 9.8 us  [the longest x1 3.11 us: per_device(): local_call(grad_out_kernel, (shape((tok, width), BF16), shape((heads * DH...]
    ppermute x0 -> x1, starting transfers between devices: none -> 2.37 us  [per_device(): cot_turned = lax.ppermute(cot_own, ('y', 'x', 'c'), turn)]
  transfers between devices with their start and end apart: 5 -> 8, of which waited for: 4 -> 5; matrix products, arithmetic and copies ran while one was open for 0% -> 0% of each run, Pallas kernels for 6% -> 8%
where the time goes in v7:
time: 162 us; the launch traced here: 159 us
  blocking collectives  60.1 us (37%)
  starting transfers between devices  35.1 us (22%)
  waiting for transfers between devices  34.8 us (21%)
  Pallas kernels  14.3 us (9%)
  between operations  14.2 us (9%)
    all_to_all x5, waiting for transfers between devices, exchange(): return lax.all_to_all(x, axis, 0, 0, tiled=True)  34.8 us
    all_to_all x5, starting transfers between devices, exchange(): return lax.all_to_all(x, axis, 0, 0, tiled=True)  32.6 us
    all_to_all x1, blocking collectives, exchange(): return lax.all_to_all(x, axis, 0, 0, tiled=True)  24.8 us
    all_gather x1, blocking collectives, per_device(): cot_x = lax.all_gather(cot_own, 'x')  13.8 us
    all_gather x1, blocking collectives, per_device(): turned_x = lax.all_gather(cot_turned, 'x')  12.8 us
  transfers between devices with their start and end apart: 8, of which 5 were waited for; matrix products, arithmetic and copies ran while one was open for 0% of the time, Pallas kernels for 8%

profile of v7, /device:TPU:6, one launch (start us, length us, event | category | flops | bytes accessed | tf_op | source)
XLA Modules:
  0.0 159.2 jit_solution(2588800771625421731)
XLA Ops:
  7.2 0.0 copy-start
  7.2 0.0 copy-start.1
  7.2 0.0 copy-start.2
  7.2 0.0 all-gather.9.cloned.1.call-start
  7.2 1.4 shard_map.84
  8.6 24.8 %all_to_all.30.got_ref = bf16[8,48,512]{2,1,0:T(8,128)(2,1)S(1)} all-to-all(bf16[8,48,512]{2,1,0:T(8,128)(2,1)S(1)} %shard_map.84), channel_id=1, replica_groups=mesh['y'=8,'z'=8,'x'=4,'c'=2] {'z'}, dimensions={0} | all-to-all | bytes 786432 | tf_op jit(solution)/shard_map/all_to_all | solution.py:42
  33.4 0.0 copy-start.3
  33.4 0.8 shard_map.85
  34.2 0.0 all-gather.9.cloned.1.call-update
  34.2 7.1 %all-to-all-start.1 = ((f32[8,16,512]{2,1,0:T(8,128)}), f32[8,16,512]{2,1,0:T(8,128)S(1)}, u32[]{:S(2)}, u32[]{:S(2)}) async-start(f32[8,16,512]{2,1,0:T(8,128)} %get-tuple-element.25), calls=%async_computation.1 | async-start | bytes 524288 | tf_op jit(solution)/shard_map/all_to_all | solution.py:42
  41.4 12.5 %all-to-all-done.1.totals_ref = f32[8,16,512]{2,1,0:T(8,128)S(1)} async-done(((f32[8,16,512]{2,1,0:T(8,128)}), f32[8,16,512]{2,1,0:T(8,128)S(1)}, u32[]{:S(2)}, u32[]{:S(2)}) %all-to-all-start.1) | async-done | bytes 262176 | tf_op jit(solution)/shard_map/all_to_all | solution.py:42
  53.8 0.7 shard_map.88
  54.5 3.4 %all-to-all-start.2 = ((bf16[8,16,512]{2,1,0:T(8,128)(2,1)}), bf16[8,16,512]{2,1,0:T(8,128)(2,1)S(1)}, u32[]{:S(2)}, u32[]{:S(2)}) async-start(bf16[8,16,512]{2,1,0:T(8,128)(2,1)} %shard_map.88), calls=%async_computation.2 | async-start | bytes 262144 | tf_op jit(solution)/shard_map/all_to_all | solution.py:42
  57.9 0.0 all-gather.11.cloned.1.call-start
  58.0 0.0 copy-done
  58.0 0.0 copy-done.1
  58.0 0.0 copy-done.2
  58.0 0.7 shard_map.87
  58.6 8.3 %all-to-all-done.2 = bf16[8,16,512]{2,1,0:T(8,128)(2,1)S(1)} async-done(((bf16[8,16,512]{2,1,0:T(8,128)(2,1)}), bf16[8,16,512]{2,1,0:T(8,128)(2,1)S(1)}, u32[]{:S(2)}, u32[]{:S(2)}) %all-to-all-start.2) | async-done | bytes 131104 | tf_op jit(solution)/shard_map/all_to_all | solution.py:42
  66.9 0.9 shard_map.92
  67.8 0.0 all-gather.11.cloned.1.call-update
  67.9 0.0 copy-done.3
  67.9 2.4 %collective-permute-start = (bf16[256,256]{1,0:T(8,128)(2,1)S(1)}, bf16[256,256]{1,0:T(8,128)(2,1)S(1)}, u32[]{:S(2)}, u32[]{:S(2)}) collective-permute-start(bf16[256,256]{1,0:T(8,128)(2,1)S(1)} %copy-done.3), channel_id=1, source_target_pairs={{0,0},{1,64},{2,128},{3,192},{4,256},{5,320},{6,384},{7,448},{64,1... | collective-permute-start | bytes 393224 | tf_op jit(solution)/shard_map/ppermute | solution.py:241
  70.2 13.8 %all-gather = bf16[1024,256]{1,0:T(8,128)(2,1)S(1)} all-gather(bf16[256,256]{1,0:T(8,128)(2,1)S(1)} %copy-done.3), channel_id=2, replica_groups=mesh['y'=8,'z'=8,'x'=4,'c'=2] {'x'}, dimensions={0}, use_global_device_ids=true | all-gather | bytes 655360 | tf_op jit(solution)/shard_map/all_gather | solution.py:220
  84.1 2.2 %all-gather.1 = bf16[8,128,256]{2,1,0:T(8,128)(2,1)S(1)} all-gather(bf16[4,128,256]{2,1,0:T(8,128)(2,1)S(1)} %get-tuple-element.39), channel_id=3, replica_groups=mesh['y'=8,'z'=8,'x'=4,'c'=2] {'c'}, dimensions={0}, use_global_device_ids=true | all-gather | bytes 786432 | tf_op jit(solution)/shard_map/all_gather | solution.py:222
  86.3 2.2 %all-gather.2 = bf16[8,128,256]{2,1,0:T(8,128)(2,1)S(1)} all-gather(bf16[4,128,256]{2,1,0:T(8,128)(2,1)S(1)} %get-tuple-element.38), channel_id=4, replica_groups=mesh['y'=8,'z'=8,'x'=4,'c'=2] {'c'}, dimensions={0}, use_global_device_ids=true | all-gather | bytes 786432 | tf_op jit(solution)/shard_map/all_gather | solution.py:223
  88.4 0.0 all-gather.9.cloned.1.call-done
  88.4 3.1 %shard_map.86 = (bf16[256,512]{1,0:T(8,128)(2,1)S(1)}, bf16[512,128]{1,0:T(8,128)(2,1)}) custom-call(bf16[2,4,128,256]{3,2,1,0:T(8,128)(2,1)S(1)} %bitcast.16, bf16[2,4,128,256]{3,2,1,0:T(8,128)(2,1)S(1)} %bitcast.17, bf16[4,2,256,512]{3,2,1,0:T(8,128)(2,1)} %bitcast.25, bf16[256,512]{1,0:T(8,128)(2,1)S(1)} %copy-done.2), custom_call_target="tpu_custom_call" | custom-call | flops 570425344 | bytes 2097152 | tf_op jit(solution)/shard_map/pallas_call | solution.py:243
  91.5 0.0 collective-permute-done
  91.5 7.3 %all-to-all-start.3 = ((bf16[64,8,128]{2,1,0:T(8,128)(2,1)}), bf16[64,8,128]{2,1,0:T(8,128)(2,1)S(1)}, u32[]{:S(2)}, u32[]{:S(2)}) async-start(bf16[64,8,128]{2,1,0:T(8,128)(2,1)} %bitcast.7), calls=%async_computation.3 | async-start | bytes 262144 | tf_op jit(solution)/shard_map/all_to_all | solution.py:42
  98.9 12.8 %all-gather.3 = bf16[1024,256]{1,0:T(8,128)(2,1)S(1)} all-gather(bf16[256,256]{1,0:T(8,128)(2,1)S(1)} %collective-permute-done), channel_id=5, replica_groups=mesh['y'=8,'z'=8,'x'=4,'c'=2] {'x'}, dimensions={0}, use_global_device_ids=true | all-gather | bytes 655360 | tf_op jit(solution)/shard_map/all_gather | solution.py:254
  111.7 1.3 all-to-all-done.3.got_ref
  113.0 0.7 shard_map.90
  113.7 11.4 %all-to-all-start.4 = ((bf16[64,8,128]{2,1,0:T(8,128)(2,1)}), bf16[64,8,128]{2,1,0:T(8,128)(2,1)S(1)}, u32[]{:S(2)}, u32[]{:S(2)}) async-start(bf16[64,8,128]{2,1,0:T(8,128)(2,1)} %shard_map.90), calls=%async_computation.4 | async-start | bytes 262144 | tf_op jit(solution)/shard_map/all_to_all | solution.py:42
  125.1 2.2 %all-gather.4 = bf16[8,128,256]{2,1,0:T(8,128)(2,1)S(1)} all-gather(bf16[4,128,256]{2,1,0:T(8,128)(2,1)S(1)} %get-tuple-element.37), channel_id=6, replica_groups=mesh['y'=8,'z'=8,'x'=4,'c'=2] {'c'}, dimensions={0}, use_global_device_ids=true | all-gather | bytes 786432 | tf_op jit(solution)/shard_map/all_gather | solution.py:255
  127.3 2.2 %all-gather.5 = bf16[8,128,256]{2,1,0:T(8,128)(2,1)S(1)} all-gather(bf16[4,128,256]{2,1,0:T(8,128)(2,1)S(1)} %get-tuple-element.36), channel_id=7, replica_groups=mesh['y'=8,'z'=8,'x'=4,'c'=2] {'c'}, dimensions={0}, use_global_device_ids=true | all-gather | bytes 786432 | tf_op jit(solution)/shard_map/all_gather | solution.py:256
  129.5 0.0 all-gather.11.cloned.1.call-done
  129.5 3.0 %shard_map.93 = bf16[256,512]{1,0:T(8,128)(2,1)} custom-call(bf16[4,2,256,512]{3,2,1,0:T(8,128)(2,1)} %bitcast.26, bf16[2,4,128,256]{3,2,1,0:T(8,128)(2,1)S(1)} %bitcast.18, bf16[2,4,128,256]{3,2,1,0:T(8,128)(2,1)S(1)} %bitcast.19), custom_call_target="tpu_custom_call" | custom-call | flops 536870912 | bytes 3145728 | tf_op jit(solution)/shard_map/pallas_call | solution.py:274
  132.5 5.4 %all-to-all-done.4 = bf16[64,8,128]{2,1,0:T(8,128)(2,1)S(1)} async-done(((bf16[64,8,128]{2,1,0:T(8,128)(2,1)}), bf16[64,8,128]{2,1,0:T(8,128)(2,1)S(1)}, u32[]{:S(2)}, u32[]{:S(2)}) %all-to-all-start.4) | async-done | bytes 131104 | tf_op jit(solution)/shard_map/all_to_all | solution.py:42
  137.9 3.4 %all-to-all-start.5 = ((bf16[8,32,512]{2,1,0:T(8,128)(2,1)}), bf16[8,32,512]{2,1,0:T(8,128)(2,1)S(1)}, u32[]{:S(2)}, u32[]{:S(2)}) async-start(bf16[8,32,512]{2,1,0:T(8,128)(2,1)} %bitcast.13), calls=%async_computation.5 | async-start | bytes 524288 | tf_op jit(solution)/shard_map/all_to_all | solution.py:42
  141.3 1.9 %shard_map.89 = (bf16[256,512]{1,0:T(8,128)(2,1)}, f32[256,512]{1,0:T(8,128)S(1)}, f32[256,512]{1,0:T(8,128)S(1)}) custom-call(bf16[256,512]{1,0:T(8,128)(2,1)S(1)} %copy-done.2, bf16[256,512]{1,0:T(8,128)(2,1)S(1)} %copy-done, bf16[256,512]{1,0:T(8,128)(2,1)S(1)} %copy-done.1, bf16[256,512]{1,0:T(8,128)(2,1)S(1)} %get-tuple-element.23.g_ref, ...), custom_call_target="tpu_custom_call" | custom-call | flops 301989888 | bytes 2097152 | tf_op jit(solution)/shard_map/pallas_call | solution.py:260
  143.2 1.1 shard_map.91
  144.3 7.4 %all-to-all-done.5 = bf16[8,32,512]{2,1,0:T(8,128)(2,1)S(1)} async-done(((bf16[8,32,512]{2,1,0:T(8,128)(2,1)}), bf16[8,32,512]{2,1,0:T(8,128)(2,1)S(1)}, u32[]{:S(2)}, u32[]{:S(2)}) %all-to-all-start.5) | async-done | bytes 262176 | tf_op jit(solution)/shard_map/all_to_all | solution.py:42
  151.7 0.6 multiply_bitcast_fusion
  (3 shorter events, 0.1 us)
Async XLA Ops:
  7.2 50.8 %copy-start = (bf16[256,512]{1,0:T(8,128)(2,1)S(1)}, bf16[256,512]{1,0:T(8,128)(2,1)}, u32[]{:S(2)}) copy-start(bf16[256,512]{1,0:T(8,128)(2,1)} %k_ref.7) | copy-start | bytes 786436
  7.2 50.8 %copy-start.1 = (bf16[256,512]{1,0:T(8,128)(2,1)S(1)}, bf16[256,512]{1,0:T(8,128)(2,1)}, u32[]{:S(2)}) copy-start(bf16[256,512]{1,0:T(8,128)(2,1)} %v_ref.7) | copy-start | bytes 786436
  7.2 50.8 %copy-start.2 = (bf16[256,512]{1,0:T(8,128)(2,1)S(1)}, bf16[256,512]{1,0:T(8,128)(2,1)}, u32[]{:S(2)}) copy-start(bf16[256,512]{1,0:T(8,128)(2,1)} %q_ref.7) | copy-start | bytes 786436
  7.2 81.2 %all-gather.9.cloned.1.call-start = ((), (), s32[]{:S(2)}) async-start(), calls=%async_computation.6 | async-start | bytes 2359296 | tf_op jit(solution)/shard_map/all_gather | solution.py:218
  33.4 34.4 %copy-start.3 = (bf16[256,256]{1,0:T(8,128)(2,1)S(1)}, bf16[256,256]{1,0:T(8,128)(2,1)}, u32[]{:S(2)}) copy-start(bf16[256,256]{1,0:T(8,128)(2,1)} %param.8) | copy-start | bytes 393220
  34.2 19.6 %all-to-all-start.1 = ((f32[8,16,512]{2,1,0:T(8,128)}), f32[8,16,512]{2,1,0:T(8,128)S(1)}, u32[]{:S(2)}, u32[]{:S(2)}) async-start(f32[8,16,512]{2,1,0:T(8,128)} %get-tuple-element.25), calls=%async_computation.1 | async-start | bytes 524288 | tf_op jit(solution)/shard_map/all_to_all | solution.py:42
  54.5 12.4 %all-to-all-start.2 = ((bf16[8,16,512]{2,1,0:T(8,128)(2,1)}), bf16[8,16,512]{2,1,0:T(8,128)(2,1)S(1)}, u32[]{:S(2)}, u32[]{:S(2)}) async-start(bf16[8,16,512]{2,1,0:T(8,128)(2,1)} %shard_map.88), calls=%async_computation.2 | async-start | bytes 262144 | tf_op jit(solution)/shard_map/all_to_all | solution.py:42
  57.9 71.6 %all-gather.11.cloned.1.call-start = ((), (), s32[]{:S(2)}) async-start(), calls=%async_computation.7 | async-start | bytes 2359296 | tf_op jit(solution)/shard_map/all_gather | solution.py:239
  67.9 23.7 %collective-permute-start = (bf16[256,256]{1,0:T(8,128)(2,1)S(1)}, bf16[256,256]{1,0:T(8,128)(2,1)S(1)}, u32[]{:S(2)}, u32[]{:S(2)}) collective-permute-start(bf16[256,256]{1,0:T(8,128)(2,1)S(1)} %copy-done.3), channel_id=1, source_target_pairs={{0,0},{1,64},{2,128},{3,192},{4,256},{5,320},{6,384},{7,448},{64,1... | collective-permute-start | bytes 393224 | tf_op jit(solution)/shard_map/ppermute | solution.py:241
  91.5 21.4 %all-to-all-start.3 = ((bf16[64,8,128]{2,1,0:T(8,128)(2,1)}), bf16[64,8,128]{2,1,0:T(8,128)(2,1)S(1)}, u32[]{:S(2)}, u32[]{:S(2)}) async-start(bf16[64,8,128]{2,1,0:T(8,128)(2,1)} %bitcast.7), calls=%async_computation.3 | async-start | bytes 262144 | tf_op jit(solution)/shard_map/all_to_all | solution.py:42
  113.7 24.2 %all-to-all-start.4 = ((bf16[64,8,128]{2,1,0:T(8,128)(2,1)}), bf16[64,8,128]{2,1,0:T(8,128)(2,1)S(1)}, u32[]{:S(2)}, u32[]{:S(2)}) async-start(bf16[64,8,128]{2,1,0:T(8,128)(2,1)} %shard_map.90), calls=%async_computation.4 | async-start | bytes 262144 | tf_op jit(solution)/shard_map/all_to_all | solution.py:42
  137.9 13.8 %all-to-all-start.5 = ((bf16[8,32,512]{2,1,0:T(8,128)(2,1)}), bf16[8,32,512]{2,1,0:T(8,128)(2,1)S(1)}, u32[]{:S(2)}, u32[]{:S(2)}) async-start(bf16[8,32,512]{2,1,0:T(8,128)(2,1)} %bitcast.13), calls=%async_computation.5 | async-start | bytes 524288 | tf_op jit(solution)/shard_map/all_to_all | solution.py:42
Sparse Core Ops, SparseCore 0:
  34.4 44.4 all-gather.8
  81.6 45.7 all-gather.10

commit v8 on v4

v8 whole, which is shorter than its diff:
```python
import functools

import jax
import jax.numpy as jnp
from jax import lax
from jax.experimental import pallas as pl
from jax.experimental.pallas import tpu as pltpu
from jax.sharding import Mesh, PartitionSpec as P

DH = 128
SEQ = ("y", "z")
BF16 = jnp.bfloat16
F32 = jnp.float32
VMEM_BYTES = 24 * 1024 * 1024


def mm(a, b, ca, cb):
    return lax.dot_general(a, b, (((ca,), (cb,)), ((), ())), preferred_element_type=F32)


def head(h):
    return slice(h * DH, (h + 1) * DH)


def local_call(kernel, out_shape, flops, moved, **kwargs):
    return pl.pallas_call(
        kernel,
        out_shape=out_shape,
        cost_estimate=pl.CostEstimate(flops=flops, transcendentals=0, bytes_accessed=moved),
        compiler_params=pltpu.CompilerParams(vmem_limit_bytes=VMEM_BYTES),
        **kwargs,
    )


def causal(tok):
    rows = lax.broadcasted_iota(jnp.int32, (tok, tok), 0)
    cols = lax.broadcasted_iota(jnp.int32, (tok, tok), 1)
    return rows >= cols


def exchange(x, axis):
    return lax.all_to_all(x, axis, 0, 0, tiled=True)


def spread_kernel(w_ref, out_ref):
    for p in range(out_ref.shape[0]):
        out_ref[p] = w_ref[...]


def kv_kernel(k_ref, v_ref, out_ref):
    share = out_ref.shape[1] // 2
    per_head = DH // share
    for h in range(k_ref.shape[1] // DH):
        kv = mm(k_ref[:, head(h)], v_ref[:, head(h)], 0, 0)
        high = kv.astype(BF16)
        low = (kv - high.astype(F32)).astype(BF16)
        for i in range(per_head):
            piece = slice(i * share, (i + 1) * share)
            out_ref[h * per_head + i, :share, :] = high[piece]
            out_ref[h * per_head + i, share:, :] = low[piece]


def prior_kernel(got_ref, sums_ref):
    count, share, _ = sums_ref.shape
    at = got_ref.shape[1] - 2 * share
    running = jnp.zeros(sums_ref.shape[1:], F32)
    for s in range(count):
        sums_ref[s] = running.astype(BF16)
        high = got_ref[s, at : at + share, :].astype(F32)
        running = running + (high + got_ref[s, at + share :, :].astype(F32))


def later_kernel(got_ref, sums_ref):
    running = jnp.zeros(sums_ref.shape[1:], F32)
    for s in reversed(range(sums_ref.shape[0])):
        sums_ref[s] = running.astype(BF16)
        running = running + got_ref[s].astype(F32)


def attn_kernel(q_ref, k_ref, v_ref, attn_ref, inner_ref):
    mask = causal(q_ref.shape[0])
    for h in range(q_ref.shape[1] // DH):
        scores = mm(q_ref[:, head(h)], k_ref[:, head(h)], 1, 1)
        attn = jnp.where(mask, scores, 0.0).astype(BF16)
        attn_ref[h] = attn
        inner_ref[:, head(h)] = mm(attn, v_ref[:, head(h)], 1, 0)


def proj_kernel(scale, q_ref, prior_ref, inner_ref, top_ref, low_ref, out_ref, attn_out_ref):
    @pl.when(pl.program_id(0) == 0)
    def _():
        for h in range(q_ref.shape[1] // DH):
            far = mm(q_ref[:, head(h)], prior_ref[head(h), :], 1, 0)
            attn_out_ref[:, head(h)] = (scale * (inner_ref[:, head(h)] + far)).astype(BF16)

    for x in range(out_ref.shape[0]):
        cot = jnp.concatenate([top_ref[0, x], low_ref[0, x]], axis=0)
        out_ref[x, 0] = mm(cot, attn_out_ref[...], 0, 0).astype(BF16)


def grad_out_kernel(top_ref, low_ref, w_ref, q_ref, g_ref, qg_ref, acc_ref):
    step = pl.program_id(0)
    term = None
    for x in range(w_ref.shape[0]):
        cot = jnp.concatenate([top_ref[0, x], low_ref[0, x]], axis=0)
        one = mm(cot, w_ref[x, 0], 1, 0)
        term = one if term is None else term + one

    @pl.when(step == 0)
    def _():
        acc_ref[...] = term

    @pl.when(step > 0)
    def _():
        acc_ref[...] += term

    @pl.when(step == pl.num_programs(0) - 1)
    def _():
        g = acc_ref[...].astype(BF16)
        g_ref[...] = g
        for h in range(g.shape[1] // DH):
            qg_ref[head(h), :] = mm(q_ref[:, head(h)], g[:, head(h)], 0, 0).astype(BF16)


def inner_grads_kernel(scale, q_ref, k_ref, v_ref, g_ref, attn_ref, prior_ref, dq_ref, dk_ref, dv_ref):
    mask = causal(q_ref.shape[0])
    for h in range(q_ref.shape[1] // DH):
        g = g_ref[:, head(h)]
        back = jnp.where(mask, mm(g, v_ref[:, head(h)], 1, 1), 0.0).astype(BF16)
        near = mm(back, k_ref[:, head(h)], 1, 0)
        far = mm(g, prior_ref[head(h), :], 1, 1)
        dq_ref[:, head(h)] = (scale * (near + far)).astype(BF16)
        dk_ref[:, head(h)] = mm(back, q_ref[:, head(h)], 0, 0)
        dv_ref[:, head(h)] = mm(attn_ref[h], g, 0, 0)


def outer_grads_kernel(scale, k_ref, v_ref, later_ref, near_k_ref, near_v_ref, dk_ref, dv_ref):
    for h in range(k_ref.shape[1] // DH):
        later = later_ref[head(h), :]
        far_k = mm(v_ref[:, head(h)], later, 1, 1)
        dk_ref[:, head(h)] = (scale * (near_k_ref[:, head(h)] + far_k)).astype(BF16)
        far_v = mm(k_ref[:, head(h)], later, 1, 0)
        dv_ref[:, head(h)] = (scale * (near_v_ref[:, head(h)] + far_v)).astype(BF16)


def shape(dims, dtype):
    return jax.ShapeDtypeStruct(dims, dtype)


def in_hbm(x):
    return pltpu.with_memory_space_constraint(x, pltpu.HBM)


def per_device(queries, keys, values, out_cotangent, proj_weight):
    tok, width = queries.shape
    heads = width // DH
    ny, nz = lax.axis_size("y"), lax.axis_size("z")
    nx, nc = lax.axis_size("x"), lax.axis_size("c")
    cols = out_cotangent.shape[1]
    scale = (DH * tok * ny * nz) ** -0.5
    weight_t = proj_weight.T
    own = weight_t.shape[0]
    share = heads * DH // (ny * nz)
    square = 2 * tok * DH * DH * heads
    wide = 2 * tok * tok * DH * heads
    big = tok * width
    pieces = (ny * nz, share, DH)

    spread = local_call(spread_kernel, shape((nz, own, width), BF16), 0, big)(in_hbm(weight_t))
    weight_z = exchange(spread, "z").reshape(nz * own, width)
    weight_full = lax.all_gather(weight_z, "y", axis=0, tiled=True)
    kv_pieces = local_call(
        kv_kernel, shape((ny * nz, 2 * share, DH), BF16), square, 3 * big
    )(in_hbm(keys), in_hbm(values))
    kv_pieces, cot_own, weight_z = lax.optimization_barrier((kv_pieces, out_cotangent, weight_z))
    got = exchange(kv_pieces, SEQ)
    cot_x = lax.all_gather(cot_own, "x")
    got, cot_x = lax.optimization_barrier((got, cot_x))
    half = tok // 2
    cot_top = lax.all_gather(cot_x[:, :half], "c")
    cot_low = lax.all_gather(cot_x[:, half:], "c")
    attn, attn_inner = local_call(
        attn_kernel,
        (shape((heads, tok, tok), BF16), shape((tok, width), F32)),
        2 * wide,
        10 * big,
    )(queries, keys, values)
    sums = local_call(prior_kernel, shape(pieces, BF16), 0, 2 * big)(got)
    prior = exchange(sums, SEQ).reshape(heads * DH, DH)

    n_blocks = nx * nc

    whole = pl.BlockSpec((tok, width), lambda i: (0, 0))
    state = pl.BlockSpec((heads * DH, DH), lambda i: (0, 0))
    cot_spec = pl.BlockSpec((1, nx, half, cols), lambda i: (i, 0, 0, 0))
    by_core = pl.BlockSpec((nx, 1, cols, width), lambda i: (0, i, 0, 0))
    proj_term = local_call(
        functools.partial(proj_kernel, scale),
        pltpu.HBM((nx, nc, cols, width), BF16),
        square + 2 * tok * cols * width * n_blocks,
        2 * n_blocks * cols * width,
        grid=(nc,),
        in_specs=[whole, state, whole, cot_spec, cot_spec],
        out_specs=by_core,
        scratch_shapes=[pltpu.VMEM((tok, width), BF16)],
    )(queries, prior, attn_inner, cot_top, cot_low)
    proj_term = proj_term.reshape(n_blocks * cols, width)
    proj_y = lax.psum_scatter(proj_term, "y", scatter_dimension=0, tiled=True)

    grad_out, qg = local_call(
        grad_out_kernel,
        (shape((tok, width), BF16), shape((heads * DH, DH), BF16)),
        square + 2 * tok * cols * width * n_blocks,
        2 * n_blocks * cols * width,
        grid=(nc,),
        in_specs=[cot_spec, cot_spec, by_core, whole],
        out_specs=[whole, state],
        scratch_shapes=[pltpu.VMEM((tok, width), F32)],
    )(cot_top, cot_low, in_hbm(weight_full.reshape(nx, nc, cols, width)), queries)
    qg_got = exchange(qg.reshape(pieces), SEQ)
    sums = local_call(later_kernel, shape(pieces, BF16), 0, 2 * big)(qg_got)
    grad_q, near_k, near_v = local_call(
        functools.partial(inner_grads_kernel, scale),
        (shape((tok, width), BF16), shape((tok, width), F32), shape((tok, width), F32)),
        4 * wide + square,
        16 * big,
    )(queries, keys, values, grad_out, attn, prior)
    later = exchange(sums, SEQ).reshape(heads * DH, DH)
    grad_k, grad_v = local_call(
        functools.partial(outer_grads_kernel, scale),
        (shape((tok, width), BF16), shape((tok, width), BF16)),
        2 * square,
        12 * big,
    )(keys, values, later, near_k, near_v)

    proj_parts = exchange(proj_y.reshape(nz, own, width), "z")
    proj_sum = jnp.sum(proj_parts.astype(F32), axis=0)
    grad_proj = (proj_sum / jnp.sqrt(F32(tok * ny * nz))).T
    return grad_q, grad_k, grad_v, grad_proj


def solution(mesh):
    seq, tp = mesh.devices.shape
    inner, cores = 8, 2
    grid = Mesh(
        mesh.devices.reshape(seq // inner, inner, tp // cores, cores), ("y", "z", "x", "c")
    )
    tokens, weight = P(SEQ, ("x", "c")), P(("x", "c"), SEQ)
    return jax.shard_map(
        per_device,
        mesh=grid,
        in_specs=(tokens, tokens, tokens, tokens, weight),
        out_specs=(tokens, tokens, tokens, weight),
        check_vma=False,
    )
```

time: 152 us -> 150 us (0.987)
  blocking collectives: 89.8 us -> 74.1 us
  starting transfers between devices: 17 us -> 25.2 us
  waiting for transfers between devices: 18.5 us -> 22.9 us
    all_to_all x4 -> x3, blocking collectives: 72.7 us -> 56.3 us  [exchange(): return lax.all_to_all(x, axis, 0, 0, tiled=True)]
    all_to_all x3, starting transfers between devices: 16.9 us -> 25.2 us  [exchange(): return lax.all_to_all(x, axis, 0, 0, tiled=True)]
    all_to_all x3, waiting for transfers between devices: 12.1 us -> 18.4 us  [exchange(): return lax.all_to_all(x, axis, 0, 0, tiled=True)]
    all_gather x1, waiting for transfers between devices: 5.41 us -> 0.02 us  [per_device(): weight_full = lax.all_gather(weight_z, 'y', axis=0, tiled=True)]
    reduce_scatter x1, waiting for transfers between devices: 0.99 us -> 4.46 us  [per_device(): proj_y = lax.psum_scatter(proj_term, 'y', scatter_dimension=0, tiled=True)]
    pallas_call x6 -> x5, Pallas kernels: 5.44 us -> 6.15 us  [the longest x1 2.48 us: per_device(): local_call(grad_out_kernel, (shape((tok, width), BF16), shape((heads * DH...]
  transfers between devices with their start and end apart: 5 -> 5, of which waited for: 4 -> 4; matrix products, arithmetic and copies ran while one was open for 0% -> 0% of each run, Pallas kernels for 6% -> 7%
where the time goes in v8:
time: 150 us; the launch traced here: 149 us
  blocking collectives  74.1 us (49%)
  starting transfers between devices  25.2 us (17%)
  waiting for transfers between devices  22.9 us (15%)
  between operations  14.2 us (9%)
  Pallas kernels  12 us (8%)
    all_to_all x3, blocking collectives, exchange(): return lax.all_to_all(x, axis, 0, 0, tiled=True)  56.3 us
    all_to_all x3, starting transfers between devices, exchange(): return lax.all_to_all(x, axis, 0, 0, tiled=True)  25.2 us
    all_to_all x3, waiting for transfers between devices, exchange(): return lax.all_to_all(x, axis, 0, 0, tiled=True)  18.4 us
    all_gather x1, blocking collectives, per_device(): cot_x = lax.all_gather(cot_own, 'x')  13.4 us
    reduce_scatter x1, waiting for transfers between devices, per_device(): proj_y = lax.psum_scatter(proj_term, 'y', scatter_dimension=0, tiled=True)  4.46 us
  transfers between devices with their start and end apart: 5, of which 4 were waited for; matrix products, arithmetic and copies ran while one was open for 0% of the time, Pallas kernels for 7%

profile of v8, /device:TPU:6, one launch (start us, length us, event | category | flops | bytes accessed | tf_op | source)
XLA Modules:
  0.0 149.1 jit_solution(705597501951701522)
XLA Ops:
  7.2 0.0 copy-start
  7.2 0.0 copy-start.1
  7.2 0.0 copy-start.3
  7.2 0.0 copy-start.2
  7.2 0.0 all-gather.5.cloned.1.call-start
  7.3 0.9 shard_map.85
  8.1 22.1 %all_to_all.30 = bf16[8,32,512]{2,1,0:T(8,128)(2,1)} all-to-all(bf16[8,32,512]{2,1,0:T(8,128)(2,1)S(1)} %shard_map.85), channel_id=1, replica_groups=mesh['y'=8,'z'=8,'x'=4,'c'=2] {'z'}, dimensions={0} | all-to-all | bytes 524288 | tf_op jit(solution)/shard_map/all_to_all | solution.py:42
  30.2 0.0 all-gather.5.cloned.1.call-update
  30.2 2.0 %shard_map.84 = bf16[64,16,128]{2,1,0:T(8,128)(2,1)} custom-call(bf16[256,512]{1,0:T(8,128)(2,1)} %k_ref.7, bf16[256,512]{1,0:T(8,128)(2,1)} %v_ref.7), custom_call_target="tpu_custom_call" | custom-call | flops 33554432 | bytes 393216 | tf_op jit(solution)/shard_map/pallas_call | solution.py:172
  32.2 8.1 %all-to-all-start.1 = ((bf16[64,16,128]{2,1,0:T(8,128)(2,1)}), bf16[64,16,128]{2,1,0:T(8,128)(2,1)S(1)}, u32[]{:S(2)}, u32[]{:S(2)}) async-start(bf16[64,16,128]{2,1,0:T(8,128)(2,1)} %shard_map.84), calls=%async_computation.1 | async-start | bytes 524288 | tf_op jit(solution)/shard_map/all_to_all | solution.py:42
  40.4 0.0 copy-done
  40.4 0.0 copy-done.1
  40.4 0.0 copy-done.2
  40.4 0.7 shard_map.87
  41.1 0.0 copy-done.3
  41.1 13.4 %all-gather = bf16[1024,256]{1,0:T(8,128)(2,1)S(1)} all-gather(bf16[256,256]{1,0:T(8,128)(2,1)S(1)} %copy-done.3), channel_id=2, replica_groups=mesh['y'=8,'z'=8,'x'=4,'c'=2] {'x'}, dimensions={0}, use_global_device_ids=true | all-gather | bytes 655360 | tf_op jit(solution)/shard_map/all_gather | solution.py:177
  54.5 2.4 %all-to-all-done.1.got_ref = bf16[64,16,128]{2,1,0:T(8,128)(2,1)S(1)} async-done(((bf16[64,16,128]{2,1,0:T(8,128)(2,1)}), bf16[64,16,128]{2,1,0:T(8,128)(2,1)S(1)}, u32[]{:S(2)}, u32[]{:S(2)}) %all-to-all-start.1) | async-done | bytes 262176 | tf_op jit(solution)/shard_map/all_to_all | solution.py:42
  56.9 0.7 shard_map.88
  57.6 10.2 %all-to-all-start.2 = ((bf16[64,8,128]{2,1,0:T(8,128)(2,1)}), bf16[64,8,128]{2,1,0:T(8,128)(2,1)S(1)}, u32[]{:S(2)}, u32[]{:S(2)}) async-start(bf16[64,8,128]{2,1,0:T(8,128)(2,1)} %shard_map.88), calls=%async_computation.2 | async-start | bytes 262144 | tf_op jit(solution)/shard_map/all_to_all | solution.py:42
  67.8 0.0 reduce-scatter.2.cloned.1.call-start
  67.9 2.2 %all-gather.1 = bf16[8,128,256]{2,1,0:T(8,128)(2,1)S(1)} all-gather(bf16[4,128,256]{2,1,0:T(8,128)(2,1)S(1)} %get-tuple-element.31), channel_id=3, replica_groups=mesh['y'=8,'z'=8,'x'=4,'c'=2] {'c'}, dimensions={0}, use_global_device_ids=true | all-gather | bytes 786432 | tf_op jit(solution)/shard_map/all_gather | solution.py:180
  70.1 2.2 %all-gather.2 = bf16[8,128,256]{2,1,0:T(8,128)(2,1)S(1)} all-gather(bf16[4,128,256]{2,1,0:T(8,128)(2,1)S(1)} %get-tuple-element.30), channel_id=4, replica_groups=mesh['y'=8,'z'=8,'x'=4,'c'=2] {'c'}, dimensions={0}, use_global_device_ids=true | all-gather | bytes 786432 | tf_op jit(solution)/shard_map/all_gather | solution.py:181
  72.2 8.5 %all-to-all-done.2 = bf16[64,8,128]{2,1,0:T(8,128)(2,1)S(1)} async-done(((bf16[64,8,128]{2,1,0:T(8,128)(2,1)}), bf16[64,8,128]{2,1,0:T(8,128)(2,1)S(1)}, u32[]{:S(2)}, u32[]{:S(2)}) %all-to-all-start.2) | async-done | bytes 131104 | tf_op jit(solution)/shard_map/all_to_all | solution.py:42
  80.8 2.2 %shard_map.92 = bf16[4,2,256,512]{3,2,1,0:T(8,128)(2,1)} custom-call(bf16[256,512]{1,0:T(8,128)(2,1)S(1)} %copy-done.2, bf16[512,128]{1,0:T(8,128)(2,1)S(1)} %bitcast.17, f32[256,512]{1,0:T(8,128)S(1)} %get-tuple-element.29.inner_ref, bf16[2,4,128,256]{3,2,1,0:T(8,128)(2,1)S(1)} %bitcast.13, bf16[2,4,128,256]{3,2,1,0:T(8,128)(2,1)S(1)} %bitcast.15), custom_call_target="tpu_custom_call" | custom-call | flops 570425344 | bytes 2097152 | tf_op jit(solution)/shard_map/pallas_call | solution.py:197
  83.0 0.0 reduce-scatter.2.cloned.1.call-update
  83.0 0.0 all-gather.5.cloned.1.call-done
  83.0 2.5 %shard_map.86 = (bf16[256,512]{1,0:T(8,128)(2,1)S(1)}, bf16[512,128]{1,0:T(8,128)(2,1)S(1)}) custom-call(bf16[2,4,128,256]{3,2,1,0:T(8,128)(2,1)S(1)} %bitcast.14, bf16[2,4,128,256]{3,2,1,0:T(8,128)(2,1)S(1)} %bitcast.16, bf16[4,2,256,512]{3,2,1,0:T(8,128)(2,1)} %bitcast.23, bf16[256,512]{1,0:T(8,128)(2,1)S(1)} %copy-done.2), custom_call_target="tpu_custom_call" | custom-call | flops 570425344 | bytes 2097152 | tf_op jit(solution)/shard_map/pallas_call | solution.py:210
  85.5 17.7 %all_to_all.31.got_ref = bf16[64,8,128]{2,1,0:T(8,128)(2,1)S(1)} all-to-all(bf16[64,8,128]{2,1,0:T(8,128)(2,1)S(1)} %bitcast.20), channel_id=1, replica_groups=mesh['y'=8,'z'=8,'x'=4,'c'=2] {'y','z'}, dimensions={0} | all-to-all | bytes 262144 | tf_op jit(solution)/shard_map/all_to_all | solution.py:42
  103.2 0.1 shard_map.90
  103.2 16.6 %all_to_all.32 = bf16[64,8,128]{2,1,0:T(8,128)(2,1)S(1)} all-to-all(bf16[64,8,128]{2,1,0:T(8,128)(2,1)S(1)} %shard_map.90), channel_id=1, replica_groups=mesh['y'=8,'z'=8,'x'=4,'c'=2] {'y','z'}, dimensions={0} | all-to-all | bytes 262144 | tf_op jit(solution)/shard_map/all_to_all | solution.py:42
  119.8 4.5 %reduce-scatter.2.cloned.1.call-done = bf16[256,512]{1,0:T(8,128)(2,1)} async-done(((bf16[2048,512]{1,0:T(8,128)(2,1)}), bf16[256,512]{1,0:T(8,128)(2,1)}) %reduce-scatter.2.cloned.1.call-update) | async-done | bytes 262160 | tf_op jit(solution)/shard_map/reduce_scatter | solution.py:208
  124.3 6.9 %all-to-all-start.5 = ((bf16[8,32,512]{2,1,0:T(8,128)(2,1)}), bf16[8,32,512]{2,1,0:T(8,128)(2,1)S(1)}, u32[]{:S(2)}, u32[]{:S(2)}) async-start(bf16[8,32,512]{2,1,0:T(8,128)(2,1)} %bitcast.25), calls=%async_computation.6 | async-start | bytes 524288 | tf_op jit(solution)/shard_map/all_to_all | solution.py:42
  131.1 1.9 %shard_map.89 = (bf16[256,512]{1,0:T(8,128)(2,1)}, f32[256,512]{1,0:T(8,128)S(1)}, f32[256,512]{1,0:T(8,128)S(1)}) custom-call(bf16[256,512]{1,0:T(8,128)(2,1)S(1)} %copy-done.2, bf16[256,512]{1,0:T(8,128)(2,1)S(1)} %copy-done, bf16[256,512]{1,0:T(8,128)(2,1)S(1)} %copy-done.1, bf16[256,512]{1,0:T(8,128)(2,1)S(1)} %get-tuple-element.20.g_ref, ...), custom_call_target="tpu_custom_call" | custom-call | flops 301989888 | bytes 2097152 | tf_op jit(solution)/shard_map/pallas_call | solution.py:222
  133.0 1.1 shard_map.91
  134.1 7.5 %all-to-all-done.5 = bf16[8,32,512]{2,1,0:T(8,128)(2,1)S(1)} async-done(((bf16[8,32,512]{2,1,0:T(8,128)(2,1)}), bf16[8,32,512]{2,1,0:T(8,128)(2,1)S(1)}, u32[]{:S(2)}, u32[]{:S(2)}) %all-to-all-start.5) | async-done | bytes 262176 | tf_op jit(solution)/shard_map/all_to_all | solution.py:42
  141.6 0.6 multiply_bitcast_fusion
  (2 shorter events, 0.1 us)
Async XLA Ops:
  7.2 33.2 %copy-start = (bf16[256,512]{1,0:T(8,128)(2,1)S(1)}, bf16[256,512]{1,0:T(8,128)(2,1)}, u32[]{:S(2)}) copy-start(bf16[256,512]{1,0:T(8,128)(2,1)} %k_ref.7) | copy-start | bytes 786436
  7.2 33.2 %copy-start.1 = (bf16[256,512]{1,0:T(8,128)(2,1)S(1)}, bf16[256,512]{1,0:T(8,128)(2,1)}, u32[]{:S(2)}) copy-start(bf16[256,512]{1,0:T(8,128)(2,1)} %v_ref.7) | copy-start | bytes 786436
  7.2 33.9 %copy-start.3 = (bf16[256,256]{1,0:T(8,128)(2,1)S(1)}, bf16[256,256]{1,0:T(8,128)(2,1)}, u32[]{:S(2)}) copy-start(bf16[256,256]{1,0:T(8,128)(2,1)} %param.8) | copy-start | bytes 393220
  7.2 33.2 %copy-start.2 = (bf16[256,512]{1,0:T(8,128)(2,1)S(1)}, bf16[256,512]{1,0:T(8,128)(2,1)}, u32[]{:S(2)}) copy-start(bf16[256,512]{1,0:T(8,128)(2,1)} %q_ref.7) | copy-start | bytes 786436
  7.2 75.8 %all-gather.5.cloned.1.call-start = ((), (), s32[]{:S(2)}) async-start(), calls=%async_computation.7 | async-start | bytes 2359296 | tf_op jit(solution)/shard_map/all_gather | solution.py:171
  32.2 24.6 %all-to-all-start.1 = ((bf16[64,16,128]{2,1,0:T(8,128)(2,1)}), bf16[64,16,128]{2,1,0:T(8,128)(2,1)S(1)}, u32[]{:S(2)}, u32[]{:S(2)}) async-start(bf16[64,16,128]{2,1,0:T(8,128)(2,1)} %shard_map.84), calls=%async_computation.1 | async-start | bytes 524288 | tf_op jit(solution)/shard_map/all_to_all | solution.py:42
  57.6 23.2 %all-to-all-start.2 = ((bf16[64,8,128]{2,1,0:T(8,128)(2,1)}), bf16[64,8,128]{2,1,0:T(8,128)(2,1)S(1)}, u32[]{:S(2)}, u32[]{:S(2)}) async-start(bf16[64,8,128]{2,1,0:T(8,128)(2,1)} %shard_map.88), calls=%async_computation.2 | async-start | bytes 262144 | tf_op jit(solution)/shard_map/all_to_all | solution.py:42
  67.8 56.5 %reduce-scatter.2.cloned.1.call-start = ((), (), s32[]{:S(2)}) async-start(), calls=%async_computation.8 | async-start | bytes 2359296 | tf_op jit(solution)/shard_map/reduce_scatter | solution.py:208
  124.3 17.3 %all-to-all-start.5 = ((bf16[8,32,512]{2,1,0:T(8,128)(2,1)}), bf16[8,32,512]{2,1,0:T(8,128)(2,1)S(1)}, u32[]{:S(2)}, u32[]{:S(2)}) async-start(bf16[8,32,512]{2,1,0:T(8,128)(2,1)} %bitcast.25), calls=%async_computation.6 | async-start | bytes 524288 | tf_op jit(solution)/shard_map/all_to_all | solution.py:42
Sparse Core Ops, SparseCore 0:
  30.4 44.8 all-gather.4
  83.1 41.1 reduce-scatter.1

commit v9 on v8

--- a/solution.py
+++ b/solution.py
@@ -48,26 +48,27 @@
 
 
 def kv_kernel(k_ref, v_ref, out_ref):
-    share = out_ref.shape[1] // 2
-    per_head = DH // share
     for h in range(k_ref.shape[1] // DH):
-        kv = mm(k_ref[:, head(h)], v_ref[:, head(h)], 0, 0)
-        high = kv.astype(BF16)
-        low = (kv - high.astype(F32)).astype(BF16)
-        for i in range(per_head):
-            piece = slice(i * share, (i + 1) * share)
-            out_ref[h * per_head + i, :share, :] = high[piece]
-            out_ref[h * per_head + i, share:, :] = low[piece]
-
-
-def prior_kernel(got_ref, sums_ref):
-    count, share, _ = sums_ref.shape
-    at = got_ref.shape[1] - 2 * share
-    running = jnp.zeros(sums_ref.shape[1:], F32)
-    for s in range(count):
-        sums_ref[s] = running.astype(BF16)
-        high = got_ref[s, at : at + share, :].astype(F32)
-        running = running + (high + got_ref[s, at + share :, :].astype(F32))
+        out_ref[:, head(h)] = mm(k_ref[:, head(h)], v_ref[:, head(h)], 0, 0)
+
+
+def part_kernel(got_ref, part_ref, total_ref):
+    running = jnp.zeros(got_ref.shape[1:], F32)
+    for p in range(got_ref.shape[0]):
+        part_ref[p] = running
+        running = running + got_ref[p]
+    for p in range(total_ref.shape[0]):
+        total_ref[p] = running
+
+
+def join_kernel(place_ref, totals_ref, part_ref, out_ref):
+    place = place_ref[0]
+    base = jnp.zeros(totals_ref.shape[1:], F32)
+    for other in range(totals_ref.shape[0]):
+        counts = place > other
+        base = base + jnp.where(counts, totals_ref[other], 0.0)
+    for p in range(part_ref.shape[0]):
+        out_ref[p] = (base + part_ref[p]).astype(out_ref.dtype)
 
 
 def later_kernel(got_ref, sums_ref):
@@ -90,7 +91,7 @@
     @pl.when(pl.program_id(0) == 0)
     def _():
         for h in range(q_ref.shape[1] // DH):
-            far = mm(q_ref[:, head(h)], prior_ref[head(h), :], 1, 0)
+            far = mm(q_ref[:, head(h)], prior_ref[:, head(h)], 1, 0)
             attn_out_ref[:, head(h)] = (scale * (inner_ref[:, head(h)] + far)).astype(BF16)
 
     for x in range(out_ref.shape[0]):
@@ -128,7 +129,7 @@
         g = g_ref[:, head(h)]
         back = jnp.where(mask, mm(g, v_ref[:, head(h)], 1, 1), 0.0).astype(BF16)
         near = mm(back, k_ref[:, head(h)], 1, 0)
-        far = mm(g, prior_ref[head(h), :], 1, 1)
+        far = mm(g, prior_ref[:, head(h)], 1, 1)
         dq_ref[:, head(h)] = (scale * (near + far)).astype(BF16)
         dk_ref[:, head(h)] = mm(back, q_ref[:, head(h)], 0, 0)
         dv_ref[:, head(h)] = mm(attn_ref[h], g, 0, 0)
@@ -151,6 +152,20 @@
     return pltpu.with_memory_space_constraint(x, pltpu.HBM)
 
 
+def join(place, totals, part):
+    return local_call(
+        join_kernel,
+        shape(part.shape, BF16),
+        0,
+        3 * part.size * 4,
+        in_specs=[
+            pl.BlockSpec(memory_space=pltpu.SMEM),
+            pl.BlockSpec(memory_space=pltpu.VMEM),
+            pl.BlockSpec(memory_space=pltpu.VMEM),
+        ],
+    )(place, totals, part)
+
+
 def per_device(queries, keys, values, out_cotangent, proj_weight):
     tok, width = queries.shape
     heads = width // DH
@@ -158,6 +173,7 @@
     nx, nc = lax.axis_size("x"), lax.axis_size("c")
     cols = out_cotangent.shape[1]
     scale = (DH * tok * ny * nz) ** -0.5
+    place = lax.axis_index("y").reshape(1)
     weight_t = proj_weight.T
     own = weight_t.shape[0]
     share = heads * DH // (ny * nz)
@@ -168,14 +184,20 @@
 
     spread = local_call(spread_kernel, shape((nz, own, width), BF16), 0, big)(in_hbm(weight_t))
     weight_z = exchange(spread, "z").reshape(nz * own, width)
+    kv = local_call(kv_kernel, shape((DH, width), F32), square, 3 * big)(
+        in_hbm(keys), in_hbm(values)
+    )
+    kv, cot_own, weight_z = lax.optimization_barrier((kv, out_cotangent, weight_z))
     weight_full = lax.all_gather(weight_z, "y", axis=0, tiled=True)
-    kv_pieces = local_call(
-        kv_kernel, shape((ny * nz, 2 * share, DH), BF16), square, 3 * big
-    )(in_hbm(keys), in_hbm(values))
-    kv_pieces, cot_own, weight_z = lax.optimization_barrier((kv_pieces, out_cotangent, weight_z))
-    got = exchange(kv_pieces, SEQ)
+    got = exchange(kv.reshape(nz, DH // nz, width), "z")
     cot_x = lax.all_gather(cot_own, "x")
     got, cot_x = lax.optimization_barrier((got, cot_x))
+    kv_part, kv_total = local_call(
+        part_kernel,
+        (shape(got.shape, F32), shape((ny,) + got.shape[1:], F32)),
+        0,
+        2 * big,
+    )(got)
     half = tok // 2
     cot_top = lax.all_gather(cot_x[:, :half], "c")
     cot_low = lax.all_gather(cot_x[:, half:], "c")
@@ -185,13 +207,12 @@
         2 * wide,
         10 * big,
     )(queries, keys, values)
-    sums = local_call(prior_kernel, shape(pieces, BF16), 0, 2 * big)(got)
-    prior = exchange(sums, SEQ).reshape(heads * DH, DH)
+    prior = exchange(join(place, exchange(kv_total, "y"), kv_part), "z").reshape(DH, width)
 
     n_blocks = nx * nc
 
     whole = pl.BlockSpec((tok, width), lambda i: (0, 0))
-    state = pl.BlockSpec((heads * DH, DH), lambda i: (0, 0))
+    state = pl.BlockSpec((DH, width), lambda i: (0, 0))
     cot_spec = pl.BlockSpec((1, nx, half, cols), lambda i: (i, 0, 0, 0))
     by_core = pl.BlockSpec((nx, 1, cols, width), lambda i: (0, i, 0, 0))
     proj_term = local_call(
@@ -214,7 +235,7 @@
         2 * n_blocks * cols * width,
         grid=(nc,),
         in_specs=[cot_spec, cot_spec, by_core, whole],
-        out_specs=[whole, state],
+        out_specs=[whole, pl.BlockSpec((heads * DH, DH), lambda i: (0, 0))],
         scratch_shapes=[pltpu.VMEM((tok, width), F32)],
     )(cot_top, cot_low, in_hbm(weight_full.reshape(nx, nc, cols, width)), queries)
     qg_got = exchange(qg.reshape(pieces), SEQ)

time: 150 us -> 155 us (1.033)
  blocking collectives: 74.1 us -> 51.5 us
  waiting for transfers between devices: 22.9 us -> 38 us
  starting transfers between devices: 25.2 us -> 35.6 us
    all_to_all x3 -> x2, blocking collectives: 56.3 us -> 34.4 us  [exchange(): return lax.all_to_all(x, axis, 0, 0, tiled=True)]
    all_to_all x3 -> x5, waiting for transfers between devices: 18.4 us -> 35 us  [exchange(): return lax.all_to_all(x, axis, 0, 0, tiled=True)]
    all_to_all x3 -> x5, starting transfers between devices: 25.2 us -> 35.5 us  [exchange(): return lax.all_to_all(x, axis, 0, 0, tiled=True)]
    pallas_call x2 -> x3, Pallas kernels: 2.73 us -> 3.44 us  [the longest x1 2 us: per_device(): local_call(kv_kernel, shape((DH, width), F32), square, 3 * big)]
  transfers between devices with their start and end apart: 5 -> 7, of which waited for: 4 -> 5; matrix products, arithmetic and copies ran while one was open for 0% -> 0% of each run, Pallas kernels for 7% -> 8%
where the time goes in v9:
time: 155 us; the launch traced here: 154 us
  blocking collectives  51.5 us (33%)
  waiting for transfers between devices  38 us (25%)
  starting transfers between devices  35.6 us (23%)
  between operations  14.1 us (9%)
  Pallas kernels  13.3 us (9%)
    all_to_all x5, starting transfers between devices, exchange(): return lax.all_to_all(x, axis, 0, 0, tiled=True)  35.5 us
    all_to_all x5, waiting for transfers between devices, exchange(): return lax.all_to_all(x, axis, 0, 0, tiled=True)  35 us
    all_to_all x2, blocking collectives, exchange(): return lax.all_to_all(x, axis, 0, 0, tiled=True)  34.4 us
    all_gather x1, blocking collectives, per_device(): cot_x = lax.all_gather(cot_own, 'x')  12.8 us
  transfers between devices with their start and end apart: 7, of which 5 were waited for; matrix products, arithmetic and copies ran while one was open for 0% of the time, Pallas kernels for 8%

profile of v9, /device:TPU:6, one launch (start us, length us, event | category | flops | bytes accessed | tf_op | source)
XLA Modules:
  0.0 154.0 jit_solution(376848406726412955)
XLA Ops:
  7.2 0.0 copy-start
  7.2 0.0 copy-start.1
  7.2 0.0 copy-start.4
  7.2 0.0 copy-start.2
  7.2 1.6 %shard_map.85 = bf16[8,32,512]{2,1,0:T(8,128)(2,1)} custom-call(bf16[32,512]{1,0:T(8,128)(2,1)} %bitcast.28), custom_call_target="tpu_custom_call" | custom-call | bytes 131072 | tf_op jit(solution)/shard_map/pallas_call | solution.py:185
  8.8 10.3 %all-to-all-start = ((bf16[8,32,512]{2,1,0:T(8,128)(2,1)}), bf16[8,32,512]{2,1,0:T(8,128)(2,1)S(1)}, u32[]{:S(2)}, u32[]{:S(2)}) async-start(bf16[8,32,512]{2,1,0:T(8,128)(2,1)} %shard_map.85), calls=%async_computation | async-start | bytes 524288 | tf_op jit(solution)/shard_map/all_to_all | solution.py:42
  19.1 0.0 all-gather.5.cloned.1.call-start
  19.1 2.0 %shard_map.84 = f32[128,512]{1,0:T(8,128)} custom-call(bf16[256,512]{1,0:T(8,128)(2,1)} %k_ref.7, bf16[256,512]{1,0:T(8,128)(2,1)} %v_ref.7), custom_call_target="tpu_custom_call" | custom-call | flops 33554432 | bytes 393216 | tf_op jit(solution)/shard_map/pallas_call | solution.py:187
  21.1 9.8 %all-to-all-done = bf16[8,32,512]{2,1,0:T(8,128)(2,1)S(1)} async-done(((bf16[8,32,512]{2,1,0:T(8,128)(2,1)}), bf16[8,32,512]{2,1,0:T(8,128)(2,1)S(1)}, u32[]{:S(2)}, u32[]{:S(2)}) %all-to-all-start) | async-done | bytes 262176 | tf_op jit(solution)/shard_map/all_to_all | solution.py:42
  31.0 0.0 copy-start.3
  31.0 0.7 copy-done.3
  31.7 0.0 all-gather.5.cloned.1.call-update
  31.7 3.4 %all-to-all-start.1 = ((f32[8,16,512]{2,1,0:T(8,128)}), f32[8,16,512]{2,1,0:T(8,128)S(1)}, u32[]{:S(2)}, u32[]{:S(2)}) async-start(f32[8,16,512]{2,1,0:T(8,128)} %bitcast.2), calls=%async_computation.1 | async-start | bytes 524288 | tf_op jit(solution)/shard_map/all_to_all | solution.py:42
  35.1 0.0 copy-done.4
  35.1 12.8 %all-gather = bf16[1024,256]{1,0:T(8,128)(2,1)S(1)} all-gather(bf16[256,256]{1,0:T(8,128)(2,1)S(1)} %copy-done.4), channel_id=2, replica_groups=mesh['y'=8,'z'=8,'x'=4,'c'=2] {'x'}, dimensions={0}, use_global_device_ids=true | all-gather | bytes 655360 | tf_op jit(solution)/shard_map/all_gather | solution.py:193
  47.9 0.0 all-to-all-done.1.got_ref
  47.9 0.7 shard_map.88
  48.7 7.1 %all-to-all-start.2 = ((f32[8,16,512]{2,1,0:T(8,128)}), f32[8,16,512]{2,1,0:T(8,128)S(1)}, u32[]{:S(2)}, u32[]{:S(2)}) async-start(f32[8,16,512]{2,1,0:T(8,128)} %get-tuple-element.27), calls=%async_computation.2 | async-start | bytes 524288 | tf_op jit(solution)/shard_map/all_to_all | solution.py:42
  55.8 0.0 copy-done
  55.8 0.0 copy-done.1
  55.8 0.0 copy-done.2
  55.8 0.7 shard_map.87
  56.5 13.0 %all-to-all-done.2.totals_ref = f32[8,16,512]{2,1,0:T(8,128)S(1)} async-done(((f32[8,16,512]{2,1,0:T(8,128)}), f32[8,16,512]{2,1,0:T(8,128)S(1)}, u32[]{:S(2)}, u32[]{:S(2)}) %all-to-all-start.2) | async-done | bytes 262176 | tf_op jit(solution)/shard_map/all_to_all | solution.py:42
  69.5 0.7 shard_map.89
  70.2 7.1 %all-to-all-start.3 = ((bf16[8,16,512]{2,1,0:T(8,128)(2,1)}), bf16[8,16,512]{2,1,0:T(8,128)(2,1)S(1)}, u32[]{:S(2)}, u32[]{:S(2)}) async-start(bf16[8,16,512]{2,1,0:T(8,128)(2,1)} %shard_map.89), calls=%async_computation.3 | async-start | bytes 262144 | tf_op jit(solution)/shard_map/all_to_all | solution.py:42
  77.3 0.0 reduce-scatter.2.cloned.1.call-start
  77.4 2.2 %all-gather.1 = bf16[8,128,256]{2,1,0:T(8,128)(2,1)S(1)} all-gather(bf16[4,128,256]{2,1,0:T(8,128)(2,1)S(1)} %get-tuple-element.37), channel_id=3, replica_groups=mesh['y'=8,'z'=8,'x'=4,'c'=2] {'c'}, dimensions={0}, use_global_device_ids=true | all-gather | bytes 786432 | tf_op jit(solution)/shard_map/all_gather | solution.py:202
  79.5 2.2 %all-gather.2 = bf16[8,128,256]{2,1,0:T(8,128)(2,1)S(1)} all-gather(bf16[4,128,256]{2,1,0:T(8,128)(2,1)S(1)} %get-tuple-element.36), channel_id=4, replica_groups=mesh['y'=8,'z'=8,'x'=4,'c'=2] {'c'}, dimensions={0}, use_global_device_ids=true | all-gather | bytes 786432 | tf_op jit(solution)/shard_map/all_gather | solution.py:203
  81.7 4.7 %all-to-all-done.3 = bf16[8,16,512]{2,1,0:T(8,128)(2,1)S(1)} async-done(((bf16[8,16,512]{2,1,0:T(8,128)(2,1)}), bf16[8,16,512]{2,1,0:T(8,128)(2,1)S(1)}, u32[]{:S(2)}, u32[]{:S(2)}) %all-to-all-start.3) | async-done | bytes 131104 | tf_op jit(solution)/shard_map/all_to_all | solution.py:42
  86.4 2.1 %shard_map.93 = bf16[4,2,256,512]{3,2,1,0:T(8,128)(2,1)} custom-call(bf16[256,512]{1,0:T(8,128)(2,1)S(1)} %copy-done.2, bf16[128,512]{1,0:T(8,128)(2,1)S(1)} %bitcast.19, f32[256,512]{1,0:T(8,128)S(1)} %get-tuple-element.35.inner_ref, bf16[2,4,128,256]{3,2,1,0:T(8,128)(2,1)S(1)} %bitcast.15, bf16[2,4,128,256]{3,2,1,0:T(8,128)(2,1)S(1)} %bitcast.17), custom_call_target="tpu_custom_call" | custom-call | flops 570425344 | bytes 2097152 | tf_op jit(solution)/shard_map/pallas_call | solution.py:218
  88.5 0.0 reduce-scatter.2.cloned.1.call-update
  88.5 0.0 all-gather.5.cloned.1.call-done
  88.6 2.5 %shard_map.86 = (bf16[256,512]{1,0:T(8,128)(2,1)S(1)}, bf16[512,128]{1,0:T(8,128)(2,1)S(1)}) custom-call(bf16[2,4,128,256]{3,2,1,0:T(8,128)(2,1)S(1)} %bitcast.16, bf16[2,4,128,256]{3,2,1,0:T(8,128)(2,1)S(1)} %bitcast.18, bf16[4,2,256,512]{3,2,1,0:T(8,128)(2,1)} %bitcast.25, bf16[256,512]{1,0:T(8,128)(2,1)S(1)} %copy-done.2), custom_call_target="tpu_custom_call" | custom-call | flops 570425344 | bytes 2097152 | tf_op jit(solution)/shard_map/pallas_call | solution.py:231
  91.1 17.7 %all_to_all.35.got_ref = bf16[64,8,128]{2,1,0:T(8,128)(2,1)S(1)} all-to-all(bf16[64,8,128]{2,1,0:T(8,128)(2,1)S(1)} %bitcast.22), channel_id=1, replica_groups=mesh['y'=8,'z'=8,'x'=4,'c'=2] {'y','z'}, dimensions={0} | all-to-all | bytes 262144 | tf_op jit(solution)/shard_map/all_to_all | solution.py:42
  108.8 0.1 shard_map.91
  108.8 16.6 %all_to_all.36 = bf16[64,8,128]{2,1,0:T(8,128)(2,1)S(1)} all-to-all(bf16[64,8,128]{2,1,0:T(8,128)(2,1)S(1)} %shard_map.91), channel_id=1, replica_groups=mesh['y'=8,'z'=8,'x'=4,'c'=2] {'y','z'}, dimensions={0} | all-to-all | bytes 262144 | tf_op jit(solution)/shard_map/all_to_all | solution.py:42
  125.5 3.0 %reduce-scatter.2.cloned.1.call-done = bf16[256,512]{1,0:T(8,128)(2,1)} async-done(((bf16[2048,512]{1,0:T(8,128)(2,1)}), bf16[256,512]{1,0:T(8,128)(2,1)}) %reduce-scatter.2.cloned.1.call-update) | async-done | bytes 262160 | tf_op jit(solution)/shard_map/reduce_scatter | solution.py:229
  128.5 7.6 %all-to-all-start.6 = ((bf16[8,32,512]{2,1,0:T(8,128)(2,1)}), bf16[8,32,512]{2,1,0:T(8,128)(2,1)S(1)}, u32[]{:S(2)}, u32[]{:S(2)}) async-start(bf16[8,32,512]{2,1,0:T(8,128)(2,1)} %bitcast.27), calls=%async_computation.7 | async-start | bytes 524288 | tf_op jit(solution)/shard_map/all_to_all | solution.py:42
  136.0 1.9 %shard_map.90 = (bf16[256,512]{1,0:T(8,128)(2,1)}, f32[256,512]{1,0:T(8,128)S(1)}, f32[256,512]{1,0:T(8,128)S(1)}) custom-call(bf16[256,512]{1,0:T(8,128)(2,1)S(1)} %copy-done.2, bf16[256,512]{1,0:T(8,128)(2,1)S(1)} %copy-done, bf16[256,512]{1,0:T(8,128)(2,1)S(1)} %copy-done.1, bf16[256,512]{1,0:T(8,128)(2,1)S(1)} %get-tuple-element.24.g_ref, ...), custom_call_target="tpu_custom_call" | custom-call | flops 301989888 | bytes 2097152 | tf_op jit(solution)/shard_map/pallas_call | solution.py:243
  138.0 1.1 shard_map.92
  139.0 7.5 %all-to-all-done.6 = bf16[8,32,512]{2,1,0:T(8,128)(2,1)S(1)} async-done(((bf16[8,32,512]{2,1,0:T(8,128)(2,1)}), bf16[8,32,512]{2,1,0:T(8,128)(2,1)S(1)}, u32[]{:S(2)}, u32[]{:S(2)}) %all-to-all-start.6) | async-done | bytes 262176 | tf_op jit(solution)/shard_map/all_to_all | solution.py:42
  146.6 0.6 multiply_bitcast_fusion
  (2 shorter events, 0.1 us)
Async XLA Ops:
  7.2 48.6 %copy-start = (bf16[256,512]{1,0:T(8,128)(2,1)S(1)}, bf16[256,512]{1,0:T(8,128)(2,1)}, u32[]{:S(2)}) copy-start(bf16[256,512]{1,0:T(8,128)(2,1)} %k_ref.7) | copy-start | bytes 786436
  7.2 48.6 %copy-start.1 = (bf16[256,512]{1,0:T(8,128)(2,1)S(1)}, bf16[256,512]{1,0:T(8,128)(2,1)}, u32[]{:S(2)}) copy-start(bf16[256,512]{1,0:T(8,128)(2,1)} %v_ref.7) | copy-start | bytes 786436
  7.2 27.9 %copy-start.4 = (bf16[256,256]{1,0:T(8,128)(2,1)S(1)}, bf16[256,256]{1,0:T(8,128)(2,1)}, u32[]{:S(2)}) copy-start(bf16[256,256]{1,0:T(8,128)(2,1)} %param.8) | copy-start | bytes 393220
  7.2 48.6 %copy-start.2 = (bf16[256,512]{1,0:T(8,128)(2,1)S(1)}, bf16[256,512]{1,0:T(8,128)(2,1)}, u32[]{:S(2)}) copy-start(bf16[256,512]{1,0:T(8,128)(2,1)} %q_ref.7) | copy-start | bytes 786436
  8.8 22.2 %all-to-all-start = ((bf16[8,32,512]{2,1,0:T(8,128)(2,1)}), bf16[8,32,512]{2,1,0:T(8,128)(2,1)S(1)}, u32[]{:S(2)}, u32[]{:S(2)}) async-start(bf16[8,32,512]{2,1,0:T(8,128)(2,1)} %shard_map.85), calls=%async_computation | async-start | bytes 524288 | tf_op jit(solution)/shard_map/all_to_all | solution.py:42
  19.1 69.5 %all-gather.5.cloned.1.call-start = ((), (), s32[]{:S(2)}) async-start(), calls=%async_computation.8 | async-start | bytes 2359296 | tf_op jit(solution)/shard_map/all_gather | solution.py:191
  31.0 0.7 copy-start.3
  31.7 16.2 %all-to-all-start.1 = ((f32[8,16,512]{2,1,0:T(8,128)}), f32[8,16,512]{2,1,0:T(8,128)S(1)}, u32[]{:S(2)}, u32[]{:S(2)}) async-start(f32[8,16,512]{2,1,0:T(8,128)} %bitcast.2), calls=%async_computation.1 | async-start | bytes 524288 | tf_op jit(solution)/shard_map/all_to_all | solution.py:42
  48.7 20.8 %all-to-all-start.2 = ((f32[8,16,512]{2,1,0:T(8,128)}), f32[8,16,512]{2,1,0:T(8,128)S(1)}, u32[]{:S(2)}, u32[]{:S(2)}) async-start(f32[8,16,512]{2,1,0:T(8,128)} %get-tuple-element.27), calls=%async_computation.2 | async-start | bytes 524288 | tf_op jit(solution)/shard_map/all_to_all | solution.py:42
  70.2 16.2 %all-to-all-start.3 = ((bf16[8,16,512]{2,1,0:T(8,128)(2,1)}), bf16[8,16,512]{2,1,0:T(8,128)(2,1)S(1)}, u32[]{:S(2)}, u32[]{:S(2)}) async-start(bf16[8,16,512]{2,1,0:T(8,128)(2,1)} %shard_map.89), calls=%async_computation.3 | async-start | bytes 262144 | tf_op jit(solution)/shard_map/all_to_all | solution.py:42
  77.3 51.2 %reduce-scatter.2.cloned.1.call-start = ((), (), s32[]{:S(2)}) async-start(), calls=%async_computation.9 | async-start | bytes 2359296 | tf_op jit(solution)/shard_map/reduce_scatter | solution.py:229
  128.5 18.0 %all-to-all-start.6 = ((bf16[8,32,512]{2,1,0:T(8,128)(2,1)}), bf16[8,32,512]{2,1,0:T(8,128)(2,1)S(1)}, u32[]{:S(2)}, u32[]{:S(2)}) async-start(bf16[8,32,512]{2,1,0:T(8,128)(2,1)} %bitcast.27), calls=%async_computation.7 | async-start | bytes 524288 | tf_op jit(solution)/shard_map/all_to_all | solution.py:42
Sparse Core Ops, SparseCore 0:
  31.8 43.0 all-gather.4
  88.7 39.7 reduce-scatter.1

commit v10 on v4

--- a/solution.py
+++ b/solution.py
@@ -11,7 +11,7 @@
 SEQ = ("y", "z")
 BF16 = jnp.bfloat16
 F32 = jnp.float32
-VMEM_BYTES = 48 * 1024 * 1024
+VMEM_BYTES = 24 * 1024 * 1024
 
 
 def mm(a, b, ca, cb):
@@ -71,21 +71,18 @@
         total_ref[p] = running
 
 
-def back_scan_kernel(got_ref, part_ref, total_ref):
-    peers, rows, width = got_ref.shape
-    running = jnp.zeros((rows, width), F32)
-    for p in reversed(range(peers)):
-        part_ref[p] = running
-        running = running + got_ref[p]
-    for p in range(total_ref.shape[0]):
-        total_ref[p] = running
-
-
-def join_kernel(reverse, place_ref, totals_ref, part_ref, out_ref):
+def later_kernel(got_ref, sums_ref):
+    running = jnp.zeros(sums_ref.shape[1:], F32)
+    for s in reversed(range(sums_ref.shape[0])):
+        sums_ref[s] = running.astype(BF16)
+        running = running + got_ref[s].astype(F32)
+
+
+def join_kernel(place_ref, totals_ref, part_ref, out_ref):
     place = place_ref[0]
     base = jnp.zeros(totals_ref.shape[1:], F32)
     for other in range(totals_ref.shape[0]):
-        counts = place < other if reverse else place > other
+        counts = place > other
         base = base + jnp.where(counts, totals_ref[other], 0.0)
     for p in range(part_ref.shape[0]):
         out_ref[p] = (base + part_ref[p]).astype(out_ref.dtype)
@@ -133,7 +130,7 @@
         g = acc_ref[...].astype(BF16)
         g_ref[...] = g
         for h in range(g.shape[1] // DH):
-            qg_ref[:, head(h)] = mm(q_ref[:, head(h)], g[:, head(h)], 0, 0)
+            qg_ref[head(h), :] = mm(q_ref[:, head(h)], g[:, head(h)], 0, 0).astype(BF16)
 
 
 def inner_grads_kernel(scale, q_ref, k_ref, v_ref, g_ref, attn_ref, prior_ref, dq_ref, dk_ref, dv_ref):
@@ -150,7 +147,7 @@
 
 def outer_grads_kernel(scale, k_ref, v_ref, later_ref, near_k_ref, near_v_ref, dk_ref, dv_ref):
     for h in range(k_ref.shape[1] // DH):
-        later = later_ref[:, head(h)]
+        later = later_ref[head(h), :]
         far_k = mm(v_ref[:, head(h)], later, 1, 1)
         dk_ref[:, head(h)] = (scale * (near_k_ref[:, head(h)] + far_k)).astype(BF16)
         far_v = mm(k_ref[:, head(h)], later, 1, 0)
@@ -165,9 +162,9 @@
     return pltpu.with_memory_space_constraint(x, pltpu.HBM)
 
 
-def join(place, totals, part, reverse):
+def join(place, totals, part):
     return local_call(
-        functools.partial(join_kernel, reverse),
+        join_kernel,
         shape(part.shape, BF16),
         0,
         3 * part.size * 4,
@@ -220,7 +217,7 @@
         2 * wide,
         10 * big,
     )(queries, keys, values)
-    prior = exchange(join(place, exchange(kv_total, "y"), kv_part, False), "z")
+    prior = exchange(join(place, exchange(kv_total, "y"), kv_part), "z")
     prior = prior.reshape(DH, width)
 
     n_blocks = nx * nc
@@ -244,29 +241,24 @@
 
     grad_out, qg = local_call(
         grad_out_kernel,
-        (shape((tok, width), BF16), shape((DH, width), F32)),
+        (shape((tok, width), BF16), shape((heads * DH, DH), BF16)),
         square + 2 * tok * cols * width * n_blocks,
         2 * n_blocks * cols * width,
         grid=(nc,),
         in_specs=[cot_spec, cot_spec, by_core, whole],
-        out_specs=[whole, state],
+        out_specs=[whole, pl.BlockSpec((heads * DH, DH), lambda i: (0, 0))],
         scratch_shapes=[pltpu.VMEM((tok, width), F32)],
     )(cot_top, cot_low, in_hbm(weight_full.reshape(nx, nc, cols, width)), queries)
-    qg_got = exchange(qg.reshape(nz, share, width), "z")
-    qg_part, qg_total = local_call(
-        back_scan_kernel,
-        (shape((nz, share, width), F32), shape((ny, share, width), F32)),
-        0,
-        2 * big,
-    )(qg_got)
+    pieces = (ny * nz, heads * DH // (ny * nz), DH)
+    qg_got = exchange(qg.reshape(pieces), SEQ)
+    sums = local_call(later_kernel, shape(pieces, BF16), 0, 2 * big)(qg_got)
     grad_q, near_k, near_v = local_call(
         functools.partial(inner_grads_kernel, scale),
         (shape((tok, width), BF16), shape((tok, width), F32), shape((tok, width), F32)),
         4 * wide + square,
         16 * big,
     )(queries, keys, values, grad_out, attn, prior)
-    later = exchange(join(place, exchange(qg_total, "y"), qg_part, True), "z")
-    later = later.reshape(DH, width)
+    later = exchange(sums, SEQ).reshape(heads * DH, DH)
     grad_k, grad_v = local_call(
         functools.partial(outer_grads_kernel, scale),
         (shape((tok, width), BF16), shape((tok, width), BF16)),

time: 152 us -> 151 us (level)
  blocking collectives: 89.8 us -> 84.1 us
  waiting for transfers between devices: 18.5 us -> 22.7 us
    all_to_all x4 -> x3, blocking collectives: 72.7 us -> 67 us  [exchange(): return lax.all_to_all(x, axis, 0, 0, tiled=True)]
    reduce_scatter x1, waiting for transfers between devices: 0.99 us -> 5.2 us  [per_device(): proj_y = lax.psum_scatter(proj_term, 'y', scatter_dimension=0, tiled=True)]
    pallas_call x4 -> x3, Pallas kernels: 3.24 us -> 3.24 us  [the longest x1 2.47 us: per_device(): local_call(grad_out_kernel, (shape((tok, width), BF16), shape((heads * DH...]
where the time goes in v10:
time: 151 us; the launch traced here: 150 us
  blocking collectives  84.1 us (56%)
  waiting for transfers between devices  22.7 us (15%)
  starting transfers between devices  17.3 us (11%)
  between operations  14.1 us (9%)
  Pallas kernels  11.2 us (7%)
    all_to_all x3, blocking collectives, exchange(): return lax.all_to_all(x, axis, 0, 0, tiled=True)  67 us
    all_to_all x3, starting transfers between devices, exchange(): return lax.all_to_all(x, axis, 0, 0, tiled=True)  17.2 us
    all_gather x1, blocking collectives, per_device(): cot_x = lax.all_gather(cot_own, 'x')  12.8 us
    all_to_all x3, waiting for transfers between devices, exchange(): return lax.all_to_all(x, axis, 0, 0, tiled=True)  12.1 us
    all_gather x1, waiting for transfers between devices, per_device(): weight_full = lax.all_gather(weight_z, 'y', axis=0, tiled=True)  5.38 us
    reduce_scatter x1, waiting for transfers between devices, per_device(): proj_y = lax.psum_scatter(proj_term, 'y', scatter_dimension=0, tiled=True)  5.2 us
  transfers between devices with their start and end apart: 5, of which 4 were waited for; matrix products, arithmetic and copies ran while one was open for 0% of the time, Pallas kernels for 6%

profile of v10, /device:TPU:6, one launch (start us, length us, event | category | flops | bytes accessed | tf_op | source)
XLA Modules:
  0.0 150.2 jit_solution(12304442074583023056)
XLA Ops:
  7.2 0.0 copy-start.1
  7.2 0.0 copy-start.2
  7.2 0.0 copy-start
  7.2 0.0 all-gather.5.cloned.1.call-start
  7.2 0.0 copy-start.3
  7.3 1.4 shard_map.84
  8.6 27.6 %all_to_all.30.got_ref = bf16[8,64,512]{2,1,0:T(8,128)(2,1)S(1)} all-to-all(bf16[8,64,512]{2,1,0:T(8,128)(2,1)S(1)} %shard_map.84), channel_id=1, replica_groups=mesh['y'=8,'z'=8,'x'=4,'c'=2] {'z'}, dimensions={0} | all-to-all | bytes 1048576 | tf_op jit(solution)/shard_map/all_to_all | solution.py:42
  36.2 0.8 shard_map.85
  37.1 0.0 all-gather.5.cloned.1.call-update
  37.1 7.1 %all-to-all-start.1 = ((f32[8,16,512]{2,1,0:T(8,128)}), f32[8,16,512]{2,1,0:T(8,128)S(1)}, u32[]{:S(2)}, u32[]{:S(2)}) async-start(f32[8,16,512]{2,1,0:T(8,128)} %get-tuple-element.23), calls=%async_computation.1 | async-start | bytes 524288 | tf_op jit(solution)/shard_map/all_to_all | solution.py:42
  44.2 0.0 copy-done.1
  44.2 0.0 copy-done.2
  44.2 0.0 copy-done
  44.2 0.7 shard_map.87
  44.9 0.0 copy-done.3
  44.9 12.8 %all-gather = bf16[1024,256]{1,0:T(8,128)(2,1)S(1)} all-gather(bf16[256,256]{1,0:T(8,128)(2,1)S(1)} %copy-done.3), channel_id=2, replica_groups=mesh['y'=8,'z'=8,'x'=4,'c'=2] {'x'}, dimensions={0}, use_global_device_ids=true | all-gather | bytes 655360 | tf_op jit(solution)/shard_map/all_gather | solution.py:210
  57.7 0.0 all-to-all-done.1.totals_ref
  57.7 0.7 shard_map.88
  58.4 3.4 %all-to-all-start.2 = ((bf16[8,16,512]{2,1,0:T(8,128)(2,1)}), bf16[8,16,512]{2,1,0:T(8,128)(2,1)S(1)}, u32[]{:S(2)}, u32[]{:S(2)}) async-start(bf16[8,16,512]{2,1,0:T(8,128)(2,1)} %shard_map.88), calls=%async_computation.2 | async-start | bytes 262144 | tf_op jit(solution)/shard_map/all_to_all | solution.py:42
  61.8 0.0 reduce-scatter.2.cloned.1.call-start
  61.9 2.2 %all-gather.1 = bf16[8,128,256]{2,1,0:T(8,128)(2,1)S(1)} all-gather(bf16[4,128,256]{2,1,0:T(8,128)(2,1)S(1)} %get-tuple-element.33), channel_id=3, replica_groups=mesh['y'=8,'z'=8,'x'=4,'c'=2] {'c'}, dimensions={0}, use_global_device_ids=true | all-gather | bytes 786432 | tf_op jit(solution)/shard_map/all_gather | solution.py:212
  64.0 2.2 %all-gather.2 = bf16[8,128,256]{2,1,0:T(8,128)(2,1)S(1)} all-gather(bf16[4,128,256]{2,1,0:T(8,128)(2,1)S(1)} %get-tuple-element.32), channel_id=4, replica_groups=mesh['y'=8,'z'=8,'x'=4,'c'=2] {'c'}, dimensions={0}, use_global_device_ids=true | all-gather | bytes 786432 | tf_op jit(solution)/shard_map/all_gather | solution.py:213
  66.2 4.6 %all-to-all-done.2 = bf16[8,16,512]{2,1,0:T(8,128)(2,1)S(1)} async-done(((bf16[8,16,512]{2,1,0:T(8,128)(2,1)}), bf16[8,16,512]{2,1,0:T(8,128)(2,1)S(1)}, u32[]{:S(2)}, u32[]{:S(2)}) %all-to-all-start.2) | async-done | bytes 131104 | tf_op jit(solution)/shard_map/all_to_all | solution.py:42
  70.8 2.2 %shard_map.92 = bf16[4,2,256,512]{3,2,1,0:T(8,128)(2,1)} custom-call(bf16[256,512]{1,0:T(8,128)(2,1)S(1)} %copy-done, bf16[128,512]{1,0:T(8,128)(2,1)S(1)} %bitcast.17, f32[256,512]{1,0:T(8,128)S(1)} %get-tuple-element.31.inner_ref, bf16[2,4,128,256]{3,2,1,0:T(8,128)(2,1)S(1)} %bitcast.13, bf16[2,4,128,256]{3,2,1,0:T(8,128)(2,1)S(1)} %bitcast.15), custom_call_target="tpu_custom_call" | custom-call | flops 570425344 | bytes 2097152 | tf_op jit(solution)/shard_map/pallas_call | solution.py:229
  73.0 0.0 reduce-scatter.2.cloned.1.call-update
  73.0 5.4 %all-gather.5.cloned.1.call-done = bf16[2048,512]{1,0:T(8,128)(2,1)} async-done(((bf16[256,512]{1,0:T(8,128)(2,1)}), bf16[2048,512]{1,0:T(8,128)(2,1)}) %all-gather.5.cloned.1.call-update) | async-done | bytes 2097168 | tf_op jit(solution)/shard_map/all_gather | solution.py:208
  78.4 2.5 %shard_map.86 = (bf16[256,512]{1,0:T(8,128)(2,1)S(1)}, bf16[512,128]{1,0:T(8,128)(2,1)S(1)}) custom-call(bf16[2,4,128,256]{3,2,1,0:T(8,128)(2,1)S(1)} %bitcast.14, bf16[2,4,128,256]{3,2,1,0:T(8,128)(2,1)S(1)} %bitcast.16, bf16[4,2,256,512]{3,2,1,0:T(8,128)(2,1)} %bitcast.23, bf16[256,512]{1,0:T(8,128)(2,1)S(1)} %copy-done), custom_call_target="tpu_custom_call" | custom-call | flops 570425344 | bytes 2097152 | tf_op jit(solution)/shard_map/pallas_call | solution.py:242
  80.9 22.1 %all_to_all.31.got_ref = bf16[64,8,128]{2,1,0:T(8,128)(2,1)S(1)} all-to-all(bf16[64,8,128]{2,1,0:T(8,128)(2,1)S(1)} %bitcast.20), channel_id=1, replica_groups=mesh['y'=8,'z'=8,'x'=4,'c'=2] {'y','z'}, dimensions={0} | all-to-all | bytes 262144 | tf_op jit(solution)/shard_map/all_to_all | solution.py:42
  103.0 0.1 shard_map.90
  103.1 17.2 %all_to_all.32 = bf16[64,8,128]{2,1,0:T(8,128)(2,1)S(1)} all-to-all(bf16[64,8,128]{2,1,0:T(8,128)(2,1)S(1)} %shard_map.90), channel_id=1, replica_groups=mesh['y'=8,'z'=8,'x'=4,'c'=2] {'y','z'}, dimensions={0} | all-to-all | bytes 262144 | tf_op jit(solution)/shard_map/all_to_all | solution.py:42
  120.3 5.2 %reduce-scatter.2.cloned.1.call-done = bf16[256,512]{1,0:T(8,128)(2,1)} async-done(((bf16[2048,512]{1,0:T(8,128)(2,1)}), bf16[256,512]{1,0:T(8,128)(2,1)}) %reduce-scatter.2.cloned.1.call-update) | async-done | bytes 262160 | tf_op jit(solution)/shard_map/reduce_scatter | solution.py:240
  125.5 6.7 %all-to-all-start.5 = ((bf16[8,32,512]{2,1,0:T(8,128)(2,1)}), bf16[8,32,512]{2,1,0:T(8,128)(2,1)S(1)}, u32[]{:S(2)}, u32[]{:S(2)}) async-start(bf16[8,32,512]{2,1,0:T(8,128)(2,1)} %bitcast.24), calls=%async_computation.6 | async-start | bytes 524288 | tf_op jit(solution)/shard_map/all_to_all | solution.py:42
  132.2 1.9 %shard_map.89 = (bf16[256,512]{1,0:T(8,128)(2,1)}, f32[256,512]{1,0:T(8,128)S(1)}, f32[256,512]{1,0:T(8,128)S(1)}) custom-call(bf16[256,512]{1,0:T(8,128)(2,1)S(1)} %copy-done, bf16[256,512]{1,0:T(8,128)(2,1)S(1)} %copy-done.1, bf16[256,512]{1,0:T(8,128)(2,1)S(1)} %copy-done.2, bf16[256,512]{1,0:T(8,128)(2,1)S(1)} %get-tuple-element.21.g_ref, ...), custom_call_target="tpu_custom_call" | custom-call | flops 301989888 | bytes 2097152 | tf_op jit(solution)/shard_map/pallas_call | solution.py:255
  134.1 1.1 shard_map.91
  135.2 7.5 %all-to-all-done.5 = bf16[8,32,512]{2,1,0:T(8,128)(2,1)S(1)} async-done(((bf16[8,32,512]{2,1,0:T(8,128)(2,1)}), bf16[8,32,512]{2,1,0:T(8,128)(2,1)S(1)}, u32[]{:S(2)}, u32[]{:S(2)}) %all-to-all-start.5) | async-done | bytes 262176 | tf_op jit(solution)/shard_map/all_to_all | solution.py:42
  142.7 0.6 multiply_bitcast_fusion
  (2 shorter events, 0.1 us)
Async XLA Ops:
  7.2 37.0 %copy-start.1 = (bf16[256,512]{1,0:T(8,128)(2,1)S(1)}, bf16[256,512]{1,0:T(8,128)(2,1)}, u32[]{:S(2)}) copy-start(bf16[256,512]{1,0:T(8,128)(2,1)} %k_ref.7) | copy-start | bytes 786436
  7.2 37.0 %copy-start.2 = (bf16[256,512]{1,0:T(8,128)(2,1)S(1)}, bf16[256,512]{1,0:T(8,128)(2,1)}, u32[]{:S(2)}) copy-start(bf16[256,512]{1,0:T(8,128)(2,1)} %v_ref.7) | copy-start | bytes 786436
  7.2 37.0 %copy-start = (bf16[256,512]{1,0:T(8,128)(2,1)S(1)}, bf16[256,512]{1,0:T(8,128)(2,1)}, u32[]{:S(2)}) copy-start(bf16[256,512]{1,0:T(8,128)(2,1)} %q_ref.7) | copy-start | bytes 786436
  7.2 71.2 %all-gather.5.cloned.1.call-start = ((), (), s32[]{:S(2)}) async-start(), calls=%async_computation.7 | async-start | bytes 2359296 | tf_op jit(solution)/shard_map/all_gather | solution.py:208
  7.2 37.6 %copy-start.3 = (bf16[256,256]{1,0:T(8,128)(2,1)S(1)}, bf16[256,256]{1,0:T(8,128)(2,1)}, u32[]{:S(2)}) copy-start(bf16[256,256]{1,0:T(8,128)(2,1)} %param.8) | copy-start | bytes 393220
  37.1 20.6 %all-to-all-start.1 = ((f32[8,16,512]{2,1,0:T(8,128)}), f32[8,16,512]{2,1,0:T(8,128)S(1)}, u32[]{:S(2)}, u32[]{:S(2)}) async-start(f32[8,16,512]{2,1,0:T(8,128)} %get-tuple-element.23), calls=%async_computation.1 | async-start | bytes 524288 | tf_op jit(solution)/shard_map/all_to_all | solution.py:42
  58.4 12.4 %all-to-all-start.2 = ((bf16[8,16,512]{2,1,0:T(8,128)(2,1)}), bf16[8,16,512]{2,1,0:T(8,128)(2,1)S(1)}, u32[]{:S(2)}, u32[]{:S(2)}) async-start(bf16[8,16,512]{2,1,0:T(8,128)(2,1)} %shard_map.88), calls=%async_computation.2 | async-start | bytes 262144 | tf_op jit(solution)/shard_map/all_to_all | solution.py:42
  61.8 63.7 %reduce-scatter.2.cloned.1.call-start = ((), (), s32[]{:S(2)}) async-start(), calls=%async_computation.8 | async-start | bytes 2359296 | tf_op jit(solution)/shard_map/reduce_scatter | solution.py:240
  125.5 17.2 %all-to-all-start.5 = ((bf16[8,32,512]{2,1,0:T(8,128)(2,1)}), bf16[8,32,512]{2,1,0:T(8,128)(2,1)S(1)}, u32[]{:S(2)}, u32[]{:S(2)}) async-start(bf16[8,32,512]{2,1,0:T(8,128)(2,1)} %bitcast.24), calls=%async_computation.6 | async-start | bytes 524288 | tf_op jit(solution)/shard_map/all_to_all | solution.py:42
Sparse Core Ops, SparseCore 0:
  37.2 41.1 all-gather.4
  81.2 44.2 reduce-scatter.1

commit v11 on v9

--- a/solution.py
+++ b/solution.py
@@ -88,7 +88,7 @@
 
 
 def proj_kernel(scale, q_ref, prior_ref, inner_ref, top_ref, low_ref, out_ref, attn_out_ref):
-    @pl.when(pl.program_id(0) == 0)
+    @pl.when((pl.program_id(0) == 0) & (pl.program_id(1) == 0))
     def _():
         for h in range(q_ref.shape[1] // DH):
             far = mm(q_ref[:, head(h)], prior_ref[:, head(h)], 1, 0)
@@ -102,9 +102,9 @@
 def grad_out_kernel(top_ref, low_ref, w_ref, q_ref, g_ref, qg_ref, acc_ref):
     step = pl.program_id(0)
     term = None
-    for x in range(w_ref.shape[0]):
+    for x in range(w_ref.shape[1]):
         cot = jnp.concatenate([top_ref[0, x], low_ref[0, x]], axis=0)
-        one = mm(cot, w_ref[x, 0], 1, 0)
+        one = mm(cot, w_ref[:, x, 0].reshape(cot.shape[1], w_ref.shape[4]), 1, 0)
         term = one if term is None else term + one
 
     @pl.when(step == 0)
@@ -182,13 +182,13 @@
     big = tok * width
     pieces = (ny * nz, share, DH)
 
-    spread = local_call(spread_kernel, shape((nz, own, width), BF16), 0, big)(in_hbm(weight_t))
-    weight_z = exchange(spread, "z").reshape(nz * own, width)
+    spread = local_call(spread_kernel, shape((ny, own, width), BF16), 0, big)(in_hbm(weight_t))
+    weight_y = exchange(spread, "y").reshape(ny * own, width)
     kv = local_call(kv_kernel, shape((DH, width), F32), square, 3 * big)(
         in_hbm(keys), in_hbm(values)
     )
-    kv, cot_own, weight_z = lax.optimization_barrier((kv, out_cotangent, weight_z))
-    weight_full = lax.all_gather(weight_z, "y", axis=0, tiled=True)
+    kv, cot_own, weight_y = lax.optimization_barrier((kv, out_cotangent, weight_y))
+    weight_full = lax.all_gather(weight_y, "z", axis=0, tiled=True)
     got = exchange(kv.reshape(nz, DH // nz, width), "z")
     cot_x = lax.all_gather(cot_own, "x")
     got, cot_x = lax.optimization_barrier((got, cot_x))
@@ -215,14 +215,23 @@
     state = pl.BlockSpec((DH, width), lambda i: (0, 0))
     cot_spec = pl.BlockSpec((1, nx, half, cols), lambda i: (i, 0, 0, 0))
     by_core = pl.BlockSpec((nx, 1, cols, width), lambda i: (0, i, 0, 0))
+    few = nx // 2
+    cot_few = pl.BlockSpec((1, few, half, cols), lambda i, j: (i, j, 0, 0))
+    same = pl.BlockSpec((tok, width), lambda i, j: (0, 0))
     proj_term = local_call(
         functools.partial(proj_kernel, scale),
         pltpu.HBM((nx, nc, cols, width), BF16),
         square + 2 * tok * cols * width * n_blocks,
         2 * n_blocks * cols * width,
-        grid=(nc,),
-        in_specs=[whole, state, whole, cot_spec, cot_spec],
-        out_specs=by_core,
+        grid=(nc, nx // few),
+        in_specs=[
+            same,
+            pl.BlockSpec((DH, width), lambda i, j: (0, 0)),
+            same,
+            cot_few,
+            cot_few,
+        ],
+        out_specs=pl.BlockSpec((few, 1, cols, width), lambda i, j: (j, i, 0, 0)),
         scratch_shapes=[pltpu.VMEM((tok, width), BF16)],
     )(queries, prior, attn_inner, cot_top, cot_low)
     proj_term = proj_term.reshape(n_blocks * cols, width)
@@ -234,10 +243,15 @@
         square + 2 * tok * cols * width * n_blocks,
         2 * n_blocks * cols * width,
         grid=(nc,),
-        in_specs=[cot_spec, cot_spec, by_core, whole],
+        in_specs=[
+            cot_spec,
+            cot_spec,
+            pl.BlockSpec((nz, nx, 1, own, width), lambda i: (0, 0, i, 0, 0)),
+            whole,
+        ],
         out_specs=[whole, pl.BlockSpec((heads * DH, DH), lambda i: (0, 0))],
         scratch_shapes=[pltpu.VMEM((tok, width), F32)],
-    )(cot_top, cot_low, in_hbm(weight_full.reshape(nx, nc, cols, width)), queries)
+    )(cot_top, cot_low, in_hbm(weight_full.reshape(nz, nx, nc, own, width)), queries)
     qg_got = exchange(qg.reshape(pieces), SEQ)
     sums = local_call(later_kernel, shape(pieces, BF16), 0, 2 * big)(qg_got)
     grad_q, near_k, near_v = local_call(

time: 155 us -> 154 us (level)
  waiting for transfers between devices: 38 us -> 34.6 us
    all_to_all x5, waiting for transfers between devices: 35 us -> 31.7 us  [exchange(): return lax.all_to_all(x, axis, 0, 0, tiled=True)]
where the time goes in v11:
time: 154 us; the launch traced here: 153 us
  blocking collectives  51.6 us (34%)
  starting transfers between devices  35.6 us (23%)
  waiting for transfers between devices  34.6 us (22%)
  between operations  15.6 us (10%)
  Pallas kernels  14 us (9%)
    all_to_all x5, starting transfers between devices, exchange(): return lax.all_to_all(x, axis, 0, 0, tiled=True)  35.5 us
    all_to_all x2, blocking collectives, exchange(): return lax.all_to_all(x, axis, 0, 0, tiled=True)  34.4 us
    all_to_all x5, waiting for transfers between devices, exchange(): return lax.all_to_all(x, axis, 0, 0, tiled=True)  31.7 us
    all_gather x1, blocking collectives, per_device(): cot_x = lax.all_gather(cot_own, 'x')  12.8 us
  transfers between devices with their start and end apart: 7, of which 5 were waited for; matrix products, arithmetic and copies ran while one was open for 0% of the time, Pallas kernels for 8%

profile of v11, /device:TPU:6, one launch (start us, length us, event | category | flops | bytes accessed | tf_op | source)
XLA Modules:
  0.0 152.7 jit_solution(5272916385311671122)
XLA Ops:
  8.0 0.0 copy-start
  8.0 0.0 copy-start.1
  8.0 0.0 copy-start.4
  8.0 0.0 copy-start.2
  8.0 1.6 %shard_map.85 = bf16[8,32,512]{2,1,0:T(8,128)(2,1)} custom-call(bf16[32,512]{1,0:T(8,128)(2,1)} %bitcast.28), custom_call_target="tpu_custom_call" | custom-call | bytes 131072 | tf_op jit(solution)/shard_map/pallas_call | solution.py:185
  9.6 7.1 %all-to-all-start = ((bf16[8,32,512]{2,1,0:T(8,128)(2,1)}), bf16[8,32,512]{2,1,0:T(8,128)(2,1)S(1)}, u32[]{:S(2)}, u32[]{:S(2)}) async-start(bf16[8,32,512]{2,1,0:T(8,128)(2,1)} %shard_map.85), calls=%async_computation | async-start | bytes 524288 | tf_op jit(solution)/shard_map/all_to_all | solution.py:42
  16.7 0.0 all-gather.5.cloned.1.call-start
  16.8 2.0 %shard_map.84 = f32[128,512]{1,0:T(8,128)} custom-call(bf16[256,512]{1,0:T(8,128)(2,1)} %k_ref.7, bf16[256,512]{1,0:T(8,128)(2,1)} %v_ref.7), custom_call_target="tpu_custom_call" | custom-call | flops 33554432 | bytes 393216 | tf_op jit(solution)/shard_map/pallas_call | solution.py:187
  18.8 9.8 %all-to-all-done = bf16[8,32,512]{2,1,0:T(8,128)(2,1)S(1)} async-done(((bf16[8,32,512]{2,1,0:T(8,128)(2,1)}), bf16[8,32,512]{2,1,0:T(8,128)(2,1)S(1)}, u32[]{:S(2)}, u32[]{:S(2)}) %all-to-all-start) | async-done | bytes 262176 | tf_op jit(solution)/shard_map/all_to_all | solution.py:42
  28.6 0.0 copy-start.3
  28.6 0.7 copy-done.3
  29.3 0.0 all-gather.5.cloned.1.call-update
  29.3 10.3 %all-to-all-start.1 = ((f32[8,16,512]{2,1,0:T(8,128)}), f32[8,16,512]{2,1,0:T(8,128)S(1)}, u32[]{:S(2)}, u32[]{:S(2)}) async-start(f32[8,16,512]{2,1,0:T(8,128)} %bitcast.2), calls=%async_computation.1 | async-start | bytes 524288 | tf_op jit(solution)/shard_map/all_to_all | solution.py:42
  39.6 0.0 copy-done.4
  39.6 12.8 %all-gather = bf16[1024,256]{1,0:T(8,128)(2,1)S(1)} all-gather(bf16[256,256]{1,0:T(8,128)(2,1)S(1)} %copy-done.4), channel_id=2, replica_groups=mesh['y'=8,'z'=8,'x'=4,'c'=2] {'x'}, dimensions={0}, use_global_device_ids=true | all-gather | bytes 655360 | tf_op jit(solution)/shard_map/all_gather | solution.py:193
  52.4 0.0 all-to-all-done.1.got_ref
  52.4 0.7 shard_map.88
  53.2 3.4 %all-to-all-start.2 = ((f32[8,16,512]{2,1,0:T(8,128)}), f32[8,16,512]{2,1,0:T(8,128)S(1)}, u32[]{:S(2)}, u32[]{:S(2)}) async-start(f32[8,16,512]{2,1,0:T(8,128)} %get-tuple-element.27), calls=%async_computation.2 | async-start | bytes 524288 | tf_op jit(solution)/shard_map/all_to_all | solution.py:42
  56.6 0.0 copy-done
  56.6 0.0 copy-done.1
  56.6 0.0 copy-done.2
  56.6 0.7 shard_map.87
  57.3 9.6 %all-to-all-done.2.totals_ref = f32[8,16,512]{2,1,0:T(8,128)S(1)} async-done(((f32[8,16,512]{2,1,0:T(8,128)}), f32[8,16,512]{2,1,0:T(8,128)S(1)}, u32[]{:S(2)}, u32[]{:S(2)}) %all-to-all-start.2) | async-done | bytes 262176 | tf_op jit(solution)/shard_map/all_to_all | solution.py:42
  67.0 0.7 shard_map.89
  67.7 7.2 %all-to-all-start.3 = ((bf16[8,16,512]{2,1,0:T(8,128)(2,1)}), bf16[8,16,512]{2,1,0:T(8,128)(2,1)S(1)}, u32[]{:S(2)}, u32[]{:S(2)}) async-start(bf16[8,16,512]{2,1,0:T(8,128)(2,1)} %shard_map.89), calls=%async_computation.3 | async-start | bytes 262144 | tf_op jit(solution)/shard_map/all_to_all | solution.py:42
  74.9 0.0 reduce-scatter.2.cloned.1.call-start
  74.9 2.2 %all-gather.1 = bf16[8,128,256]{2,1,0:T(8,128)(2,1)S(1)} all-gather(bf16[4,128,256]{2,1,0:T(8,128)(2,1)S(1)} %get-tuple-element.37), channel_id=3, replica_groups=mesh['y'=8,'z'=8,'x'=4,'c'=2] {'c'}, dimensions={0}, use_global_device_ids=true | all-gather | bytes 786432 | tf_op jit(solution)/shard_map/all_gather | solution.py:202
  77.1 2.2 %all-gather.2 = bf16[8,128,256]{2,1,0:T(8,128)(2,1)S(1)} all-gather(bf16[4,128,256]{2,1,0:T(8,128)(2,1)S(1)} %get-tuple-element.36), channel_id=4, replica_groups=mesh['y'=8,'z'=8,'x'=4,'c'=2] {'c'}, dimensions={0}, use_global_device_ids=true | all-gather | bytes 786432 | tf_op jit(solution)/shard_map/all_gather | solution.py:203
  79.3 4.7 %all-to-all-done.3 = bf16[8,16,512]{2,1,0:T(8,128)(2,1)S(1)} async-done(((bf16[8,16,512]{2,1,0:T(8,128)(2,1)}), bf16[8,16,512]{2,1,0:T(8,128)(2,1)S(1)}, u32[]{:S(2)}, u32[]{:S(2)}) %all-to-all-start.3) | async-done | bytes 131104 | tf_op jit(solution)/shard_map/all_to_all | solution.py:42
  84.0 2.8 %shard_map.93 = bf16[4,2,256,512]{3,2,1,0:T(8,128)(2,1)} custom-call(bf16[256,512]{1,0:T(8,128)(2,1)S(1)} %copy-done.2, bf16[128,512]{1,0:T(8,128)(2,1)S(1)} %bitcast.19, f32[256,512]{1,0:T(8,128)S(1)} %get-tuple-element.35.inner_ref, bf16[2,4,128,256]{3,2,1,0:T(8,128)(2,1)S(1)} %bitcast.15, bf16[2,4,128,256]{3,2,1,0:T(8,128)(2,1)S(1)} %bitcast.17), custom_call_target="tpu_custom_call" | custom-call | flops 570425344 | bytes 2097152 | tf_op jit(solution)/shard_map/pallas_call | solution.py:221
  86.8 0.0 reduce-scatter.2.cloned.1.call-update
  86.8 0.0 all-gather.5.cloned.1.call-done
  86.8 2.5 %shard_map.86 = (bf16[256,512]{1,0:T(8,128)(2,1)S(1)}, bf16[512,128]{1,0:T(8,128)(2,1)S(1)}) custom-call(bf16[2,4,128,256]{3,2,1,0:T(8,128)(2,1)S(1)} %bitcast.16, bf16[2,4,128,256]{3,2,1,0:T(8,128)(2,1)S(1)} %bitcast.18, bf16[8,4,2,32,512]{4,3,2,1,0:T(8,128)(2,1)} %bitcast.25, bf16[256,512]{1,0:T(8,128)(2,1)S(1)} %copy-done.2), custom_call_target="tpu_custom_call" | custom-call | flops 570425344 | bytes 2097152 | tf_op jit(solution)/shard_map/pallas_call | solution.py:240
  89.3 17.8 %all_to_all.35.got_ref = bf16[64,8,128]{2,1,0:T(8,128)(2,1)S(1)} all-to-all(bf16[64,8,128]{2,1,0:T(8,128)(2,1)S(1)} %bitcast.22), channel_id=1, replica_groups=mesh['y'=8,'z'=8,'x'=4,'c'=2] {'y','z'}, dimensions={0} | all-to-all | bytes 262144 | tf_op jit(solution)/shard_map/all_to_all | solution.py:42
  107.1 0.1 shard_map.91
  107.1 16.7 %all_to_all.36 = bf16[64,8,128]{2,1,0:T(8,128)(2,1)S(1)} all-to-all(bf16[64,8,128]{2,1,0:T(8,128)(2,1)S(1)} %shard_map.91), channel_id=1, replica_groups=mesh['y'=8,'z'=8,'x'=4,'c'=2] {'y','z'}, dimensions={0} | all-to-all | bytes 262144 | tf_op jit(solution)/shard_map/all_to_all | solution.py:42
  123.8 2.9 %reduce-scatter.2.cloned.1.call-done = bf16[256,512]{1,0:T(8,128)(2,1)} async-done(((bf16[2048,512]{1,0:T(8,128)(2,1)}), bf16[256,512]{1,0:T(8,128)(2,1)}) %reduce-scatter.2.cloned.1.call-update) | async-done | bytes 262160 | tf_op jit(solution)/shard_map/reduce_scatter | solution.py:238
  126.7 7.5 %all-to-all-start.6 = ((bf16[8,32,512]{2,1,0:T(8,128)(2,1)}), bf16[8,32,512]{2,1,0:T(8,128)(2,1)S(1)}, u32[]{:S(2)}, u32[]{:S(2)}) async-start(bf16[8,32,512]{2,1,0:T(8,128)(2,1)} %bitcast.27), calls=%async_computation.7 | async-start | bytes 524288 | tf_op jit(solution)/shard_map/all_to_all | solution.py:42
  134.1 1.9 %shard_map.90 = (bf16[256,512]{1,0:T(8,128)(2,1)}, f32[256,512]{1,0:T(8,128)S(1)}, f32[256,512]{1,0:T(8,128)S(1)}) custom-call(bf16[256,512]{1,0:T(8,128)(2,1)S(1)} %copy-done.2, bf16[256,512]{1,0:T(8,128)(2,1)S(1)} %copy-done, bf16[256,512]{1,0:T(8,128)(2,1)S(1)} %copy-done.1, bf16[256,512]{1,0:T(8,128)(2,1)S(1)} %get-tuple-element.24.g_ref, ...), custom_call_target="tpu_custom_call" | custom-call | flops 301989888 | bytes 2097152 | tf_op jit(solution)/shard_map/pallas_call | solution.py:257
  136.0 1.1 shard_map.92
  137.1 7.5 %all-to-all-done.6 = bf16[8,32,512]{2,1,0:T(8,128)(2,1)S(1)} async-done(((bf16[8,32,512]{2,1,0:T(8,128)(2,1)}), bf16[8,32,512]{2,1,0:T(8,128)(2,1)S(1)}, u32[]{:S(2)}, u32[]{:S(2)}) %all-to-all-start.6) | async-done | bytes 262176 | tf_op jit(solution)/shard_map/all_to_all | solution.py:42
  144.6 0.6 multiply_bitcast_fusion
  (2 shorter events, 0.1 us)
Async XLA Ops:
  8.0 48.6 %copy-start = (bf16[256,512]{1,0:T(8,128)(2,1)S(1)}, bf16[256,512]{1,0:T(8,128)(2,1)}, u32[]{:S(2)}) copy-start(bf16[256,512]{1,0:T(8,128)(2,1)} %k_ref.7) | copy-start | bytes 786436
  8.0 48.6 %copy-start.1 = (bf16[256,512]{1,0:T(8,128)(2,1)S(1)}, bf16[256,512]{1,0:T(8,128)(2,1)}, u32[]{:S(2)}) copy-start(bf16[256,512]{1,0:T(8,128)(2,1)} %v_ref.7) | copy-start | bytes 786436
  8.0 31.6 %copy-start.4 = (bf16[256,256]{1,0:T(8,128)(2,1)S(1)}, bf16[256,256]{1,0:T(8,128)(2,1)}, u32[]{:S(2)}) copy-start(bf16[256,256]{1,0:T(8,128)(2,1)} %param.8) | copy-start | bytes 393220
  8.0 48.6 %copy-start.2 = (bf16[256,512]{1,0:T(8,128)(2,1)S(1)}, bf16[256,512]{1,0:T(8,128)(2,1)}, u32[]{:S(2)}) copy-start(bf16[256,512]{1,0:T(8,128)(2,1)} %q_ref.7) | copy-start | bytes 786436
  9.6 19.0 %all-to-all-start = ((bf16[8,32,512]{2,1,0:T(8,128)(2,1)}), bf16[8,32,512]{2,1,0:T(8,128)(2,1)S(1)}, u32[]{:S(2)}, u32[]{:S(2)}) async-start(bf16[8,32,512]{2,1,0:T(8,128)(2,1)} %shard_map.85), calls=%async_computation | async-start | bytes 524288 | tf_op jit(solution)/shard_map/all_to_all | solution.py:42
  16.7 70.1 %all-gather.5.cloned.1.call-start = ((), (), s32[]{:S(2)}) async-start(), calls=%async_computation.8 | async-start | bytes 2359296 | tf_op jit(solution)/shard_map/all_gather | solution.py:191
  28.6 0.7 copy-start.3
  29.3 23.1 %all-to-all-start.1 = ((f32[8,16,512]{2,1,0:T(8,128)}), f32[8,16,512]{2,1,0:T(8,128)S(1)}, u32[]{:S(2)}, u32[]{:S(2)}) async-start(f32[8,16,512]{2,1,0:T(8,128)} %bitcast.2), calls=%async_computation.1 | async-start | bytes 524288 | tf_op jit(solution)/shard_map/all_to_all | solution.py:42
  53.2 13.8 %all-to-all-start.2 = ((f32[8,16,512]{2,1,0:T(8,128)}), f32[8,16,512]{2,1,0:T(8,128)S(1)}, u32[]{:S(2)}, u32[]{:S(2)}) async-start(f32[8,16,512]{2,1,0:T(8,128)} %get-tuple-element.27), calls=%async_computation.2 | async-start | bytes 524288 | tf_op jit(solution)/shard_map/all_to_all | solution.py:42
  67.7 16.3 %all-to-all-start.3 = ((bf16[8,16,512]{2,1,0:T(8,128)(2,1)}), bf16[8,16,512]{2,1,0:T(8,128)(2,1)S(1)}, u32[]{:S(2)}, u32[]{:S(2)}) async-start(bf16[8,16,512]{2,1,0:T(8,128)(2,1)} %shard_map.89), calls=%async_computation.3 | async-start | bytes 262144 | tf_op jit(solution)/shard_map/all_to_all | solution.py:42
  74.9 51.8 %reduce-scatter.2.cloned.1.call-start = ((), (), s32[]{:S(2)}) async-start(), calls=%async_computation.9 | async-start | bytes 2359296 | tf_op jit(solution)/shard_map/reduce_scatter | solution.py:238
  126.7 17.9 %all-to-all-start.6 = ((bf16[8,32,512]{2,1,0:T(8,128)(2,1)}), bf16[8,32,512]{2,1,0:T(8,128)(2,1)S(1)}, u32[]{:S(2)}, u32[]{:S(2)}) async-start(bf16[8,32,512]{2,1,0:T(8,128)(2,1)} %bitcast.27), calls=%async_computation.7 | async-start | bytes 524288 | tf_op jit(solution)/shard_map/all_to_all | solution.py:42
Sparse Core Ops, SparseCore 0:
  29.4 44.2 all-gather.4
Sparse Core Ops, SparseCore 1:
  86.9 39.8 reduce-scatter.1

commit v12 on v10

--- a/solution.py
+++ b/solution.py
@@ -98,15 +98,16 @@
 
 
 def proj_kernel(scale, q_ref, prior_ref, inner_ref, top_ref, low_ref, out_ref, attn_out_ref):
-    @pl.when(pl.program_id(0) == 0)
+    @pl.when((pl.program_id(0) == 0) & (pl.program_id(1) == 0))
     def _():
         for h in range(q_ref.shape[1] // DH):
             far = mm(q_ref[:, head(h)], prior_ref[:, head(h)], 1, 0)
             attn_out_ref[:, head(h)] = (scale * (inner_ref[:, head(h)] + far)).astype(BF16)
 
-    for x in range(out_ref.shape[0]):
+    for x in range(out_ref.shape[1]):
         cot = jnp.concatenate([top_ref[0, x], low_ref[0, x]], axis=0)
-        out_ref[x, 0] = mm(cot, attn_out_ref[...], 0, 0).astype(BF16)
+        term = mm(cot, attn_out_ref[...], 0, 0).astype(BF16)
+        out_ref[:, x, 0] = term.reshape(out_ref.shape[0], out_ref.shape[3], out_ref.shape[4])
 
 
 def grad_out_kernel(top_ref, low_ref, w_ref, q_ref, g_ref, qg_ref, acc_ref):
@@ -226,18 +227,27 @@
     state = pl.BlockSpec((DH, width), lambda i: (0, 0))
     cot_spec = pl.BlockSpec((1, nx, half, cols), lambda i: (i, 0, 0, 0))
     by_core = pl.BlockSpec((nx, 1, cols, width), lambda i: (0, i, 0, 0))
+    few = nx // 2
+    cot_few = pl.BlockSpec((1, few, half, cols), lambda i, j: (i, j, 0, 0))
+    same = pl.BlockSpec((tok, width), lambda i, j: (0, 0))
     proj_term = local_call(
         functools.partial(proj_kernel, scale),
-        pltpu.HBM((nx, nc, cols, width), BF16),
+        pltpu.HBM((nz, nx, nc, own, width), BF16),
         square + 2 * tok * cols * width * n_blocks,
         2 * n_blocks * cols * width,
-        grid=(nc,),
-        in_specs=[whole, state, whole, cot_spec, cot_spec],
-        out_specs=by_core,
+        grid=(nc, nx // few),
+        in_specs=[
+            same,
+            pl.BlockSpec((DH, width), lambda i, j: (0, 0)),
+            same,
+            cot_few,
+            cot_few,
+        ],
+        out_specs=pl.BlockSpec((nz, few, 1, own, width), lambda i, j: (0, j, i, 0, 0)),
         scratch_shapes=[pltpu.VMEM((tok, width), BF16)],
     )(queries, prior, attn_inner, cot_top, cot_low)
     proj_term = proj_term.reshape(n_blocks * cols, width)
-    proj_y = lax.psum_scatter(proj_term, "y", scatter_dimension=0, tiled=True)
+    proj_z = lax.psum_scatter(proj_term, "z", scatter_dimension=0, tiled=True)
 
     grad_out, qg = local_call(
         grad_out_kernel,
@@ -266,7 +276,7 @@
         12 * big,
     )(keys, values, later, near_k, near_v)
 
-    proj_parts = exchange(proj_y.reshape(nz, own, width), "z")
+    proj_parts = exchange(proj_z.reshape(ny, own, width), "y")
     proj_sum = jnp.sum(proj_parts.astype(F32), axis=0)
     grad_proj = (proj_sum / jnp.sqrt(F32(tok * ny * nz))).T
     return grad_q, grad_k, grad_v, grad_proj

time: 151 us -> 146 us (0.967)
  waiting for transfers between devices: 22.7 us -> 16.8 us
    reduce_scatter x1, waiting for transfers between devices: 5.2 us -> 0.01 us  [per_device(): proj_z = lax.psum_scatter(proj_term, 'z', scatter_dimension=0, tiled=True)]
  transfers between devices with their start and end apart: 5 -> 5, of which waited for: 4 -> 3; matrix products, arithmetic and copies ran while one was open for 0% -> 0% of each run, Pallas kernels for 6% -> 7%
where the time goes in v12:
time: 146 us; the launch traced here: 145 us
  blocking collectives  83.4 us (57%)
  waiting for transfers between devices  16.8 us (12%)
  starting transfers between devices  16.6 us (11%)
  between operations  15.6 us (11%)
  Pallas kernels  12 us (8%)
    all_to_all x3, blocking collectives, exchange(): return lax.all_to_all(x, axis, 0, 0, tiled=True)  66.3 us
    all_to_all x3, starting transfers between devices, exchange(): return lax.all_to_all(x, axis, 0, 0, tiled=True)  16.6 us
    all_gather x1, blocking collectives, per_device(): cot_x = lax.all_gather(cot_own, 'x')  12.8 us
    all_to_all x3, waiting for transfers between devices, exchange(): return lax.all_to_all(x, axis, 0, 0, tiled=True)  12.1 us
    all_gather x1, waiting for transfers between devices, per_device(): weight_full = lax.all_gather(weight_z, 'y', axis=0, tiled=True)  4.67 us
  transfers between devices with their start and end apart: 5, of which 3 were waited for; matrix products, arithmetic and copies ran while one was open for 0% of the time, Pallas kernels for 7%

profile of v12, /device:TPU:6, one launch (start us, length us, event | category | flops | bytes accessed | tf_op | source)
XLA Modules:
  0.0 145.1 jit_solution(16842531020018883618)
XLA Ops:
  8.0 0.0 copy-start.1
  8.0 0.0 copy-start.2
  8.0 0.0 copy-start
  8.0 0.0 all-gather.5.cloned.1.call-start
  8.1 0.0 copy-start.3
  8.1 1.4 shard_map.84
  9.5 27.6 %all_to_all.30.got_ref = bf16[8,64,512]{2,1,0:T(8,128)(2,1)S(1)} all-to-all(bf16[8,64,512]{2,1,0:T(8,128)(2,1)S(1)} %shard_map.84), channel_id=1, replica_groups=mesh['y'=8,'z'=8,'x'=4,'c'=2] {'z'}, dimensions={0} | all-to-all | bytes 1048576 | tf_op jit(solution)/shard_map/all_to_all | solution.py:42
  37.1 0.8 shard_map.85
  37.9 0.0 all-gather.5.cloned.1.call-update
  37.9 7.1 %all-to-all-start.1 = ((f32[8,16,512]{2,1,0:T(8,128)}), f32[8,16,512]{2,1,0:T(8,128)S(1)}, u32[]{:S(2)}, u32[]{:S(2)}) async-start(f32[8,16,512]{2,1,0:T(8,128)} %get-tuple-element.23), calls=%async_computation.1 | async-start | bytes 524288 | tf_op jit(solution)/shard_map/all_to_all | solution.py:42
  45.0 0.0 copy-done.1
  45.0 0.0 copy-done.2
  45.0 0.0 copy-done
  45.1 0.7 shard_map.87
  45.7 0.0 copy-done.3
  45.7 12.8 %all-gather = bf16[1024,256]{1,0:T(8,128)(2,1)S(1)} all-gather(bf16[256,256]{1,0:T(8,128)(2,1)S(1)} %copy-done.3), channel_id=2, replica_groups=mesh['y'=8,'z'=8,'x'=4,'c'=2] {'x'}, dimensions={0}, use_global_device_ids=true | all-gather | bytes 655360 | tf_op jit(solution)/shard_map/all_gather | solution.py:211
  58.6 0.0 all-to-all-done.1.totals_ref
  58.6 0.7 shard_map.88
  59.3 3.4 %all-to-all-start.2 = ((bf16[8,16,512]{2,1,0:T(8,128)(2,1)}), bf16[8,16,512]{2,1,0:T(8,128)(2,1)S(1)}, u32[]{:S(2)}, u32[]{:S(2)}) async-start(bf16[8,16,512]{2,1,0:T(8,128)(2,1)} %shard_map.88), calls=%async_computation.2 | async-start | bytes 262144 | tf_op jit(solution)/shard_map/all_to_all | solution.py:42
  62.6 0.0 reduce-scatter.2.cloned.1.call-start
  62.7 2.2 %all-gather.1 = bf16[8,128,256]{2,1,0:T(8,128)(2,1)S(1)} all-gather(bf16[4,128,256]{2,1,0:T(8,128)(2,1)S(1)} %get-tuple-element.33), channel_id=3, replica_groups=mesh['y'=8,'z'=8,'x'=4,'c'=2] {'c'}, dimensions={0}, use_global_device_ids=true | all-gather | bytes 786432 | tf_op jit(solution)/shard_map/all_gather | solution.py:213
  64.9 2.2 %all-gather.2 = bf16[8,128,256]{2,1,0:T(8,128)(2,1)S(1)} all-gather(bf16[4,128,256]{2,1,0:T(8,128)(2,1)S(1)} %get-tuple-element.32), channel_id=4, replica_groups=mesh['y'=8,'z'=8,'x'=4,'c'=2] {'c'}, dimensions={0}, use_global_device_ids=true | all-gather | bytes 786432 | tf_op jit(solution)/shard_map/all_gather | solution.py:214
  67.0 4.6 %all-to-all-done.2 = bf16[8,16,512]{2,1,0:T(8,128)(2,1)S(1)} async-done(((bf16[8,16,512]{2,1,0:T(8,128)(2,1)}), bf16[8,16,512]{2,1,0:T(8,128)(2,1)S(1)}, u32[]{:S(2)}, u32[]{:S(2)}) %all-to-all-start.2) | async-done | bytes 131104 | tf_op jit(solution)/shard_map/all_to_all | solution.py:42
  71.6 2.9 %shard_map.92 = bf16[8,4,2,32,512]{4,3,2,1,0:T(8,128)(2,1)} custom-call(bf16[256,512]{1,0:T(8,128)(2,1)S(1)} %copy-done, bf16[128,512]{1,0:T(8,128)(2,1)S(1)} %bitcast.17, f32[256,512]{1,0:T(8,128)S(1)} %get-tuple-element.31.inner_ref, bf16[2,4,128,256]{3,2,1,0:T(8,128)(2,1)S(1)} %bitcast.13, bf16[2,4,128,256]{3,2,1,0:T(8,128)(2,1)S(1)} %bitcast.15), custom_call_target="tpu_custom_call" | custom-call | flops 570425344 | bytes 2097152 | tf_op jit(solution)/shard_map/pallas_call | solution.py:233
  74.5 0.0 reduce-scatter.2.cloned.1.call-update
  74.6 4.7 %all-gather.5.cloned.1.call-done = bf16[2048,512]{1,0:T(8,128)(2,1)} async-done(((bf16[256,512]{1,0:T(8,128)(2,1)}), bf16[2048,512]{1,0:T(8,128)(2,1)}) %all-gather.5.cloned.1.call-update) | async-done | bytes 2097168 | tf_op jit(solution)/shard_map/all_gather | solution.py:209
  79.2 2.5 %shard_map.86 = (bf16[256,512]{1,0:T(8,128)(2,1)S(1)}, bf16[512,128]{1,0:T(8,128)(2,1)S(1)}) custom-call(bf16[2,4,128,256]{3,2,1,0:T(8,128)(2,1)S(1)} %bitcast.14, bf16[2,4,128,256]{3,2,1,0:T(8,128)(2,1)S(1)} %bitcast.16, bf16[4,2,256,512]{3,2,1,0:T(8,128)(2,1)} %bitcast.23, bf16[256,512]{1,0:T(8,128)(2,1)S(1)} %copy-done), custom_call_target="tpu_custom_call" | custom-call | flops 570425344 | bytes 2097152 | tf_op jit(solution)/shard_map/pallas_call | solution.py:252
  81.7 22.1 %all_to_all.31.got_ref = bf16[64,8,128]{2,1,0:T(8,128)(2,1)S(1)} all-to-all(bf16[64,8,128]{2,1,0:T(8,128)(2,1)S(1)} %bitcast.20), channel_id=1, replica_groups=mesh['y'=8,'z'=8,'x'=4,'c'=2] {'y','z'}, dimensions={0} | all-to-all | bytes 262144 | tf_op jit(solution)/shard_map/all_to_all | solution.py:42
  103.8 0.1 shard_map.90
  103.9 16.5 %all_to_all.32 = bf16[64,8,128]{2,1,0:T(8,128)(2,1)S(1)} all-to-all(bf16[64,8,128]{2,1,0:T(8,128)(2,1)S(1)} %shard_map.90), channel_id=1, replica_groups=mesh['y'=8,'z'=8,'x'=4,'c'=2] {'y','z'}, dimensions={0} | all-to-all | bytes 262144 | tf_op jit(solution)/shard_map/all_to_all | solution.py:42
  120.5 0.0 reduce-scatter.2.cloned.1.call-done
  120.5 6.1 %all-to-all-start.5 = ((bf16[8,32,512]{2,1,0:T(8,128)(2,1)}), bf16[8,32,512]{2,1,0:T(8,128)(2,1)S(1)}, u32[]{:S(2)}, u32[]{:S(2)}) async-start(bf16[8,32,512]{2,1,0:T(8,128)(2,1)} %bitcast.24), calls=%async_computation.6 | async-start | bytes 524288 | tf_op jit(solution)/shard_map/all_to_all | solution.py:42
  126.5 1.9 %shard_map.89 = (bf16[256,512]{1,0:T(8,128)(2,1)}, f32[256,512]{1,0:T(8,128)S(1)}, f32[256,512]{1,0:T(8,128)S(1)}) custom-call(bf16[256,512]{1,0:T(8,128)(2,1)S(1)} %copy-done, bf16[256,512]{1,0:T(8,128)(2,1)S(1)} %copy-done.1, bf16[256,512]{1,0:T(8,128)(2,1)S(1)} %copy-done.2, bf16[256,512]{1,0:T(8,128)(2,1)S(1)} %get-tuple-element.21.g_ref, ...), custom_call_target="tpu_custom_call" | custom-call | flops 301989888 | bytes 2097152 | tf_op jit(solution)/shard_map/pallas_call | solution.py:265
  128.4 1.1 shard_map.91
  129.5 7.5 %all-to-all-done.5 = bf16[8,32,512]{2,1,0:T(8,128)(2,1)S(1)} async-done(((bf16[8,32,512]{2,1,0:T(8,128)(2,1)}), bf16[8,32,512]{2,1,0:T(8,128)(2,1)S(1)}, u32[]{:S(2)}, u32[]{:S(2)}) %all-to-all-start.5) | async-done | bytes 262176 | tf_op jit(solution)/shard_map/all_to_all | solution.py:42
  137.0 0.6 multiply_bitcast_fusion
  (2 shorter events, 0.1 us)
Async XLA Ops:
  8.0 37.0 %copy-start.1 = (bf16[256,512]{1,0:T(8,128)(2,1)S(1)}, bf16[256,512]{1,0:T(8,128)(2,1)}, u32[]{:S(2)}) copy-start(bf16[256,512]{1,0:T(8,128)(2,1)} %k_ref.7) | copy-start | bytes 786436
  8.0 37.0 %copy-start.2 = (bf16[256,512]{1,0:T(8,128)(2,1)S(1)}, bf16[256,512]{1,0:T(8,128)(2,1)}, u32[]{:S(2)}) copy-start(bf16[256,512]{1,0:T(8,128)(2,1)} %v_ref.7) | copy-start | bytes 786436
  8.0 37.0 %copy-start = (bf16[256,512]{1,0:T(8,128)(2,1)S(1)}, bf16[256,512]{1,0:T(8,128)(2,1)}, u32[]{:S(2)}) copy-start(bf16[256,512]{1,0:T(8,128)(2,1)} %q_ref.7) | copy-start | bytes 786436
  8.0 71.2 %all-gather.5.cloned.1.call-start = ((), (), s32[]{:S(2)}) async-start(), calls=%async_computation.7 | async-start | bytes 2359296 | tf_op jit(solution)/shard_map/all_gather | solution.py:209
  8.1 37.6 %copy-start.3 = (bf16[256,256]{1,0:T(8,128)(2,1)S(1)}, bf16[256,256]{1,0:T(8,128)(2,1)}, u32[]{:S(2)}) copy-start(bf16[256,256]{1,0:T(8,128)(2,1)} %param.8) | copy-start | bytes 393220
  37.9 20.6 %all-to-all-start.1 = ((f32[8,16,512]{2,1,0:T(8,128)}), f32[8,16,512]{2,1,0:T(8,128)S(1)}, u32[]{:S(2)}, u32[]{:S(2)}) async-start(f32[8,16,512]{2,1,0:T(8,128)} %get-tuple-element.23), calls=%async_computation.1 | async-start | bytes 524288 | tf_op jit(solution)/shard_map/all_to_all | solution.py:42
  59.3 12.4 %all-to-all-start.2 = ((bf16[8,16,512]{2,1,0:T(8,128)(2,1)}), bf16[8,16,512]{2,1,0:T(8,128)(2,1)S(1)}, u32[]{:S(2)}, u32[]{:S(2)}) async-start(bf16[8,16,512]{2,1,0:T(8,128)(2,1)} %shard_map.88), calls=%async_computation.2 | async-start | bytes 262144 | tf_op jit(solution)/shard_map/all_to_all | solution.py:42
  62.6 57.8 %reduce-scatter.2.cloned.1.call-start = ((), (), s32[]{:S(2)}) async-start(), calls=%async_computation.8 | async-start | bytes 2359296 | tf_op jit(solution)/shard_map/reduce_scatter | solution.py:250
  120.5 16.6 %all-to-all-start.5 = ((bf16[8,32,512]{2,1,0:T(8,128)(2,1)}), bf16[8,32,512]{2,1,0:T(8,128)(2,1)S(1)}, u32[]{:S(2)}, u32[]{:S(2)}) async-start(bf16[8,32,512]{2,1,0:T(8,128)(2,1)} %bitcast.24), calls=%async_computation.6 | async-start | bytes 524288 | tf_op jit(solution)/shard_map/all_to_all | solution.py:42
Sparse Core Ops, SparseCore 0:
  38.0 41.1 all-gather.4
Sparse Core Ops, SparseCore 1:
  74.6 44.0 reduce-scatter.1

commit v13 on v12

--- a/solution.py
+++ b/solution.py
@@ -57,13 +57,17 @@
         out_ref[p, :own, :] = w_ref[...]
 
 
-def split_kernel(got_ref, weight_ref, part_ref, total_ref):
-    peers, rows, width = got_ref.shape
+def weight_kernel(got_ref, weight_ref):
+    peers = got_ref.shape[0]
     own = weight_ref.shape[0] // peers
-    share = (rows - own) // 2
-    running = jnp.zeros((share, width), F32)
     for p in range(peers):
         weight_ref[p * own : (p + 1) * own, :] = got_ref[p, :own, :]
+
+
+def part_kernel(own, got_ref, part_ref, total_ref):
+    share = part_ref.shape[1]
+    running = jnp.zeros(part_ref.shape[1:], F32)
+    for p in range(got_ref.shape[0]):
         part_ref[p] = running
         high = got_ref[p, own : own + share, :].astype(F32)
         running = running + (high + got_ref[p, own + share :, :].astype(F32))
@@ -196,13 +200,11 @@
         first_kernel, shape((nz, own + 2 * share, width), BF16), square, 3 * big
     )(in_hbm(keys), in_hbm(values), in_hbm(weight_t))
     got = exchange(sent, "z")
-    weight_z, kv_part, kv_total = local_call(
-        split_kernel,
-        (
-            shape((nz * own, width), BF16),
-            shape((nz, share, width), F32),
-            shape((ny, share, width), F32),
-        ),
+    weight_z = local_call(weight_kernel, shape((nz * own, width), BF16), 0, big)(got)
+    got, weight_z = lax.optimization_barrier((got, weight_z))
+    kv_part, kv_total = local_call(
+        functools.partial(part_kernel, own),
+        (shape((nz, share, width), F32), shape((ny, share, width), F32)),
         0,
         2 * big,
     )(got)
@@ -249,13 +251,16 @@
     proj_term = proj_term.reshape(n_blocks * cols, width)
     proj_z = lax.psum_scatter(proj_term, "z", scatter_dimension=0, tiled=True)
 
+    turns = nx // few
+    cot_step = pl.BlockSpec((1, few, half, cols), lambda i: (i // turns, i % turns, 0, 0))
+    weight_step = pl.BlockSpec((few, 1, cols, width), lambda i: (i % turns, i // turns, 0, 0))
     grad_out, qg = local_call(
         grad_out_kernel,
         (shape((tok, width), BF16), shape((heads * DH, DH), BF16)),
         square + 2 * tok * cols * width * n_blocks,
         2 * n_blocks * cols * width,
-        grid=(nc,),
-        in_specs=[cot_spec, cot_spec, by_core, whole],
+        grid=(nc * (nx // few),),
+        in_specs=[cot_step, cot_step, weight_step, whole],
         out_specs=[whole, pl.BlockSpec((heads * DH, DH), lambda i: (0, 0))],
         scratch_shapes=[pltpu.VMEM((tok, width), F32)],
     )(cot_top, cot_low, in_hbm(weight_full.reshape(nx, nc, cols, width)), queries)

time: 146 us -> 147 us (level)
  Pallas kernels: 12 us -> 13.7 us
  transfers between devices with their start and end apart: 5 -> 5, of which waited for: 3 -> 3; matrix products, arithmetic and copies ran while one was open for 0% -> 0% of each run, Pallas kernels for 7% -> 8%
where the time goes in v13:
time: 147 us; the launch traced here: 146 us
  blocking collectives  83.2 us (57%)
  starting transfers between devices  16.6 us (11%)
  waiting for transfers between devices  16.4 us (11%)
  between operations  15.6 us (11%)
  Pallas kernels  13.7 us (9%)
    all_to_all x3, blocking collectives, exchange(): return lax.all_to_all(x, axis, 0, 0, tiled=True)  66 us
    all_to_all x3, starting transfers between devices, exchange(): return lax.all_to_all(x, axis, 0, 0, tiled=True)  16.5 us
    all_gather x1, blocking collectives, per_device(): cot_x = lax.all_gather(cot_own, 'x')  12.8 us
    all_to_all x3, waiting for transfers between devices, exchange(): return lax.all_to_all(x, axis, 0, 0, tiled=True)  12.1 us
    all_gather x1, waiting for transfers between devices, per_device(): weight_full = lax.all_gather(weight_z, 'y', axis=0, tiled=True)  4.3 us
    pallas_call x1, Pallas kernels, per_device(): local_call(grad_out_kernel, (shape((tok, width), BF16), shape((heads * DH...  3.5 us
  transfers between devices with their start and end apart: 5, of which 3 were waited for; matrix products, arithmetic and copies ran while one was open for 0% of the time, Pallas kernels for 8%

profile of v13, /device:TPU:6, one launch (start us, length us, event | category | flops | bytes accessed | tf_op | source)
XLA Modules:
  0.0 146.2 jit_solution(7777325898154761629)
XLA Ops:
  8.0 0.0 all-gather.5.cloned.1.call-start
  8.0 0.0 copy-start
  8.1 0.0 copy-start.1
  8.1 0.0 copy-start.2
  8.1 1.4 shard_map.84
  9.5 0.0 copy-start.3
  9.5 27.7 %all_to_all.30.got_ref = bf16[8,64,512]{2,1,0:T(8,128)(2,1)S(1)} all-to-all(bf16[8,64,512]{2,1,0:T(8,128)(2,1)S(1)} %shard_map.84), channel_id=1, replica_groups=mesh['y'=8,'z'=8,'x'=4,'c'=2] {'z'}, dimensions={0} | all-to-all | bytes 1048576 | tf_op jit(solution)/shard_map/all_to_all | solution.py:42
  37.2 0.7 shard_map.85
  37.9 0.0 all-gather.5.cloned.1.call-update
  38.0 0.8 shard_map.86
  38.7 7.1 %all-to-all-start.1 = ((f32[8,16,512]{2,1,0:T(8,128)}), f32[8,16,512]{2,1,0:T(8,128)S(1)}, u32[]{:S(2)}, u32[]{:S(2)}) async-start(f32[8,16,512]{2,1,0:T(8,128)} %get-tuple-element.25), calls=%async_computation.1 | async-start | bytes 524288 | tf_op jit(solution)/shard_map/all_to_all | solution.py:42
  45.8 0.0 copy-done
  45.8 0.0 copy-done.1
  45.8 0.0 copy-done.2
  45.8 0.7 shard_map.88
  46.5 0.0 copy-done.3
  46.5 12.8 %all-gather = bf16[1024,256]{1,0:T(8,128)(2,1)S(1)} all-gather(bf16[256,256]{1,0:T(8,128)(2,1)S(1)} %copy-done.3), channel_id=2, replica_groups=mesh['y'=8,'z'=8,'x'=4,'c'=2] {'x'}, dimensions={0}, use_global_device_ids=true | all-gather | bytes 655360 | tf_op jit(solution)/shard_map/all_gather | solution.py:213
  59.3 0.0 all-to-all-done.1.totals_ref
  59.3 0.7 shard_map.89
  60.0 3.4 %all-to-all-start.2 = ((bf16[8,16,512]{2,1,0:T(8,128)(2,1)}), bf16[8,16,512]{2,1,0:T(8,128)(2,1)S(1)}, u32[]{:S(2)}, u32[]{:S(2)}) async-start(bf16[8,16,512]{2,1,0:T(8,128)(2,1)} %shard_map.89), calls=%async_computation.2 | async-start | bytes 262144 | tf_op jit(solution)/shard_map/all_to_all | solution.py:42
  63.4 0.0 reduce-scatter.2.cloned.1.call-start
  63.5 2.2 %all-gather.1 = bf16[8,128,256]{2,1,0:T(8,128)(2,1)S(1)} all-gather(bf16[4,128,256]{2,1,0:T(8,128)(2,1)S(1)} %get-tuple-element.35), channel_id=3, replica_groups=mesh['y'=8,'z'=8,'x'=4,'c'=2] {'c'}, dimensions={0}, use_global_device_ids=true | all-gather | bytes 786432 | tf_op jit(solution)/shard_map/all_gather | solution.py:215
  65.7 2.2 %all-gather.2 = bf16[8,128,256]{2,1,0:T(8,128)(2,1)S(1)} all-gather(bf16[4,128,256]{2,1,0:T(8,128)(2,1)S(1)} %get-tuple-element.34), channel_id=4, replica_groups=mesh['y'=8,'z'=8,'x'=4,'c'=2] {'c'}, dimensions={0}, use_global_device_ids=true | all-gather | bytes 786432 | tf_op jit(solution)/shard_map/all_gather | solution.py:216
  67.8 4.6 %all-to-all-done.2 = bf16[8,16,512]{2,1,0:T(8,128)(2,1)S(1)} async-done(((bf16[8,16,512]{2,1,0:T(8,128)(2,1)}), bf16[8,16,512]{2,1,0:T(8,128)(2,1)S(1)}, u32[]{:S(2)}, u32[]{:S(2)}) %all-to-all-start.2) | async-done | bytes 131104 | tf_op jit(solution)/shard_map/all_to_all | solution.py:42
  72.4 2.9 %shard_map.93 = bf16[8,4,2,32,512]{4,3,2,1,0:T(8,128)(2,1)} custom-call(bf16[256,512]{1,0:T(8,128)(2,1)S(1)} %copy-done, bf16[128,512]{1,0:T(8,128)(2,1)S(1)} %bitcast.17, f32[256,512]{1,0:T(8,128)S(1)} %get-tuple-element.33.inner_ref, bf16[2,4,128,256]{3,2,1,0:T(8,128)(2,1)S(1)} %bitcast.13, bf16[2,4,128,256]{3,2,1,0:T(8,128)(2,1)S(1)} %bitcast.15), custom_call_target="tpu_custom_call" | custom-call | flops 570425344 | bytes 2097152 | tf_op jit(solution)/shard_map/pallas_call | solution.py:235
  75.3 0.0 reduce-scatter.2.cloned.1.call-update
  75.3 4.3 %all-gather.5.cloned.1.call-done = bf16[2048,512]{1,0:T(8,128)(2,1)} async-done(((bf16[256,512]{1,0:T(8,128)(2,1)}), bf16[2048,512]{1,0:T(8,128)(2,1)}) %all-gather.5.cloned.1.call-update) | async-done | bytes 2097168 | tf_op jit(solution)/shard_map/all_gather | solution.py:211
  79.6 3.5 %shard_map.87 = (bf16[256,512]{1,0:T(8,128)(2,1)S(1)}, bf16[512,128]{1,0:T(8,128)(2,1)S(1)}) custom-call(bf16[2,4,128,256]{3,2,1,0:T(8,128)(2,1)S(1)} %bitcast.14, bf16[2,4,128,256]{3,2,1,0:T(8,128)(2,1)S(1)} %bitcast.16, bf16[4,2,256,512]{3,2,1,0:T(8,128)(2,1)} %bitcast.23, bf16[256,512]{1,0:T(8,128)(2,1)S(1)} %copy-done), custom_call_target="tpu_custom_call" | custom-call | flops 570425344 | bytes 2097152 | tf_op jit(solution)/shard_map/pallas_call | solution.py:257
  83.1 21.7 %all_to_all.31.got_ref = bf16[64,8,128]{2,1,0:T(8,128)(2,1)S(1)} all-to-all(bf16[64,8,128]{2,1,0:T(8,128)(2,1)S(1)} %bitcast.20), channel_id=1, replica_groups=mesh['y'=8,'z'=8,'x'=4,'c'=2] {'y','z'}, dimensions={0} | all-to-all | bytes 262144 | tf_op jit(solution)/shard_map/all_to_all | solution.py:42
  104.9 0.1 shard_map.91
  105.0 16.5 %all_to_all.32 = bf16[64,8,128]{2,1,0:T(8,128)(2,1)S(1)} all-to-all(bf16[64,8,128]{2,1,0:T(8,128)(2,1)S(1)} %shard_map.91), channel_id=1, replica_groups=mesh['y'=8,'z'=8,'x'=4,'c'=2] {'y','z'}, dimensions={0} | all-to-all | bytes 262144 | tf_op jit(solution)/shard_map/all_to_all | solution.py:42
  121.5 0.0 reduce-scatter.2.cloned.1.call-done
  121.5 6.0 %all-to-all-start.5 = ((bf16[8,32,512]{2,1,0:T(8,128)(2,1)}), bf16[8,32,512]{2,1,0:T(8,128)(2,1)S(1)}, u32[]{:S(2)}, u32[]{:S(2)}) async-start(bf16[8,32,512]{2,1,0:T(8,128)(2,1)} %bitcast.24), calls=%async_computation.6 | async-start | bytes 524288 | tf_op jit(solution)/shard_map/all_to_all | solution.py:42
  127.6 1.9 %shard_map.90 = (bf16[256,512]{1,0:T(8,128)(2,1)}, f32[256,512]{1,0:T(8,128)S(1)}, f32[256,512]{1,0:T(8,128)S(1)}) custom-call(bf16[256,512]{1,0:T(8,128)(2,1)S(1)} %copy-done, bf16[256,512]{1,0:T(8,128)(2,1)S(1)} %copy-done.1, bf16[256,512]{1,0:T(8,128)(2,1)S(1)} %copy-done.2, bf16[256,512]{1,0:T(8,128)(2,1)S(1)} %get-tuple-element.23.g_ref, ...), custom_call_target="tpu_custom_call" | custom-call | flops 301989888 | bytes 2097152 | tf_op jit(solution)/shard_map/pallas_call | solution.py:270
  129.5 1.1 shard_map.92
  130.5 7.5 %all-to-all-done.5 = bf16[8,32,512]{2,1,0:T(8,128)(2,1)S(1)} async-done(((bf16[8,32,512]{2,1,0:T(8,128)(2,1)}), bf16[8,32,512]{2,1,0:T(8,128)(2,1)S(1)}, u32[]{:S(2)}, u32[]{:S(2)}) %all-to-all-start.5) | async-done | bytes 262176 | tf_op jit(solution)/shard_map/all_to_all | solution.py:42
  138.1 0.6 multiply_bitcast_fusion
  (2 shorter events, 0.1 us)
Async XLA Ops:
  8.0 71.6 %all-gather.5.cloned.1.call-start = ((), (), s32[]{:S(2)}) async-start(), calls=%async_computation.7 | async-start | bytes 2359296 | tf_op jit(solution)/shard_map/all_gather | solution.py:211
  8.0 37.8 %copy-start = (bf16[256,512]{1,0:T(8,128)(2,1)S(1)}, bf16[256,512]{1,0:T(8,128)(2,1)}, u32[]{:S(2)}) copy-start(bf16[256,512]{1,0:T(8,128)(2,1)} %q_ref.7) | copy-start | bytes 786436
  8.1 37.8 %copy-start.1 = (bf16[256,512]{1,0:T(8,128)(2,1)S(1)}, bf16[256,512]{1,0:T(8,128)(2,1)}, u32[]{:S(2)}) copy-start(bf16[256,512]{1,0:T(8,128)(2,1)} %k_ref.7) | copy-start | bytes 786436
  8.1 37.8 %copy-start.2 = (bf16[256,512]{1,0:T(8,128)(2,1)S(1)}, bf16[256,512]{1,0:T(8,128)(2,1)}, u32[]{:S(2)}) copy-start(bf16[256,512]{1,0:T(8,128)(2,1)} %v_ref.7) | copy-start | bytes 786436
  9.5 37.0 %copy-start.3 = (bf16[256,256]{1,0:T(8,128)(2,1)S(1)}, bf16[256,256]{1,0:T(8,128)(2,1)}, u32[]{:S(2)}) copy-start(bf16[256,256]{1,0:T(8,128)(2,1)} %param.8) | copy-start | bytes 393220
  38.7 20.6 %all-to-all-start.1 = ((f32[8,16,512]{2,1,0:T(8,128)}), f32[8,16,512]{2,1,0:T(8,128)S(1)}, u32[]{:S(2)}, u32[]{:S(2)}) async-start(f32[8,16,512]{2,1,0:T(8,128)} %get-tuple-element.25), calls=%async_computation.1 | async-start | bytes 524288 | tf_op jit(solution)/shard_map/all_to_all | solution.py:42
  60.0 12.4 %all-to-all-start.2 = ((bf16[8,16,512]{2,1,0:T(8,128)(2,1)}), bf16[8,16,512]{2,1,0:T(8,128)(2,1)S(1)}, u32[]{:S(2)}, u32[]{:S(2)}) async-start(bf16[8,16,512]{2,1,0:T(8,128)(2,1)} %shard_map.89), calls=%async_computation.2 | async-start | bytes 262144 | tf_op jit(solution)/shard_map/all_to_all | solution.py:42
  63.4 58.1 %reduce-scatter.2.cloned.1.call-start = ((), (), s32[]{:S(2)}) async-start(), calls=%async_computation.8 | async-start | bytes 2359296 | tf_op jit(solution)/shard_map/reduce_scatter | solution.py:252
  121.5 16.5 %all-to-all-start.5 = ((bf16[8,32,512]{2,1,0:T(8,128)(2,1)}), bf16[8,32,512]{2,1,0:T(8,128)(2,1)S(1)}, u32[]{:S(2)}, u32[]{:S(2)}) async-start(bf16[8,32,512]{2,1,0:T(8,128)(2,1)} %bitcast.24), calls=%async_computation.6 | async-start | bytes 524288 | tf_op jit(solution)/shard_map/all_to_all | solution.py:42
Sparse Core Ops, SparseCore 0:
  38.1 41.5 all-gather.4
Sparse Core Ops, SparseCore 1:
  75.4 43.4 reduce-scatter.1

commit v14 on v12

--- a/solution.py
+++ b/solution.py
@@ -110,28 +110,17 @@
         out_ref[:, x, 0] = term.reshape(out_ref.shape[0], out_ref.shape[3], out_ref.shape[4])
 
 
-def grad_out_kernel(top_ref, low_ref, w_ref, q_ref, g_ref, qg_ref, acc_ref):
-    step = pl.program_id(0)
-    term = None
+def grad_out_kernel(top_ref, low_ref, w_ref, q_ref, g_ref, qg_ref):
+    total = None
     for x in range(w_ref.shape[0]):
-        cot = jnp.concatenate([top_ref[0, x], low_ref[0, x]], axis=0)
-        one = mm(cot, w_ref[x, 0], 1, 0)
-        term = one if term is None else term + one
-
-    @pl.when(step == 0)
-    def _():
-        acc_ref[...] = term
-
-    @pl.when(step > 0)
-    def _():
-        acc_ref[...] += term
-
-    @pl.when(step == pl.num_programs(0) - 1)
-    def _():
-        g = acc_ref[...].astype(BF16)
-        g_ref[...] = g
-        for h in range(g.shape[1] // DH):
-            qg_ref[head(h), :] = mm(q_ref[:, head(h)], g[:, head(h)], 0, 0).astype(BF16)
+        for c in range(w_ref.shape[1]):
+            cot = jnp.concatenate([top_ref[c, x], low_ref[c, x]], axis=0)
+            term = mm(cot, w_ref[x, c], 1, 0)
+            total = term if total is None else total + term
+    g = total.astype(BF16)
+    g_ref[...] = g
+    for h in range(g.shape[1] // DH):
+        qg_ref[head(h), :] = mm(q_ref[:, head(h)], g[:, head(h)], 0, 0).astype(BF16)
 
 
 def inner_grads_kernel(scale, q_ref, k_ref, v_ref, g_ref, attn_ref, prior_ref, dq_ref, dk_ref, dv_ref):
@@ -227,7 +216,7 @@
     state = pl.BlockSpec((DH, width), lambda i: (0, 0))
     cot_spec = pl.BlockSpec((1, nx, half, cols), lambda i: (i, 0, 0, 0))
     by_core = pl.BlockSpec((nx, 1, cols, width), lambda i: (0, i, 0, 0))
-    few = nx // 2
+    few = nx
     cot_few = pl.BlockSpec((1, few, half, cols), lambda i, j: (i, j, 0, 0))
     same = pl.BlockSpec((tok, width), lambda i, j: (0, 0))
     proj_term = local_call(
@@ -254,10 +243,6 @@
         (shape((tok, width), BF16), shape((heads * DH, DH), BF16)),
         square + 2 * tok * cols * width * n_blocks,
         2 * n_blocks * cols * width,
-        grid=(nc,),
-        in_specs=[cot_spec, cot_spec, by_core, whole],
-        out_specs=[whole, pl.BlockSpec((heads * DH, DH), lambda i: (0, 0))],
-        scratch_shapes=[pltpu.VMEM((tok, width), F32)],
     )(cot_top, cot_low, in_hbm(weight_full.reshape(nx, nc, cols, width)), queries)
     pieces = (ny * nz, heads * DH // (ny * nz), DH)
     qg_got = exchange(qg.reshape(pieces), SEQ)

time: 146 us -> 146 us (level)
  transfers between devices with their start and end apart: 5 -> 5, of which waited for: 3 -> 3; matrix products, arithmetic and copies ran while one was open for 0% -> 0% of each run, Pallas kernels for 7% -> 6%
where the time goes in v14:
time: 146 us; the launch traced here: 145 us
  blocking collectives  83.5 us (57%)
  waiting for transfers between devices  17.5 us (12%)
  starting transfers between devices  16.3 us (11%)
  between operations  15.6 us (11%)
  Pallas kernels  11.3 us (8%)
    all_to_all x3, blocking collectives, exchange(): return lax.all_to_all(x, axis, 0, 0, tiled=True)  66.4 us
    all_to_all x3, starting transfers between devices, exchange(): return lax.all_to_all(x, axis, 0, 0, tiled=True)  16.3 us
    all_gather x1, blocking collectives, per_device(): cot_x = lax.all_gather(cot_own, 'x')  12.8 us
    all_to_all x3, waiting for transfers between devices, exchange(): return lax.all_to_all(x, axis, 0, 0, tiled=True)  12.1 us
    all_gather x1, waiting for transfers between devices, per_device(): weight_full = lax.all_gather(weight_z, 'y', axis=0, tiled=True)  5.34 us
  transfers between devices with their start and end apart: 5, of which 3 were waited for; matrix products, arithmetic and copies ran while one was open for 0% of the time, Pallas kernels for 6%

profile of v14, /device:TPU:6, one launch (start us, length us, event | category | flops | bytes accessed | tf_op | source)
XLA Modules:
  0.0 144.9 jit_solution(15424842492902291200)
XLA Ops:
  8.0 0.0 copy-start.1
  8.0 0.0 copy-start.2
  8.0 0.0 copy-start
  8.0 0.0 all-gather.5.cloned.1.call-start
  8.1 0.0 copy-start.3
  8.1 1.4 shard_map.84
  9.5 27.6 %all_to_all.30.got_ref = bf16[8,64,512]{2,1,0:T(8,128)(2,1)S(1)} all-to-all(bf16[8,64,512]{2,1,0:T(8,128)(2,1)S(1)} %shard_map.84), channel_id=1, replica_groups=mesh['y'=8,'z'=8,'x'=4,'c'=2] {'z'}, dimensions={0} | all-to-all | bytes 1048576 | tf_op jit(solution)/shard_map/all_to_all | solution.py:42
  37.1 0.8 shard_map.85
  37.9 0.0 all-gather.5.cloned.1.call-update
  37.9 7.1 %all-to-all-start.1 = ((f32[8,16,512]{2,1,0:T(8,128)}), f32[8,16,512]{2,1,0:T(8,128)S(1)}, u32[]{:S(2)}, u32[]{:S(2)}) async-start(f32[8,16,512]{2,1,0:T(8,128)} %get-tuple-element.23), calls=%async_computation.1 | async-start | bytes 524288 | tf_op jit(solution)/shard_map/all_to_all | solution.py:42
  45.0 0.0 copy-done.1
  45.0 0.0 copy-done.2
  45.0 0.0 copy-done
  45.1 0.7 shard_map.87
  45.7 0.0 copy-done.3
  45.7 12.8 %all-gather = bf16[1024,256]{1,0:T(8,128)(2,1)S(1)} all-gather(bf16[256,256]{1,0:T(8,128)(2,1)S(1)} %copy-done.3), channel_id=2, replica_groups=mesh['y'=8,'z'=8,'x'=4,'c'=2] {'x'}, dimensions={0}, use_global_device_ids=true | all-gather | bytes 655360 | tf_op jit(solution)/shard_map/all_gather | solution.py:200
  58.6 0.0 all-to-all-done.1.totals_ref
  58.6 0.7 shard_map.88
  59.3 3.4 %all-to-all-start.2 = ((bf16[8,16,512]{2,1,0:T(8,128)(2,1)}), bf16[8,16,512]{2,1,0:T(8,128)(2,1)S(1)}, u32[]{:S(2)}, u32[]{:S(2)}) async-start(bf16[8,16,512]{2,1,0:T(8,128)(2,1)} %shard_map.88), calls=%async_computation.2 | async-start | bytes 262144 | tf_op jit(solution)/shard_map/all_to_all | solution.py:42
  62.6 0.0 reduce-scatter.2.cloned.1.call-start
  62.7 2.2 %all-gather.1 = bf16[8,128,256]{2,1,0:T(8,128)(2,1)S(1)} all-gather(bf16[4,128,256]{2,1,0:T(8,128)(2,1)S(1)} %get-tuple-element.33), channel_id=3, replica_groups=mesh['y'=8,'z'=8,'x'=4,'c'=2] {'c'}, dimensions={0}, use_global_device_ids=true | all-gather | bytes 786432 | tf_op jit(solution)/shard_map/all_gather | solution.py:202
  64.9 2.2 %all-gather.2 = bf16[8,128,256]{2,1,0:T(8,128)(2,1)S(1)} all-gather(bf16[4,128,256]{2,1,0:T(8,128)(2,1)S(1)} %get-tuple-element.32), channel_id=4, replica_groups=mesh['y'=8,'z'=8,'x'=4,'c'=2] {'c'}, dimensions={0}, use_global_device_ids=true | all-gather | bytes 786432 | tf_op jit(solution)/shard_map/all_gather | solution.py:203
  67.0 4.6 %all-to-all-done.2 = bf16[8,16,512]{2,1,0:T(8,128)(2,1)S(1)} async-done(((bf16[8,16,512]{2,1,0:T(8,128)(2,1)}), bf16[8,16,512]{2,1,0:T(8,128)(2,1)S(1)}, u32[]{:S(2)}, u32[]{:S(2)}) %all-to-all-start.2) | async-done | bytes 131104 | tf_op jit(solution)/shard_map/all_to_all | solution.py:42
  71.6 2.2 %shard_map.92 = bf16[8,4,2,32,512]{4,3,2,1,0:T(8,128)(2,1)} custom-call(bf16[256,512]{1,0:T(8,128)(2,1)S(1)} %copy-done, bf16[128,512]{1,0:T(8,128)(2,1)S(1)} %bitcast.17, f32[256,512]{1,0:T(8,128)S(1)} %get-tuple-element.31.inner_ref, bf16[2,4,128,256]{3,2,1,0:T(8,128)(2,1)S(1)} %bitcast.13, bf16[2,4,128,256]{3,2,1,0:T(8,128)(2,1)S(1)} %bitcast.15), custom_call_target="tpu_custom_call" | custom-call | flops 570425344 | bytes 2097152 | tf_op jit(solution)/shard_map/pallas_call | solution.py:222
  73.9 0.0 reduce-scatter.2.cloned.1.call-update
  73.9 5.3 %all-gather.5.cloned.1.call-done = bf16[2048,512]{1,0:T(8,128)(2,1)} async-done(((bf16[256,512]{1,0:T(8,128)(2,1)}), bf16[2048,512]{1,0:T(8,128)(2,1)}) %all-gather.5.cloned.1.call-update) | async-done | bytes 2097168 | tf_op jit(solution)/shard_map/all_gather | solution.py:198
  79.2 2.5 %shard_map.86 = (bf16[256,512]{1,0:T(8,128)(2,1)S(1)}, bf16[512,128]{1,0:T(8,128)(2,1)S(1)}) custom-call(bf16[2,4,128,256]{3,2,1,0:T(8,128)(2,1)S(1)} %bitcast.14, bf16[2,4,128,256]{3,2,1,0:T(8,128)(2,1)S(1)} %bitcast.16, bf16[4,2,256,512]{3,2,1,0:T(8,128)(2,1)} %bitcast.23, bf16[256,512]{1,0:T(8,128)(2,1)S(1)} %copy-done), custom_call_target="tpu_custom_call" | custom-call | flops 570425344 | bytes 2097152 | tf_op jit(solution)/shard_map/pallas_call | solution.py:241
  81.7 22.2 %all_to_all.31.got_ref = bf16[64,8,128]{2,1,0:T(8,128)(2,1)S(1)} all-to-all(bf16[64,8,128]{2,1,0:T(8,128)(2,1)S(1)} %bitcast.20), channel_id=1, replica_groups=mesh['y'=8,'z'=8,'x'=4,'c'=2] {'y','z'}, dimensions={0} | all-to-all | bytes 262144 | tf_op jit(solution)/shard_map/all_to_all | solution.py:42
  103.9 0.1 shard_map.90
  104.0 16.5 %all_to_all.32 = bf16[64,8,128]{2,1,0:T(8,128)(2,1)S(1)} all-to-all(bf16[64,8,128]{2,1,0:T(8,128)(2,1)S(1)} %shard_map.90), channel_id=1, replica_groups=mesh['y'=8,'z'=8,'x'=4,'c'=2] {'y','z'}, dimensions={0} | all-to-all | bytes 262144 | tf_op jit(solution)/shard_map/all_to_all | solution.py:42
  120.5 0.0 reduce-scatter.2.cloned.1.call-done
  120.6 5.8 %all-to-all-start.5 = ((bf16[8,32,512]{2,1,0:T(8,128)(2,1)}), bf16[8,32,512]{2,1,0:T(8,128)(2,1)S(1)}, u32[]{:S(2)}, u32[]{:S(2)}) async-start(bf16[8,32,512]{2,1,0:T(8,128)(2,1)} %bitcast.24), calls=%async_computation.6 | async-start | bytes 524288 | tf_op jit(solution)/shard_map/all_to_all | solution.py:42
  126.3 1.9 %shard_map.89 = (bf16[256,512]{1,0:T(8,128)(2,1)}, f32[256,512]{1,0:T(8,128)S(1)}, f32[256,512]{1,0:T(8,128)S(1)}) custom-call(bf16[256,512]{1,0:T(8,128)(2,1)S(1)} %copy-done, bf16[256,512]{1,0:T(8,128)(2,1)S(1)} %copy-done.1, bf16[256,512]{1,0:T(8,128)(2,1)S(1)} %copy-done.2, bf16[256,512]{1,0:T(8,128)(2,1)S(1)} %get-tuple-element.21.g_ref, ...), custom_call_target="tpu_custom_call" | custom-call | flops 301989888 | bytes 2097152 | tf_op jit(solution)/shard_map/pallas_call | solution.py:250
  128.2 1.1 shard_map.91
  129.3 7.5 %all-to-all-done.5 = bf16[8,32,512]{2,1,0:T(8,128)(2,1)S(1)} async-done(((bf16[8,32,512]{2,1,0:T(8,128)(2,1)}), bf16[8,32,512]{2,1,0:T(8,128)(2,1)S(1)}, u32[]{:S(2)}, u32[]{:S(2)}) %all-to-all-start.5) | async-done | bytes 262176 | tf_op jit(solution)/shard_map/all_to_all | solution.py:42
  136.8 0.6 multiply_bitcast_fusion
  (2 shorter events, 0.1 us)
Async XLA Ops:
  8.0 37.0 %copy-start.1 = (bf16[256,512]{1,0:T(8,128)(2,1)S(1)}, bf16[256,512]{1,0:T(8,128)(2,1)}, u32[]{:S(2)}) copy-start(bf16[256,512]{1,0:T(8,128)(2,1)} %k_ref.7) | copy-start | bytes 786436
  8.0 37.0 %copy-start.2 = (bf16[256,512]{1,0:T(8,128)(2,1)S(1)}, bf16[256,512]{1,0:T(8,128)(2,1)}, u32[]{:S(2)}) copy-start(bf16[256,512]{1,0:T(8,128)(2,1)} %v_ref.7) | copy-start | bytes 786436
  8.0 37.0 %copy-start = (bf16[256,512]{1,0:T(8,128)(2,1)S(1)}, bf16[256,512]{1,0:T(8,128)(2,1)}, u32[]{:S(2)}) copy-start(bf16[256,512]{1,0:T(8,128)(2,1)} %q_ref.7) | copy-start | bytes 786436
  8.0 71.2 %all-gather.5.cloned.1.call-start = ((), (), s32[]{:S(2)}) async-start(), calls=%async_computation.7 | async-start | bytes 2359296 | tf_op jit(solution)/shard_map/all_gather | solution.py:198
  8.1 37.6 %copy-start.3 = (bf16[256,256]{1,0:T(8,128)(2,1)S(1)}, bf16[256,256]{1,0:T(8,128)(2,1)}, u32[]{:S(2)}) copy-start(bf16[256,256]{1,0:T(8,128)(2,1)} %param.8) | copy-start | bytes 393220
  37.9 20.6 %all-to-all-start.1 = ((f32[8,16,512]{2,1,0:T(8,128)}), f32[8,16,512]{2,1,0:T(8,128)S(1)}, u32[]{:S(2)}, u32[]{:S(2)}) async-start(f32[8,16,512]{2,1,0:T(8,128)} %get-tuple-element.23), calls=%async_computation.1 | async-start | bytes 524288 | tf_op jit(solution)/shard_map/all_to_all | solution.py:42
  59.3 12.4 %all-to-all-start.2 = ((bf16[8,16,512]{2,1,0:T(8,128)(2,1)}), bf16[8,16,512]{2,1,0:T(8,128)(2,1)S(1)}, u32[]{:S(2)}, u32[]{:S(2)}) async-start(bf16[8,16,512]{2,1,0:T(8,128)(2,1)} %shard_map.88), calls=%async_computation.2 | async-start | bytes 262144 | tf_op jit(solution)/shard_map/all_to_all | solution.py:42
  62.6 57.9 %reduce-scatter.2.cloned.1.call-start = ((), (), s32[]{:S(2)}) async-start(), calls=%async_computation.8 | async-start | bytes 2359296 | tf_op jit(solution)/shard_map/reduce_scatter | solution.py:239
  120.6 16.3 %all-to-all-start.5 = ((bf16[8,32,512]{2,1,0:T(8,128)(2,1)}), bf16[8,32,512]{2,1,0:T(8,128)(2,1)S(1)}, u32[]{:S(2)}, u32[]{:S(2)}) async-start(bf16[8,32,512]{2,1,0:T(8,128)(2,1)} %bitcast.24), calls=%async_computation.6 | async-start | bytes 524288 | tf_op jit(solution)/shard_map/all_to_all | solution.py:42
Sparse Core Ops, SparseCore 0:
  38.0 41.1 all-gather.4
Sparse Core Ops, SparseCore 1:
  74.0 43.5 reduce-scatter.1

commit v15 on v14

--- a/solution.py
+++ b/solution.py
@@ -246,13 +246,14 @@
     )(cot_top, cot_low, in_hbm(weight_full.reshape(nx, nc, cols, width)), queries)
     pieces = (ny * nz, heads * DH // (ny * nz), DH)
     qg_got = exchange(qg.reshape(pieces), SEQ)
-    sums = local_call(later_kernel, shape(pieces, BF16), 0, 2 * big)(qg_got)
     grad_q, near_k, near_v = local_call(
         functools.partial(inner_grads_kernel, scale),
         (shape((tok, width), BF16), shape((tok, width), F32), shape((tok, width), F32)),
         4 * wide + square,
         16 * big,
     )(queries, keys, values, grad_out, attn, prior)
+    qg_got, near_k, near_v = lax.optimization_barrier((qg_got, near_k, near_v))
+    sums = local_call(later_kernel, shape(pieces, BF16), 0, 2 * big)(qg_got)
     later = exchange(sums, SEQ).reshape(heads * DH, DH)
     grad_k, grad_v = local_call(
         functools.partial(outer_grads_kernel, scale),

time: 146 us -> 145 us (level)
  blocking collectives: 83.5 us -> 61.3 us
  waiting for transfers between devices: 17.5 us -> 30.1 us
  starting transfers between devices: 16.3 us -> 25 us
    all_to_all x3 -> x2, blocking collectives: 66.4 us -> 44.2 us  [exchange(): return lax.all_to_all(x, axis, 0, 0, tiled=True)]
    all_to_all x3 -> x4, waiting for transfers between devices: 12.1 us -> 24.7 us  [exchange(): return lax.all_to_all(x, axis, 0, 0, tiled=True)]
    all_to_all x3 -> x4, starting transfers between devices: 16.3 us -> 24.9 us  [exchange(): return lax.all_to_all(x, axis, 0, 0, tiled=True)]
  transfers between devices with their start and end apart: 5 -> 6, of which waited for: 3 -> 4; matrix products, arithmetic and copies ran while one was open for 0% -> 0% of each run, Pallas kernels for 6% -> 7%
where the time goes in v15:
time: 145 us
  blocking collectives  61.3 us (42%)
  waiting for transfers between devices  30.1 us (21%)
  starting transfers between devices  25 us (17%)
  between operations  15.6 us (11%)
  Pallas kernels  12 us (8%)
    all_to_all x2, blocking collectives, exchange(): return lax.all_to_all(x, axis, 0, 0, tiled=True)  44.2 us
    all_to_all x4, starting transfers between devices, exchange(): return lax.all_to_all(x, axis, 0, 0, tiled=True)  24.9 us
    all_to_all x4, waiting for transfers between devices, exchange(): return lax.all_to_all(x, axis, 0, 0, tiled=True)  24.7 us
    all_gather x1, blocking collectives, per_device(): cot_x = lax.all_gather(cot_own, 'x')  12.8 us
    all_gather x1, waiting for transfers between devices, per_device(): weight_full = lax.all_gather(weight_z, 'y', axis=0, tiled=True)  5.35 us
    pallas_call x1, Pallas kernels, per_device(): local_call(grad_out_kernel, (shape((tok, width), BF16), shape((heads * DH...  3.15 us
  transfers between devices with their start and end apart: 6, of which 4 were waited for; matrix products, arithmetic and copies ran while one was open for 0% of the time, Pallas kernels for 7%

profile of v15, /device:TPU:6, one launch (start us, length us, event | category | flops | bytes accessed | tf_op | source)
XLA Modules:
  0.0 144.7 jit_solution(6669946683976186539)
XLA Ops:
  8.0 0.0 copy-start.2
  8.0 0.0 copy-start.1
  8.0 0.0 copy-start
  8.0 0.0 all-gather.5.cloned.1.call-start
  8.1 0.0 copy-start.3
  8.1 1.4 shard_map.84
  9.5 27.6 %all_to_all.30.got_ref = bf16[8,64,512]{2,1,0:T(8,128)(2,1)S(1)} all-to-all(bf16[8,64,512]{2,1,0:T(8,128)(2,1)S(1)} %shard_map.84), channel_id=1, replica_groups=mesh['y'=8,'z'=8,'x'=4,'c'=2] {'z'}, dimensions={0} | all-to-all | bytes 1048576 | tf_op jit(solution)/shard_map/all_to_all | solution.py:42
  37.1 0.8 shard_map.85
  37.9 0.0 all-gather.5.cloned.1.call-update
  37.9 7.1 %all-to-all-start.1 = ((f32[8,16,512]{2,1,0:T(8,128)}), f32[8,16,512]{2,1,0:T(8,128)S(1)}, u32[]{:S(2)}, u32[]{:S(2)}) async-start(f32[8,16,512]{2,1,0:T(8,128)} %get-tuple-element.26), calls=%async_computation.1 | async-start | bytes 524288 | tf_op jit(solution)/shard_map/all_to_all | solution.py:42
  45.0 0.0 copy-done.2
  45.0 0.0 copy-done.1
  45.0 0.0 copy-done
  45.1 0.7 shard_map.87
  45.7 0.0 copy-done.3
  45.7 12.8 %all-gather = bf16[1024,256]{1,0:T(8,128)(2,1)S(1)} all-gather(bf16[256,256]{1,0:T(8,128)(2,1)S(1)} %copy-done.3), channel_id=2, replica_groups=mesh['y'=8,'z'=8,'x'=4,'c'=2] {'x'}, dimensions={0}, use_global_device_ids=true | all-gather | bytes 655360 | tf_op jit(solution)/shard_map/all_gather | solution.py:200
  58.6 0.0 all-to-all-done.1.totals_ref
  58.6 0.7 shard_map.88
  59.3 3.4 %all-to-all-start.2 = ((bf16[8,16,512]{2,1,0:T(8,128)(2,1)}), bf16[8,16,512]{2,1,0:T(8,128)(2,1)S(1)}, u32[]{:S(2)}, u32[]{:S(2)}) async-start(bf16[8,16,512]{2,1,0:T(8,128)(2,1)} %shard_map.88), calls=%async_computation.2 | async-start | bytes 262144 | tf_op jit(solution)/shard_map/all_to_all | solution.py:42
  62.6 0.0 reduce-scatter.2.cloned.1.call-start
  62.7 2.2 %all-gather.2 = bf16[8,128,256]{2,1,0:T(8,128)(2,1)S(1)} all-gather(bf16[4,128,256]{2,1,0:T(8,128)(2,1)S(1)} %get-tuple-element.38), channel_id=4, replica_groups=mesh['y'=8,'z'=8,'x'=4,'c'=2] {'c'}, dimensions={0}, use_global_device_ids=true | all-gather | bytes 786432 | tf_op jit(solution)/shard_map/all_gather | solution.py:203
  64.9 2.2 %all-gather.1 = bf16[8,128,256]{2,1,0:T(8,128)(2,1)S(1)} all-gather(bf16[4,128,256]{2,1,0:T(8,128)(2,1)S(1)} %get-tuple-element.39), channel_id=3, replica_groups=mesh['y'=8,'z'=8,'x'=4,'c'=2] {'c'}, dimensions={0}, use_global_device_ids=true | all-gather | bytes 786432 | tf_op jit(solution)/shard_map/all_gather | solution.py:202
  67.0 4.6 %all-to-all-done.2 = bf16[8,16,512]{2,1,0:T(8,128)(2,1)S(1)} async-done(((bf16[8,16,512]{2,1,0:T(8,128)(2,1)}), bf16[8,16,512]{2,1,0:T(8,128)(2,1)S(1)}, u32[]{:S(2)}, u32[]{:S(2)}) %all-to-all-start.2) | async-done | bytes 131104 | tf_op jit(solution)/shard_map/all_to_all | solution.py:42
  71.6 2.2 %shard_map.92 = bf16[8,4,2,32,512]{4,3,2,1,0:T(8,128)(2,1)} custom-call(bf16[256,512]{1,0:T(8,128)(2,1)S(1)} %copy-done, bf16[128,512]{1,0:T(8,128)(2,1)S(1)} %bitcast.17, f32[256,512]{1,0:T(8,128)S(1)} %get-tuple-element.37.inner_ref, bf16[2,4,128,256]{3,2,1,0:T(8,128)(2,1)S(1)} %bitcast.15, bf16[2,4,128,256]{3,2,1,0:T(8,128)(2,1)S(1)} %bitcast.13), custom_call_target="tpu_custom_call" | custom-call | flops 570425344 | bytes 2097152 | tf_op jit(solution)/shard_map/pallas_call | solution.py:222
  73.8 0.0 reduce-scatter.2.cloned.1.call-update
  73.9 5.4 %all-gather.5.cloned.1.call-done = bf16[2048,512]{1,0:T(8,128)(2,1)} async-done(((bf16[256,512]{1,0:T(8,128)(2,1)}), bf16[2048,512]{1,0:T(8,128)(2,1)}) %all-gather.5.cloned.1.call-update) | async-done | bytes 2097168 | tf_op jit(solution)/shard_map/all_gather | solution.py:198
  79.2 3.2 %shard_map.86 = (bf16[256,512]{1,0:T(8,128)(2,1)S(1)}, bf16[512,128]{1,0:T(8,128)(2,1)}) custom-call(bf16[2,4,128,256]{3,2,1,0:T(8,128)(2,1)S(1)} %bitcast.16, bf16[2,4,128,256]{3,2,1,0:T(8,128)(2,1)S(1)} %bitcast.14, bf16[4,2,256,512]{3,2,1,0:T(8,128)(2,1)} %bitcast.22, bf16[256,512]{1,0:T(8,128)(2,1)S(1)} %copy-done), custom_call_target="tpu_custom_call" | custom-call | flops 570425344 | bytes 2097152 | tf_op jit(solution)/shard_map/pallas_call | solution.py:241
  82.4 9.7 %all-to-all-start.3 = ((bf16[64,8,128]{2,1,0:T(8,128)(2,1)}), bf16[64,8,128]{2,1,0:T(8,128)(2,1)S(1)}, u32[]{:S(2)}, u32[]{:S(2)}) async-start(bf16[64,8,128]{2,1,0:T(8,128)(2,1)} %bitcast.7), calls=%async_computation.3 | async-start | bytes 262144 | tf_op jit(solution)/shard_map/all_to_all | solution.py:42
  92.1 1.9 %shard_map.89 = (bf16[256,512]{1,0:T(8,128)(2,1)}, f32[256,512]{1,0:T(8,128)S(1)}, f32[256,512]{1,0:T(8,128)S(1)}) custom-call(bf16[256,512]{1,0:T(8,128)(2,1)S(1)} %copy-done, bf16[256,512]{1,0:T(8,128)(2,1)S(1)} %copy-done.1, bf16[256,512]{1,0:T(8,128)(2,1)S(1)} %copy-done.2, bf16[256,512]{1,0:T(8,128)(2,1)S(1)} %get-tuple-element.24.g_ref, ...), custom_call_target="tpu_custom_call" | custom-call | flops 301989888 | bytes 2097152 | tf_op jit(solution)/shard_map/pallas_call | solution.py:249
  94.0 10.7 %all-to-all-done.3.got_ref = bf16[64,8,128]{2,1,0:T(8,128)(2,1)S(1)} async-done(((bf16[64,8,128]{2,1,0:T(8,128)(2,1)}), bf16[64,8,128]{2,1,0:T(8,128)(2,1)S(1)}, u32[]{:S(2)}, u32[]{:S(2)}) %all-to-all-start.3) | async-done | bytes 131104 | tf_op jit(solution)/shard_map/all_to_all | solution.py:42
  104.7 0.1 shard_map.90
  104.8 16.5 %all_to_all.31 = bf16[64,8,128]{2,1,0:T(8,128)(2,1)S(1)} all-to-all(bf16[64,8,128]{2,1,0:T(8,128)(2,1)S(1)} %shard_map.90), channel_id=1, replica_groups=mesh['y'=8,'z'=8,'x'=4,'c'=2] {'y','z'}, dimensions={0} | all-to-all | bytes 262144 | tf_op jit(solution)/shard_map/all_to_all | solution.py:42
  121.3 0.0 reduce-scatter.2.cloned.1.call-done
  121.3 4.8 %all-to-all-start.5 = ((bf16[8,32,512]{2,1,0:T(8,128)(2,1)}), bf16[8,32,512]{2,1,0:T(8,128)(2,1)S(1)}, u32[]{:S(2)}, u32[]{:S(2)}) async-start(bf16[8,32,512]{2,1,0:T(8,128)(2,1)} %bitcast.23), calls=%async_computation.6 | async-start | bytes 524288 | tf_op jit(solution)/shard_map/all_to_all | solution.py:42
  126.1 1.1 shard_map.91
  127.2 9.4 %all-to-all-done.5 = bf16[8,32,512]{2,1,0:T(8,128)(2,1)S(1)} async-done(((bf16[8,32,512]{2,1,0:T(8,128)(2,1)}), bf16[8,32,512]{2,1,0:T(8,128)(2,1)S(1)}, u32[]{:S(2)}, u32[]{:S(2)}) %all-to-all-start.5) | async-done | bytes 262176 | tf_op jit(solution)/shard_map/all_to_all | solution.py:42
  136.6 0.6 multiply_bitcast_fusion
  (2 shorter events, 0.1 us)
Async XLA Ops:
  8.0 37.0 %copy-start.2 = (bf16[256,512]{1,0:T(8,128)(2,1)S(1)}, bf16[256,512]{1,0:T(8,128)(2,1)}, u32[]{:S(2)}) copy-start(bf16[256,512]{1,0:T(8,128)(2,1)} %v_ref.7) | copy-start | bytes 786436
  8.0 37.0 %copy-start.1 = (bf16[256,512]{1,0:T(8,128)(2,1)S(1)}, bf16[256,512]{1,0:T(8,128)(2,1)}, u32[]{:S(2)}) copy-start(bf16[256,512]{1,0:T(8,128)(2,1)} %k_ref.7) | copy-start | bytes 786436
  8.0 37.0 %copy-start = (bf16[256,512]{1,0:T(8,128)(2,1)S(1)}, bf16[256,512]{1,0:T(8,128)(2,1)}, u32[]{:S(2)}) copy-start(bf16[256,512]{1,0:T(8,128)(2,1)} %q_ref.7) | copy-start | bytes 786436
  8.0 71.2 %all-gather.5.cloned.1.call-start = ((), (), s32[]{:S(2)}) async-start(), calls=%async_computation.7 | async-start | bytes 2359296 | tf_op jit(solution)/shard_map/all_gather | solution.py:198
  8.1 37.6 %copy-start.3 = (bf16[256,256]{1,0:T(8,128)(2,1)S(1)}, bf16[256,256]{1,0:T(8,128)(2,1)}, u32[]{:S(2)}) copy-start(bf16[256,256]{1,0:T(8,128)(2,1)} %param.8) | copy-start | bytes 393220
  37.9 20.6 %all-to-all-start.1 = ((f32[8,16,512]{2,1,0:T(8,128)}), f32[8,16,512]{2,1,0:T(8,128)S(1)}, u32[]{:S(2)}, u32[]{:S(2)}) async-start(f32[8,16,512]{2,1,0:T(8,128)} %get-tuple-element.26), calls=%async_computation.1 | async-start | bytes 524288 | tf_op jit(solution)/shard_map/all_to_all | solution.py:42
  59.3 12.4 %all-to-all-start.2 = ((bf16[8,16,512]{2,1,0:T(8,128)(2,1)}), bf16[8,16,512]{2,1,0:T(8,128)(2,1)S(1)}, u32[]{:S(2)}, u32[]{:S(2)}) async-start(bf16[8,16,512]{2,1,0:T(8,128)(2,1)} %shard_map.88), calls=%async_computation.2 | async-start | bytes 262144 | tf_op jit(solution)/shard_map/all_to_all | solution.py:42
  62.6 58.7 %reduce-scatter.2.cloned.1.call-start = ((), (), s32[]{:S(2)}) async-start(), calls=%async_computation.8 | async-start | bytes 2359296 | tf_op jit(solution)/shard_map/reduce_scatter | solution.py:239
  82.4 22.3 %all-to-all-start.3 = ((bf16[64,8,128]{2,1,0:T(8,128)(2,1)}), bf16[64,8,128]{2,1,0:T(8,128)(2,1)S(1)}, u32[]{:S(2)}, u32[]{:S(2)}) async-start(bf16[64,8,128]{2,1,0:T(8,128)(2,1)} %bitcast.7), calls=%async_computation.3 | async-start | bytes 262144 | tf_op jit(solution)/shard_map/all_to_all | solution.py:42
  121.3 15.2 %all-to-all-start.5 = ((bf16[8,32,512]{2,1,0:T(8,128)(2,1)}), bf16[8,32,512]{2,1,0:T(8,128)(2,1)S(1)}, u32[]{:S(2)}, u32[]{:S(2)}) async-start(bf16[8,32,512]{2,1,0:T(8,128)(2,1)} %bitcast.23), calls=%async_computation.6 | async-start | bytes 524288 | tf_op jit(solution)/shard_map/all_to_all | solution.py:42
Sparse Core Ops, SparseCore 0:
  38.0 41.1 all-gather.4
Sparse Core Ops, SparseCore 1:
  74.0 43.4 reduce-scatter.1

commit v16 on v15

--- a/solution.py
+++ b/solution.py
@@ -252,9 +252,9 @@
         4 * wide + square,
         16 * big,
     )(queries, keys, values, grad_out, attn, prior)
-    qg_got, near_k, near_v = lax.optimization_barrier((qg_got, near_k, near_v))
     sums = local_call(later_kernel, shape(pieces, BF16), 0, 2 * big)(qg_got)
     later = exchange(sums, SEQ).reshape(heads * DH, DH)
+    later, near_k, near_v, proj_z = lax.optimization_barrier((later, near_k, near_v, proj_z))
     grad_k, grad_v = local_call(
         functools.partial(outer_grads_kernel, scale),
         (shape((tok, width), BF16), shape((tok, width), BF16)),

time: 145 us -> 146 us (level)
  blocking collectives: 61.3 us -> 66.9 us
  starting transfers between devices: 25 us -> 19.5 us
    all_to_all x2, blocking collectives: 44.2 us -> 49.8 us  [exchange(): return lax.all_to_all(x, axis, 0, 0, tiled=True)]
    all_to_all x4, starting transfers between devices: 24.9 us -> 19.4 us  [exchange(): return lax.all_to_all(x, axis, 0, 0, tiled=True)]
where the time goes in v16:
time: 146 us; the launch traced here: 145 us
  blocking collectives  66.9 us (46%)
  waiting for transfers between devices  30.2 us (21%)
  starting transfers between devices  19.5 us (13%)
  between operations  15.6 us (11%)
  Pallas kernels  12 us (8%)
    all_to_all x2, blocking collectives, exchange(): return lax.all_to_all(x, axis, 0, 0, tiled=True)  49.8 us
    all_to_all x4, waiting for transfers between devices, exchange(): return lax.all_to_all(x, axis, 0, 0, tiled=True)  24.8 us
    all_to_all x4, starting transfers between devices, exchange(): return lax.all_to_all(x, axis, 0, 0, tiled=True)  19.4 us
    all_gather x1, blocking collectives, per_device(): cot_x = lax.all_gather(cot_own, 'x')  12.8 us
    all_gather x1, waiting for transfers between devices, per_device(): weight_full = lax.all_gather(weight_z, 'y', axis=0, tiled=True)  5.35 us
  transfers between devices with their start and end apart: 6, of which 4 were waited for; matrix products, arithmetic and copies ran while one was open for 0% of the time, Pallas kernels for 7%

profile of v16, /device:TPU:6, one launch (start us, length us, event | category | flops | bytes accessed | tf_op | source)
XLA Modules:
  0.0 145.0 jit_solution(9160269454164333900)
XLA Ops:
  8.0 0.0 copy-start.2
  8.0 0.0 copy-start.1
  8.0 0.0 copy-start
  8.0 0.0 all-gather.5.cloned.1.call-start
  8.1 0.0 copy-start.3
  8.1 1.4 shard_map.84
  9.5 27.6 %all_to_all.30.got_ref = bf16[8,64,512]{2,1,0:T(8,128)(2,1)S(1)} all-to-all(bf16[8,64,512]{2,1,0:T(8,128)(2,1)S(1)} %shard_map.84), channel_id=1, replica_groups=mesh['y'=8,'z'=8,'x'=4,'c'=2] {'z'}, dimensions={0} | all-to-all | bytes 1048576 | tf_op jit(solution)/shard_map/all_to_all | solution.py:42
  37.1 0.8 shard_map.85
  37.9 0.0 all-gather.5.cloned.1.call-update
  37.9 7.1 %all-to-all-start.1 = ((f32[8,16,512]{2,1,0:T(8,128)}), f32[8,16,512]{2,1,0:T(8,128)S(1)}, u32[]{:S(2)}, u32[]{:S(2)}) async-start(f32[8,16,512]{2,1,0:T(8,128)} %get-tuple-element.27), calls=%async_computation.1 | async-start | bytes 524288 | tf_op jit(solution)/shard_map/all_to_all | solution.py:42
  45.0 0.0 copy-done.2
  45.0 0.0 copy-done.1
  45.0 0.0 copy-done
  45.1 0.7 shard_map.87
  45.7 0.0 copy-done.3
  45.7 12.8 %all-gather = bf16[1024,256]{1,0:T(8,128)(2,1)S(1)} all-gather(bf16[256,256]{1,0:T(8,128)(2,1)S(1)} %copy-done.3), channel_id=2, replica_groups=mesh['y'=8,'z'=8,'x'=4,'c'=2] {'x'}, dimensions={0}, use_global_device_ids=true | all-gather | bytes 655360 | tf_op jit(solution)/shard_map/all_gather | solution.py:200
  58.6 0.0 all-to-all-done.1.totals_ref
  58.6 0.7 shard_map.88
  59.3 3.4 %all-to-all-start.2 = ((bf16[8,16,512]{2,1,0:T(8,128)(2,1)}), bf16[8,16,512]{2,1,0:T(8,128)(2,1)S(1)}, u32[]{:S(2)}, u32[]{:S(2)}) async-start(bf16[8,16,512]{2,1,0:T(8,128)(2,1)} %shard_map.88), calls=%async_computation.2 | async-start | bytes 262144 | tf_op jit(solution)/shard_map/all_to_all | solution.py:42
  62.6 0.0 reduce-scatter.2.cloned.1.call-start
  62.7 2.2 %all-gather.2 = bf16[8,128,256]{2,1,0:T(8,128)(2,1)S(1)} all-gather(bf16[4,128,256]{2,1,0:T(8,128)(2,1)S(1)} %get-tuple-element.40), channel_id=4, replica_groups=mesh['y'=8,'z'=8,'x'=4,'c'=2] {'c'}, dimensions={0}, use_global_device_ids=true | all-gather | bytes 786432 | tf_op jit(solution)/shard_map/all_gather | solution.py:203
  64.9 2.2 %all-gather.1 = bf16[8,128,256]{2,1,0:T(8,128)(2,1)S(1)} all-gather(bf16[4,128,256]{2,1,0:T(8,128)(2,1)S(1)} %get-tuple-element.41), channel_id=3, replica_groups=mesh['y'=8,'z'=8,'x'=4,'c'=2] {'c'}, dimensions={0}, use_global_device_ids=true | all-gather | bytes 786432 | tf_op jit(solution)/shard_map/all_gather | solution.py:202
  67.0 4.6 %all-to-all-done.2 = bf16[8,16,512]{2,1,0:T(8,128)(2,1)S(1)} async-done(((bf16[8,16,512]{2,1,0:T(8,128)(2,1)}), bf16[8,16,512]{2,1,0:T(8,128)(2,1)S(1)}, u32[]{:S(2)}, u32[]{:S(2)}) %all-to-all-start.2) | async-done | bytes 131104 | tf_op jit(solution)/shard_map/all_to_all | solution.py:42
  71.6 2.2 %shard_map.91 = bf16[8,4,2,32,512]{4,3,2,1,0:T(8,128)(2,1)} custom-call(bf16[256,512]{1,0:T(8,128)(2,1)S(1)} %copy-done, bf16[128,512]{1,0:T(8,128)(2,1)S(1)} %bitcast.17, f32[256,512]{1,0:T(8,128)S(1)} %get-tuple-element.33.inner_ref, bf16[2,4,128,256]{3,2,1,0:T(8,128)(2,1)S(1)} %bitcast.15, bf16[2,4,128,256]{3,2,1,0:T(8,128)(2,1)S(1)} %bitcast.13), custom_call_target="tpu_custom_call" | custom-call | flops 570425344 | bytes 2097152 | tf_op jit(solution)/shard_map/pallas_call | solution.py:222
  73.8 0.0 reduce-scatter.2.cloned.1.call-update
  73.9 5.4 %all-gather.5.cloned.1.call-done = bf16[2048,512]{1,0:T(8,128)(2,1)} async-done(((bf16[256,512]{1,0:T(8,128)(2,1)}), bf16[2048,512]{1,0:T(8,128)(2,1)}) %all-gather.5.cloned.1.call-update) | async-done | bytes 2097168 | tf_op jit(solution)/shard_map/all_gather | solution.py:198
  79.2 2.5 %shard_map.86 = (bf16[256,512]{1,0:T(8,128)(2,1)S(1)}, bf16[512,128]{1,0:T(8,128)(2,1)S(1)}) custom-call(bf16[2,4,128,256]{3,2,1,0:T(8,128)(2,1)S(1)} %bitcast.16, bf16[2,4,128,256]{3,2,1,0:T(8,128)(2,1)S(1)} %bitcast.14, bf16[4,2,256,512]{3,2,1,0:T(8,128)(2,1)} %bitcast.23, bf16[256,512]{1,0:T(8,128)(2,1)S(1)} %copy-done), custom_call_target="tpu_custom_call" | custom-call | flops 570425344 | bytes 2097152 | tf_op jit(solution)/shard_map/pallas_call | solution.py:241
  81.7 22.2 %all_to_all.31.got_ref = bf16[64,8,128]{2,1,0:T(8,128)(2,1)S(1)} all-to-all(bf16[64,8,128]{2,1,0:T(8,128)(2,1)S(1)} %bitcast.20), channel_id=1, replica_groups=mesh['y'=8,'z'=8,'x'=4,'c'=2] {'y','z'}, dimensions={0} | all-to-all | bytes 262144 | tf_op jit(solution)/shard_map/all_to_all | solution.py:42
  103.9 0.7 shard_map.90
  104.7 4.6 %all-to-all-start.4 = ((bf16[64,8,128]{2,1,0:T(8,128)(2,1)}), bf16[64,8,128]{2,1,0:T(8,128)(2,1)S(1)}, u32[]{:S(2)}, u32[]{:S(2)}) async-start(bf16[64,8,128]{2,1,0:T(8,128)(2,1)} %shard_map.90), calls=%async_computation.4 | async-start | bytes 262144 | tf_op jit(solution)/shard_map/all_to_all | solution.py:42
  109.3 1.9 %shard_map.89 = (bf16[256,512]{1,0:T(8,128)(2,1)}, f32[256,512]{1,0:T(8,128)S(1)}, f32[256,512]{1,0:T(8,128)S(1)}) custom-call(bf16[256,512]{1,0:T(8,128)(2,1)S(1)} %copy-done, bf16[256,512]{1,0:T(8,128)(2,1)S(1)} %copy-done.1, bf16[256,512]{1,0:T(8,128)(2,1)S(1)} %copy-done.2, bf16[256,512]{1,0:T(8,128)(2,1)S(1)} %get-tuple-element.25.g_ref, ...), custom_call_target="tpu_custom_call" | custom-call | flops 301989888 | bytes 2097152 | tf_op jit(solution)/shard_map/pallas_call | solution.py:249
  111.2 10.8 %all-to-all-done.4 = bf16[64,8,128]{2,1,0:T(8,128)(2,1)S(1)} async-done(((bf16[64,8,128]{2,1,0:T(8,128)(2,1)}), bf16[64,8,128]{2,1,0:T(8,128)(2,1)S(1)}, u32[]{:S(2)}, u32[]{:S(2)}) %all-to-all-start.4) | async-done | bytes 131104 | tf_op jit(solution)/shard_map/all_to_all | solution.py:42
  122.0 0.0 reduce-scatter.2.cloned.1.call-done
  122.0 4.3 %all-to-all-start.5 = ((bf16[8,32,512]{2,1,0:T(8,128)(2,1)}), bf16[8,32,512]{2,1,0:T(8,128)(2,1)S(1)}, u32[]{:S(2)}, u32[]{:S(2)}) async-start(bf16[8,32,512]{2,1,0:T(8,128)(2,1)} %bitcast.24), calls=%async_computation.6 | async-start | bytes 524288 | tf_op jit(solution)/shard_map/all_to_all | solution.py:42
  126.4 1.1 shard_map.92
  127.4 9.4 %all-to-all-done.5 = bf16[8,32,512]{2,1,0:T(8,128)(2,1)S(1)} async-done(((bf16[8,32,512]{2,1,0:T(8,128)(2,1)}), bf16[8,32,512]{2,1,0:T(8,128)(2,1)S(1)}, u32[]{:S(2)}, u32[]{:S(2)}) %all-to-all-start.5) | async-done | bytes 262176 | tf_op jit(solution)/shard_map/all_to_all | solution.py:42
  136.9 0.6 multiply_bitcast_fusion
  (2 shorter events, 0.1 us)
Async XLA Ops:
  8.0 37.0 %copy-start.2 = (bf16[256,512]{1,0:T(8,128)(2,1)S(1)}, bf16[256,512]{1,0:T(8,128)(2,1)}, u32[]{:S(2)}) copy-start(bf16[256,512]{1,0:T(8,128)(2,1)} %v_ref.7) | copy-start | bytes 786436
  8.0 37.0 %copy-start.1 = (bf16[256,512]{1,0:T(8,128)(2,1)S(1)}, bf16[256,512]{1,0:T(8,128)(2,1)}, u32[]{:S(2)}) copy-start(bf16[256,512]{1,0:T(8,128)(2,1)} %k_ref.7) | copy-start | bytes 786436
  8.0 37.0 %copy-start = (bf16[256,512]{1,0:T(8,128)(2,1)S(1)}, bf16[256,512]{1,0:T(8,128)(2,1)}, u32[]{:S(2)}) copy-start(bf16[256,512]{1,0:T(8,128)(2,1)} %q_ref.7) | copy-start | bytes 786436
  8.0 71.2 %all-gather.5.cloned.1.call-start = ((), (), s32[]{:S(2)}) async-start(), calls=%async_computation.7 | async-start | bytes 2359296 | tf_op jit(solution)/shard_map/all_gather | solution.py:198
  8.1 37.6 %copy-start.3 = (bf16[256,256]{1,0:T(8,128)(2,1)S(1)}, bf16[256,256]{1,0:T(8,128)(2,1)}, u32[]{:S(2)}) copy-start(bf16[256,256]{1,0:T(8,128)(2,1)} %param.8) | copy-start | bytes 393220
  37.9 20.6 %all-to-all-start.1 = ((f32[8,16,512]{2,1,0:T(8,128)}), f32[8,16,512]{2,1,0:T(8,128)S(1)}, u32[]{:S(2)}, u32[]{:S(2)}) async-start(f32[8,16,512]{2,1,0:T(8,128)} %get-tuple-element.27), calls=%async_computation.1 | async-start | bytes 524288 | tf_op jit(solution)/shard_map/all_to_all | solution.py:42
  59.3 12.4 %all-to-all-start.2 = ((bf16[8,16,512]{2,1,0:T(8,128)(2,1)}), bf16[8,16,512]{2,1,0:T(8,128)(2,1)S(1)}, u32[]{:S(2)}, u32[]{:S(2)}) async-start(bf16[8,16,512]{2,1,0:T(8,128)(2,1)} %shard_map.88), calls=%async_computation.2 | async-start | bytes 262144 | tf_op jit(solution)/shard_map/all_to_all | solution.py:42
  62.6 59.4 %reduce-scatter.2.cloned.1.call-start = ((), (), s32[]{:S(2)}) async-start(), calls=%async_computation.8 | async-start | bytes 2359296 | tf_op jit(solution)/shard_map/reduce_scatter | solution.py:239
  104.7 17.4 %all-to-all-start.4 = ((bf16[64,8,128]{2,1,0:T(8,128)(2,1)}), bf16[64,8,128]{2,1,0:T(8,128)(2,1)S(1)}, u32[]{:S(2)}, u32[]{:S(2)}) async-start(bf16[64,8,128]{2,1,0:T(8,128)(2,1)} %shard_map.90), calls=%async_computation.4 | async-start | bytes 262144 | tf_op jit(solution)/shard_map/all_to_all | solution.py:42
  122.0 14.8 %all-to-all-start.5 = ((bf16[8,32,512]{2,1,0:T(8,128)(2,1)}), bf16[8,32,512]{2,1,0:T(8,128)(2,1)S(1)}, u32[]{:S(2)}, u32[]{:S(2)}) async-start(bf16[8,32,512]{2,1,0:T(8,128)(2,1)} %bitcast.24), calls=%async_computation.6 | async-start | bytes 524288 | tf_op jit(solution)/shard_map/all_to_all | solution.py:42
Sparse Core Ops, SparseCore 0:
  38.0 41.1 all-gather.4
Sparse Core Ops, SparseCore 1:
  74.0 43.5 reduce-scatter.1
